TPU v7x, 512 devices: a whole 4x8x8 slice. The times are simulated.
512 devices in a mesh: gx: 4 (over z_lo), gy: 4 (over z_hi, core), vert: 32 (over y, x).
Axes of the slice: x: 4, y: 8, z: 8 (z_hi: 2, z_lo: 4; z = z_hi * 4 + z_lo), core: 2. Of those that a mesh axis runs over, the one named last changes fastest.
Arguments:
- distribution: float32 [1024, 16, 32, 128], P('vert', 'gx', 'gy'), may hold values from -6 to 6
- vel_index: int32 [3, 1024], P(None, 'vert'), may hold values from 0 to 7
- signs: int32 [3, 1024], P(None, 'vert'), may hold values from 0 to 1
- cell_type: int32 [16, 32, 128], P('gx', 'gy'), may hold values 0 or 1
- coupling: float32 [5, 8], replicated, may hold values from -2 to 2
Outputs:
- relaxed: float32 [1024, 16, 32, 128], P('vert', 'gx', 'gy')
All inputs are finite; a program needn't handle non-finite values. No bound on the sum of `cell_type` on one device may be relied on, other than what follows from the above.
Results may differ from a plain program's by a relative error of at most 0.0001.
Values sent between devices are 32-bit elements; how exact they have to be, the bound alone decides.
No kernel may reach another device: no remote copies, remote signals or barrier semaphores. Data moves between devices by JAX's collectives and lax.ppermute only.
A program may use at most 64 MiB of HBM per device.

v0:
```python
import jax
import jax.numpy as jnp
from jax import lax
from jax.sharding import PartitionSpec as P

V = 1024
ITERS = 2


absorb = 0.5
diffuse = 1.0
damping = 0.8
cfl_ratio = 0.2
relax_rate = 0.5
prandtl = 2.0 / 3.0


def padded_2(block, sides, width):
    for axis, dim in sides:
        count = lax.axis_size(axis)
        forward = [(i, i + 1) for i in range(count - 1)]
        forward.append((count - 1, 0))
        backward = [(target, source) for source, target in forward]
        low = lax.ppermute(
            lax.slice_in_dim(block, block.shape[dim] - width, None, axis=dim), axis, forward
        )
        high = lax.ppermute(lax.slice_in_dim(block, 0, width, axis=dim), axis, backward)
        block = jnp.concatenate([low, block, high], axis=dim)
    return block


def velocity_tables(vel_index, signs, total):
    speeds = (vel_index.astype(jnp.float32) + 0.5) * 0.25
    direction = signs.astype(jnp.float32) * 2.0 - 1.0
    veloc = speeds * direction
    square = jnp.sum(veloc * veloc, axis=0)
    weight = 64.0 * jnp.exp(-square) / total
    vel_x, vel_y, vel_z = (veloc[0], veloc[1], veloc[2])
    unit_row = jnp.ones_like(vel_x)
    heat_term = square - 2.5
    moment_basis = (
        jnp.stack(
            [
                unit_row,
                vel_x,
                vel_y,
                vel_z,
                square - 1.5,
                vel_x * vel_y,
                vel_x * vel_z,
                vel_y * vel_z,
                vel_x * vel_x - vel_y * vel_y,
                vel_y * vel_y - vel_z * vel_z,
                heat_term * vel_x,
                heat_term * vel_y,
                heat_term * vel_z,
            ]
        )
        * weight[None]
    )
    shakhov = 0.8 * (1.0 - prandtl)
    equil_table = jnp.stack(
        [
            unit_row,
            2.0 * vel_x,
            2.0 * vel_y,
            2.0 * vel_z,
            2.0 / 3.0 * (square - 1.5),
            shakhov * heat_term * vel_x,
            shakhov * heat_term * vel_y,
            shakhov * heat_term * vel_z,
        ],
        axis=1,
    )
    return (veloc, direction, moment_basis, equil_table)


def neighbour_sum(padded):
    inner = padded[:, 1:-1, 1:-1]
    total = padded[:, 2:, 1:-1] + padded[:, :-2, 1:-1] + padded[:, 1:-1, 2:] + padded[:, 1:-1, :-2]
    return total + jnp.roll(inner, 1, axis=3) + jnp.roll(inner, -1, axis=3)


def fine_apply(field):
    padded = padded_2(field, (("gx", 1), ("gy", 2)), 1)
    return (absorb + 6.0 * diffuse) * field - diffuse * neighbour_sum(padded)


def coarse_apply(field):
    padded = padded_2(field, (("gx", 1), ("gy", 2)), 1)
    return (absorb + 1.5 * diffuse) * field - 0.25 * diffuse * neighbour_sum(padded)


def two_grid(source):
    fine_diag = absorb + 6.0 * diffuse
    coarse_diag = absorb + 1.5 * diffuse
    first = damping * source / fine_diag
    resid = source - fine_apply(first)
    field_count, size_x, size_y, size_z = resid.shape
    blocked = (field_count, size_x // 2, 2, size_y // 2, 2, size_z // 2, 2)
    coarse_res = resid.reshape(blocked).mean(axis=(2, 4, 6))
    coarse_one = damping * coarse_res / coarse_diag
    coarse_two = coarse_one + damping * (coarse_res - coarse_apply(coarse_one)) / coarse_diag
    widened = jnp.broadcast_to(coarse_two[:, :, None, :, None, :, None], blocked).reshape(
        resid.shape
    )
    second = first + widened
    return second + damping * (source - fine_apply(second)) / fine_diag


def build_sources(moments, coupling):
    conserved = absorb * moments[0:5] + jnp.dot(
        coupling, moments[5:13], precision=lax.Precision.HIGHEST
    )
    return jnp.concatenate([conserved, moments[10:13]], axis=0)


def upwind(centre, back_one, back_two, front_one, front_two, upper):
    backward = 1.5 * centre - 2.0 * back_one + 0.5 * back_two
    forward = -1.5 * centre + 2.0 * front_one - 0.5 * front_two
    return upper * backward + (1.0 - upper) * forward


def local(distribution, vel_index, signs, cell_type, coupling):
    veloc, direction, moment_basis, equil_table = velocity_tables(vel_index, signs, V)
    vel_count, size_x, size_y, size_z = distribution.shape
    cells = size_x * size_y * size_z
    wall = cell_type[None] == 1
    vel_cols = [veloc[axis_number][:, None, None, None] for axis_number in range(3)]
    upper_cols = [
        ((direction[axis_number] + 1.0) * 0.5)[:, None, None, None] for axis_number in range(3)
    ]
    for sweep_index in range(ITERS):
        flat = distribution.reshape(vel_count, cells)
        local_moments = jnp.dot(moment_basis, flat, precision=lax.Precision.HIGHEST)
        summed = lax.psum(local_moments, "vert")
        sources = build_sources(summed, coupling)
        corrected = two_grid(sources[0:5].reshape(5, size_x, size_y, size_z))
        fields = jnp.concatenate([corrected.reshape(5, cells), sources[5:8]], axis=0)
        feq = jnp.dot(equil_table, fields, precision=lax.Precision.HIGHEST).reshape(
            vel_count, size_x, size_y, size_z
        )
        padded = padded_2(distribution, (("gx", 1), ("gy", 2)), 2)
        along_x = upwind(
            distribution,
            padded[:, 1:-3, 2:-2],
            padded[:, 0:-4, 2:-2],
            padded[:, 3:-1, 2:-2],
            padded[:, 4:, 2:-2],
            upper_cols[0],
        )
        along_y = upwind(
            distribution,
            padded[:, 2:-2, 1:-3],
            padded[:, 2:-2, 0:-4],
            padded[:, 2:-2, 3:-1],
            padded[:, 2:-2, 4:],
            upper_cols[1],
        )
        along_z = upwind(
            distribution,
            jnp.roll(distribution, 1, axis=3),
            jnp.roll(distribution, 2, axis=3),
            jnp.roll(distribution, -1, axis=3),
            jnp.roll(distribution, -2, axis=3),
            upper_cols[2],
        )
        advect = vel_cols[0] * along_x + vel_cols[1] * along_y + vel_cols[2] * along_z
        half = distribution + relax_rate * (feq - distribution) - cfl_ratio * advect
        distribution = jnp.where(wall, feq, half)
    return distribution


def solution(mesh):
    in_specs = (
        P("vert", "gx", "gy", None),
        P(None, "vert"),
        P(None, "vert"),
        P("gx", "gy", None),
        P(),
    )
    out_specs = P("vert", "gx", "gy", None)
    return jax.shard_map(local, mesh=mesh, in_specs=in_specs, out_specs=out_specs, check_vma=False)
```

profile of v0, /device:TPU:1, one launch (start us, length us, event | category | flops | bytes accessed | tf_op | source)
XLA Modules:
  0.0 514.2 jit_solution(3920722636657356085)
XLA Ops:
  8.0 2.4 fusion.24
  10.5 1.9 fusion.150
  12.3 4.8 collective-permute-start.12
  17.2 5.5 %collective-permute-start.13 = (f32[32,2,8,128]{3,2,1,0:T(8,128)}, f32[32,2,8,128]{3,2,1,0:T(8,128)S(1)}, u32[]{:S(2)}, u32[]{:S(2)}) collective-permute-start(f32[32,2,8,128]{3,2,1,0:T(8,128)} %get-tuple-element.32), channel_id=1, source_target_pairs={{128,0},{256,128},{384,256},{0,384},{129,1},{257,129},{385,257},{1... | collective-permute-start | bytes 786440 | tf_op jit(solution)/shard_map/ppermute | solution.py:27
  22.7 1.1 fusion.146
  23.9 1.1 fusion.147
  25.0 1.1 fusion.148
  26.1 1.1 fusion.149
  27.9 140.6 %all-reduce.3.cloned.1.call-done = f32[13,4096]{1,0:T(8,128)} async-done(((f32[13,4096]{1,0:T(8,128)}), f32[13,4096]{1,0:T(8,128)}) %all-reduce.3.cloned.1.call-update) | async-done | bytes 213008 | tf_op jit(solution)/shard_map/psum | solution.py:136
  168.5 1.2 fusion.2
  169.7 5.4 %collective-permute-start = (f32[5,1,8,128]{3,2,1,0:T(8,128)S(1)}, f32[5,1,8,128]{3,2,1,0:T(8,128)S(1)}, u32[]{:S(2)}, u32[]{:S(2)}) collective-permute-start(f32[5,1,8,128]{3,2,1,0:T(8,128)S(1)} %get-tuple-element.69), channel_id=1, source_target_pairs={{128,0},{256,128},{384,256},{0,384},{129,1},{257,129},{385,257},{1... | collective-permute-start | bytes 61448 | tf_op jit(solution)/shard_map/ppermute | solution.py:27
  175.2 1.9 collective-permute-start.1
  177.2 4.3 collective-permute-done.1
  181.5 8.5 %collective-permute-start.2 = (f32[5,6,1,128]{3,2,1,0:T(1,128)S(1)}, f32[5,6,1,128]{3,2,1,0:T(1,128)S(1)}, u32[]{:S(2)}, u32[]{:S(2)}) collective-permute-start(f32[5,6,1,128]{3,2,1,0:T(1,128)S(1)} %get-tuple-element.44), channel_id=1, source_target_pairs={{32,0},{64,32},{96,64},{0,96},{33,1},{65,33},{97,65},{1,97},{34,2}... | collective-permute-start | bytes 46088 | tf_op jit(solution)/shard_map/ppermute | solution.py:27
  190.1 4.9 collective-permute-start.3
  196.9 1.4 reduce_sum.28
  198.4 1.9 collective-permute-start.4
  200.3 3.4 collective-permute-start.5
  203.8 2.8 collective-permute-done.5
  206.5 6.0 %collective-permute-start.6 = (f32[5,4,1,64]{3,2,1,0:T(1,128)S(1)}, f32[5,4,1,64]{3,2,1,0:T(1,128)S(1)}, u32[]{:S(2)}, u32[]{:S(2)}) collective-permute-start(f32[5,4,1,64]{3,2,1,0:T(1,128)S(1)} %get-tuple-element.72), channel_id=1, source_target_pairs={{32,0},{64,32},{96,64},{0,96},{33,1},{65,33},{97,65},{1,97},{34,2}... | collective-permute-start | bytes 15368 | tf_op jit(solution)/shard_map/ppermute | solution.py:27
  212.6 4.9 collective-permute-start.7
  220.3 1.9 collective-permute-start.8
  222.2 3.4 collective-permute-start.9
  225.7 1.0 constant_dynamic-update-slice_fusion.1
  226.9 1.7 collective-permute-done.9
  228.7 6.1 %collective-permute-start.10 = (f32[5,6,1,128]{3,2,1,0:T(1,128)S(1)}, f32[5,6,1,128]{3,2,1,0:T(1,128)S(1)}, u32[]{:S(2)}, u32[]{:S(2)}) collective-permute-start(f32[5,6,1,128]{3,2,1,0:T(1,128)S(1)} %get-tuple-element.42), channel_id=1, source_target_pairs={{32,0},{64,32},{96,64},{0,96},{33,1},{65,33},{97,65},{1,97},{34,2}... | collective-permute-start | bytes 46088 | tf_op jit(solution)/shard_map/ppermute | solution.py:27
  234.8 4.9 collective-permute-start.11
  240.0 2.4 collective-permute-start.14
  242.6 2.2 collective-permute-start.15
  245.7 2.3 collective-permute-done.14
  248.2 6.3 %collective-permute-done.15 = f32[32,8,2,128]{3,1,2,0:T(8,128)S(1)} collective-permute-done((f32[32,8,2,128]{3,1,2,0:T(8,128)S(1)}, f32[32,8,2,128]{3,1,2,0:T(8,128)S(1)}, u32[]{:S(2)}, u32[]{:S(2)}) %collective-permute-start.15) | collective-permute-done | bytes 262176 | tf_op jit(solution)/shard_map/ppermute | solution.py:27
  254.7 1.9 fusion.54
  258.4 1.1 fusion.142
  259.6 1.1 fusion.143
  260.7 1.9 collective-permute-start.28
  262.6 6.6 %collective-permute-start.29 = (f32[32,2,8,128]{3,2,1,0:T(8,128)}, f32[32,2,8,128]{3,2,1,0:T(8,128)}, u32[]{:S(2)}, u32[]{:S(2)}) collective-permute-start(f32[32,2,8,128]{3,2,1,0:T(8,128)} %get-tuple-element.20), channel_id=1, source_target_pairs={{128,0},{256,128},{384,256},{0,384},{129,1},{257,129},{385,257},{1... | collective-permute-start | bytes 786440 | tf_op jit(solution)/shard_map/ppermute | solution.py:27
  269.2 1.4 fusion.21
  270.6 1.2 fusion.144
  271.7 144.3 %all-reduce.5.cloned.1.call-done = f32[13,4096]{1,0:T(8,128)} async-done(((f32[13,4096]{1,0:T(8,128)}), f32[13,4096]{1,0:T(8,128)}) %all-reduce.5.cloned.1.call-update) | async-done | bytes 213008 | tf_op jit(solution)/shard_map/psum | solution.py:136
  416.1 1.2 fusion.3
  417.3 5.4 %collective-permute-start.16 = (f32[5,1,8,128]{3,2,1,0:T(8,128)S(1)}, f32[5,1,8,128]{3,2,1,0:T(8,128)S(1)}, u32[]{:S(2)}, u32[]{:S(2)}) collective-permute-start(f32[5,1,8,128]{3,2,1,0:T(8,128)S(1)} %get-tuple-element.57), channel_id=1, source_target_pairs={{128,0},{256,128},{384,256},{0,384},{129,1},{257,129},{385,257},{1... | collective-permute-start | bytes 61448 | tf_op jit(solution)/shard_map/ppermute | solution.py:27
  422.8 1.9 collective-permute-start.17
  424.8 4.3 collective-permute-done.17
  429.1 8.5 %collective-permute-start.18 = (f32[5,6,1,128]{3,2,1,0:T(1,128)S(1)}, f32[5,6,1,128]{3,2,1,0:T(1,128)S(1)}, u32[]{:S(2)}, u32[]{:S(2)}) collective-permute-start(f32[5,6,1,128]{3,2,1,0:T(1,128)S(1)} %get-tuple-element.40), channel_id=1, source_target_pairs={{32,0},{64,32},{96,64},{0,96},{33,1},{65,33},{97,65},{1,97},{34,2}... | collective-permute-start | bytes 46088 | tf_op jit(solution)/shard_map/ppermute | solution.py:27
  437.7 5.1 collective-permute-start.19
  442.9 1.5 slice.603
  445.2 1.4 reduce_sum.29
  446.8 1.9 collective-permute-start.20
  448.7 3.4 collective-permute-start.21
  452.1 2.8 collective-permute-done.21
  454.9 5.3 %collective-permute-start.22 = (f32[5,4,1,64]{3,2,1,0:T(1,128)S(1)}, f32[5,4,1,64]{3,2,1,0:T(1,128)S(1)}, u32[]{:S(2)}, u32[]{:S(2)}) collective-permute-start(f32[5,4,1,64]{3,2,1,0:T(1,128)S(1)} %get-tuple-element.70), channel_id=1, source_target_pairs={{32,0},{64,32},{96,64},{0,96},{33,1},{65,33},{97,65},{1,97},{34,2}... | collective-permute-start | bytes 15368 | tf_op jit(solution)/shard_map/ppermute | solution.py:27
  460.2 4.9 collective-permute-start.23
  466.2 1.0 broadcast_in_dim.17
  468.0 2.1 collective-permute-start.24
  470.0 3.4 collective-permute-start.25
  473.5 3.0 collective-permute-done.25
  476.5 6.1 %collective-permute-start.26 = (f32[5,6,1,128]{3,2,1,0:T(1,128)S(1)}, f32[5,6,1,128]{3,2,1,0:T(1,128)S(1)}, u32[]{:S(2)}, u32[]{:S(2)}) collective-permute-start(f32[5,6,1,128]{3,2,1,0:T(1,128)S(1)} %get-tuple-element.38), channel_id=1, source_target_pairs={{32,0},{64,32},{96,64},{0,96},{33,1},{65,33},{97,65},{1,97},{34,2}... | collective-permute-start | bytes 46088 | tf_op jit(solution)/shard_map/ppermute | solution.py:27
  482.6 4.9 collective-permute-start.27
  487.6 1.4 pad_maximum_fusion.12
  489.0 2.4 collective-permute-start.30
  491.6 2.2 collective-permute-start.31
  494.7 2.2 collective-permute-done.30
  497.1 6.4 %collective-permute-done.31 = f32[32,8,2,128]{3,1,2,0:T(8,128)S(1)} collective-permute-done((f32[32,8,2,128]{3,1,2,0:T(8,128)S(1)}, f32[32,8,2,128]{3,1,2,0:T(8,128)S(1)}, u32[]{:S(2)}, u32[]{:S(2)}) %collective-permute-start.31) | collective-permute-done | bytes 262176 | tf_op jit(solution)/shard_map/ppermute | solution.py:27
  503.8 3.6 fusion.15
  (176 shorter events, 15.0 us)
Async XLA Ops:
  6.5 161.9 %copy-start = (f32[5,8]{1,0:T(8,128)S(1)}, f32[5,8]{1,0:T(8,128)}, u32[]{:S(2)}) copy-start(f32[5,8]{1,0:T(8,128)} %param.9) | copy-start | bytes 484
  6.5 16.2 %copy-start.1 = (f32[32,4,8,128]{3,2,1,0:T(8,128)S(1)}, f32[32,4,8,128]{3,2,1,0:T(8,128)}, u32[]{:S(2)}) copy-start(f32[32,4,8,128]{3,2,1,0:T(8,128)} %param.5) | copy-start | bytes 1572868
  6.5 161.9 %all-reduce.3.cloned.1.call-start = ((), (), s32[]{:S(2)}) async-start(), calls=%async_computation | async-start | bytes 524288 | tf_op jit(solution)/shard_map/psum | solution.py:136
  7.3 16.5 %copy-start.35 = (f32[32]{0:T(128)}, f32[32]{0:T(128)S(1)}, u32[]{:S(2)}) copy-start(f32[32]{0:T(128)S(1)} %get-tuple-element.113) | copy-start | bytes 388
  10.4 405.7 %all-reduce.5.cloned.1.call-start = ((), (), s32[]{:S(2)}) async-start(), calls=%async_computation.1 | async-start | bytes 524288 | tf_op jit(solution)/shard_map/psum | solution.py:136
  12.3 213.4 %collective-permute-start.12 = (f32[32,2,8,128]{3,2,1,0:T(8,128)}, f32[32,2,8,128]{3,2,1,0:T(8,128)}, u32[]{:S(2)}, u32[]{:S(2)}) collective-permute-start(f32[32,2,8,128]{3,2,1,0:T(8,128)} %get-tuple-element.33), channel_id=1, source_target_pairs={{0,128},{128,256},{256,384},{384,0},{1,129},{129,257},{257,385},{3... | collective-permute-start | bytes 786440 | tf_op jit(solution)/shard_map/ppermute | solution.py:24
  17.2 209.7 %collective-permute-start.13 = (f32[32,2,8,128]{3,2,1,0:T(8,128)}, f32[32,2,8,128]{3,2,1,0:T(8,128)S(1)}, u32[]{:S(2)}, u32[]{:S(2)}) collective-permute-start(f32[32,2,8,128]{3,2,1,0:T(8,128)} %get-tuple-element.32), channel_id=1, source_target_pairs={{128,0},{256,128},{384,256},{0,384},{129,1},{257,129},{385,257},{1... | collective-permute-start | bytes 786440 | tf_op jit(solution)/shard_map/ppermute | solution.py:27
  27.2 227.3 %copy-start.19 = (f32[32]{0:T(128)}, f32[32]{0:T(128)S(1)}, u32[]{:S(2)}) copy-start(f32[32]{0:T(128)S(1)} %get-tuple-element.104) | copy-start | bytes 388
  27.3 227.3 %copy-start.21 = (f32[32]{0:T(128)}, f32[32]{0:T(128)S(1)}, u32[]{:S(2)}) copy-start(f32[32]{0:T(128)S(1)} %get-tuple-element.105) | copy-start | bytes 388
  169.7 7.5 %collective-permute-start = (f32[5,1,8,128]{3,2,1,0:T(8,128)S(1)}, f32[5,1,8,128]{3,2,1,0:T(8,128)S(1)}, u32[]{:S(2)}, u32[]{:S(2)}) collective-permute-start(f32[5,1,8,128]{3,2,1,0:T(8,128)S(1)} %get-tuple-element.69), channel_id=1, source_target_pairs={{128,0},{256,128},{384,256},{0,384},{129,1},{257,129},{385,257},{1... | collective-permute-start | bytes 61448 | tf_op jit(solution)/shard_map/ppermute | solution.py:27
  175.2 6.3 %collective-permute-start.1 = (f32[5,1,8,128]{3,2,1,0:T(8,128)S(1)}, f32[5,1,8,128]{3,2,1,0:T(8,128)S(1)}, u32[]{:S(2)}, u32[]{:S(2)}) collective-permute-start(f32[5,1,8,128]{3,2,1,0:T(8,128)S(1)} %get-tuple-element.68), channel_id=1, source_target_pairs={{0,128},{128,256},{256,384},{384,0},{1,129},{129,257},{257,385},{3... | collective-permute-start | bytes 61448 | tf_op jit(solution)/shard_map/ppermute | solution.py:24
  181.5 14.5 %collective-permute-start.2 = (f32[5,6,1,128]{3,2,1,0:T(1,128)S(1)}, f32[5,6,1,128]{3,2,1,0:T(1,128)S(1)}, u32[]{:S(2)}, u32[]{:S(2)}) collective-permute-start(f32[5,6,1,128]{3,2,1,0:T(1,128)S(1)} %get-tuple-element.44), channel_id=1, source_target_pairs={{32,0},{64,32},{96,64},{0,96},{33,1},{65,33},{97,65},{1,97},{34,2}... | collective-permute-start | bytes 46088 | tf_op jit(solution)/shard_map/ppermute | solution.py:27
  190.1 6.0 %collective-permute-start.3 = (f32[5,6,1,128]{3,2,1,0:T(1,128)S(1)}, f32[5,6,1,128]{3,2,1,0:T(1,128)S(1)}, u32[]{:S(2)}, u32[]{:S(2)}) collective-permute-start(f32[5,6,1,128]{3,2,1,0:T(1,128)S(1)} %get-tuple-element.45), channel_id=1, source_target_pairs={{0,32},{32,64},{64,96},{96,0},{1,33},{33,65},{65,97},{97,1},{2,34}... | collective-permute-start | bytes 46088 | tf_op jit(solution)/shard_map/ppermute | solution.py:24
  198.4 5.4 %collective-permute-start.4 = (f32[5,1,4,64]{3,2,1,0:T(4,128)S(1)}, f32[5,1,4,64]{3,2,1,0:T(4,128)S(1)}, u32[]{:S(2)}, u32[]{:S(2)}) collective-permute-start(f32[5,1,4,64]{3,2,1,0:T(4,128)S(1)} %get-tuple-element.85), channel_id=1, source_target_pairs={{128,0},{256,128},{384,256},{0,384},{129,1},{257,129},{385,257},{1... | collective-permute-start | bytes 15368 | tf_op jit(solution)/shard_map/ppermute | solution.py:27
  200.3 6.2 %collective-permute-start.5 = (f32[5,1,4,64]{3,2,1,0:T(4,128)S(1)}, f32[5,1,4,64]{3,2,1,0:T(4,128)S(1)}, u32[]{:S(2)}, u32[]{:S(2)}) collective-permute-start(f32[5,1,4,64]{3,2,1,0:T(4,128)S(1)} %get-tuple-element.84), channel_id=1, source_target_pairs={{0,128},{128,256},{256,384},{384,0},{1,129},{129,257},{257,385},{3... | collective-permute-start | bytes 15368 | tf_op jit(solution)/shard_map/ppermute | solution.py:24
  206.5 11.1 %collective-permute-start.6 = (f32[5,4,1,64]{3,2,1,0:T(1,128)S(1)}, f32[5,4,1,64]{3,2,1,0:T(1,128)S(1)}, u32[]{:S(2)}, u32[]{:S(2)}) collective-permute-start(f32[5,4,1,64]{3,2,1,0:T(1,128)S(1)} %get-tuple-element.72), channel_id=1, source_target_pairs={{32,0},{64,32},{96,64},{0,96},{33,1},{65,33},{97,65},{1,97},{34,2}... | collective-permute-start | bytes 15368 | tf_op jit(solution)/shard_map/ppermute | solution.py:27
  212.6 5.7 %collective-permute-start.7 = (f32[5,4,1,64]{3,2,1,0:T(1,128)S(1)}, f32[5,4,1,64]{3,2,1,0:T(1,128)S(1)}, u32[]{:S(2)}, u32[]{:S(2)}) collective-permute-start(f32[5,4,1,64]{3,2,1,0:T(1,128)S(1)} %get-tuple-element.73), channel_id=1, source_target_pairs={{0,32},{32,64},{64,96},{96,0},{1,33},{33,65},{65,97},{97,1},{2,34}... | collective-permute-start | bytes 15368 | tf_op jit(solution)/shard_map/ppermute | solution.py:24
  220.3 6.6 %collective-permute-start.8 = (f32[5,1,8,128]{3,2,1,0:T(8,128)S(1)}, f32[5,1,8,128]{3,2,1,0:T(8,128)S(1)}, u32[]{:S(2)}, u32[]{:S(2)}) collective-permute-start(f32[5,1,8,128]{3,2,1,0:T(8,128)S(1)} %get-tuple-element.63), channel_id=1, source_target_pairs={{128,0},{256,128},{384,256},{0,384},{129,1},{257,129},{385,257},{1... | collective-permute-start | bytes 61448 | tf_op jit(solution)/shard_map/ppermute | solution.py:27
  222.2 6.4 %collective-permute-start.9 = (f32[5,1,8,128]{3,2,1,0:T(8,128)S(1)}, f32[5,1,8,128]{3,2,1,0:T(8,128)S(1)}, u32[]{:S(2)}, u32[]{:S(2)}) collective-permute-start(f32[5,1,8,128]{3,2,1,0:T(8,128)S(1)} %get-tuple-element.62), channel_id=1, source_target_pairs={{0,128},{128,256},{256,384},{384,0},{1,129},{129,257},{257,385},{3... | collective-permute-start | bytes 61448 | tf_op jit(solution)/shard_map/ppermute | solution.py:24
  228.7 16.1 %collective-permute-start.10 = (f32[5,6,1,128]{3,2,1,0:T(1,128)S(1)}, f32[5,6,1,128]{3,2,1,0:T(1,128)S(1)}, u32[]{:S(2)}, u32[]{:S(2)}) collective-permute-start(f32[5,6,1,128]{3,2,1,0:T(1,128)S(1)} %get-tuple-element.42), channel_id=1, source_target_pairs={{32,0},{64,32},{96,64},{0,96},{33,1},{65,33},{97,65},{1,97},{34,2}... | collective-permute-start | bytes 46088 | tf_op jit(solution)/shard_map/ppermute | solution.py:27
  234.8 9.9 %collective-permute-start.11 = (f32[5,6,1,128]{3,2,1,0:T(1,128)S(1)}, f32[5,6,1,128]{3,2,1,0:T(1,128)S(1)}, u32[]{:S(2)}, u32[]{:S(2)}) collective-permute-start(f32[5,6,1,128]{3,2,1,0:T(1,128)S(1)} %get-tuple-element.43), channel_id=1, source_target_pairs={{0,32},{32,64},{64,96},{96,0},{1,33},{33,65},{65,97},{97,1},{2,34}... | collective-permute-start | bytes 46088 | tf_op jit(solution)/shard_map/ppermute | solution.py:24
  240.0 8.0 %collective-permute-start.14 = (f32[32,8,2,128]{3,1,2,0:T(8,128)S(1)}, f32[32,8,2,128]{3,1,2,0:T(8,128)S(1)}, u32[]{:S(2)}, u32[]{:S(2)}) collective-permute-start(f32[32,8,2,128]{3,1,2,0:T(8,128)S(1)} %copy.563), channel_id=1, source_target_pairs={{0,32},{32,64},{64,96},{96,0},{1,33},{33,65},{65,97},{97,1},{2,34}... | collective-permute-start | bytes 786440 | tf_op jit(solution)/shard_map/ppermute | solution.py:24
  242.4 12.2 %copy-start.2 = (f32[32,4,8,126]{3,2,1,0:T(8,128)S(1)}, f32[32,4,8,126]{3,2,1,0:T(8,128)}, u32[]{:S(2)}) copy-start(f32[32,4,8,126]{3,2,1,0:T(8,128)} %get-tuple-element.21) | copy-start | bytes 1548292
  242.4 12.2 %copy-start.3 = (f32[32,4,8,126]{3,2,1,0:T(8,128)S(1)}, f32[32,4,8,126]{3,2,1,0:T(8,128)}, u32[]{:S(2)}) copy-start(f32[32,4,8,126]{3,2,1,0:T(8,128)} %get-tuple-element.22) | copy-start | bytes 1548292
  242.4 12.2 %copy-start.4 = (f32[32,4,8,2]{3,2,1,0:T(8,128)S(1)}, f32[32,4,8,2]{3,2,1,0:T(8,128)}, u32[]{:S(2)}) copy-start(f32[32,4,8,2]{3,2,1,0:T(8,128)} %get-tuple-element.23) | copy-start | bytes 24580
  242.4 12.2 %copy-start.5 = (f32[32,4,8,2]{3,2,1,0:T(8,128)S(1)}, f32[32,4,8,2]{3,2,1,0:T(8,128)}, u32[]{:S(2)}) copy-start(f32[32,4,8,2]{3,2,1,0:T(8,128)} %get-tuple-element.24) | copy-start | bytes 24580
  242.4 12.2 %copy-start.6 = (f32[32,4,8,127]{3,2,1,0:T(8,128)S(1)}, f32[32,4,8,127]{3,2,1,0:T(8,128)}, u32[]{:S(2)}) copy-start(f32[32,4,8,127]{3,2,1,0:T(8,128)} %get-tuple-element.25) | copy-start | bytes 1560580
  242.4 12.2 %copy-start.7 = (f32[32,4,8,127]{3,2,1,0:T(8,128)S(1)}, f32[32,4,8,127]{3,2,1,0:T(8,128)}, u32[]{:S(2)}) copy-start(f32[32,4,8,127]{3,2,1,0:T(8,128)} %get-tuple-element.26) | copy-start | bytes 1560580
  242.5 12.2 %copy-start.8 = (f32[32,4,8,1]{3,2,1,0:T(8,128)S(1)}, f32[32,4,8,1]{3,2,1,0:T(8,128)}, u32[]{:S(2)}) copy-start(f32[32,4,8,1]{3,2,1,0:T(8,128)} %get-tuple-element.27) | copy-start | bytes 12292
  242.5 12.2 %copy-start.9 = (f32[32,4,8,1]{3,2,1,0:T(8,128)S(1)}, f32[32,4,8,1]{3,2,1,0:T(8,128)}, u32[]{:S(2)}) copy-start(f32[32,4,8,1]{3,2,1,0:T(8,128)} %get-tuple-element.28) | copy-start | bytes 12292
  242.5 12.2 %copy-start.23 = (f32[32]{0:T(128)S(1)}, f32[32]{0:T(128)}, u32[]{:S(2)}) copy-start(f32[32]{0:T(128)} %get-tuple-element.106) | copy-start | bytes 388
  242.6 11.9 %collective-permute-start.15 = (f32[32,8,2,128]{3,1,2,0:T(8,128)S(1)}, f32[32,8,2,128]{3,1,2,0:T(8,128)S(1)}, u32[]{:S(2)}, u32[]{:S(2)}) collective-permute-start(f32[32,8,2,128]{3,1,2,0:T(8,128)S(1)} %copy.565), channel_id=1, source_target_pairs={{32,0},{64,32},{96,64},{0,96},{33,1},{65,33},{97,65},{1,97},{34,2}... | collective-permute-start | bytes 786440 | tf_op jit(solution)/shard_map/ppermute | solution.py:27
  260.7 226.9 %collective-permute-start.28 = (f32[32,2,8,128]{3,2,1,0:T(8,128)}, f32[32,2,8,128]{3,2,1,0:T(8,128)}, u32[]{:S(2)}, u32[]{:S(2)}) collective-permute-start(f32[32,2,8,128]{3,2,1,0:T(8,128)} %get-tuple-element.19), channel_id=1, source_target_pairs={{0,128},{128,256},{256,384},{384,0},{1,129},{129,257},{257,385},{3... | collective-permute-start | bytes 786440 | tf_op jit(solution)/shard_map/ppermute | solution.py:24
  262.6 224.9 %collective-permute-start.29 = (f32[32,2,8,128]{3,2,1,0:T(8,128)}, f32[32,2,8,128]{3,2,1,0:T(8,128)}, u32[]{:S(2)}, u32[]{:S(2)}) collective-permute-start(f32[32,2,8,128]{3,2,1,0:T(8,128)} %get-tuple-element.20), channel_id=1, source_target_pairs={{128,0},{256,128},{384,256},{0,384},{129,1},{257,129},{385,257},{1... | collective-permute-start | bytes 786440 | tf_op jit(solution)/shard_map/ppermute | solution.py:27
  417.3 7.5 %collective-permute-start.16 = (f32[5,1,8,128]{3,2,1,0:T(8,128)S(1)}, f32[5,1,8,128]{3,2,1,0:T(8,128)S(1)}, u32[]{:S(2)}, u32[]{:S(2)}) collective-permute-start(f32[5,1,8,128]{3,2,1,0:T(8,128)S(1)} %get-tuple-element.57), channel_id=1, source_target_pairs={{128,0},{256,128},{384,256},{0,384},{129,1},{257,129},{385,257},{1... | collective-permute-start | bytes 61448 | tf_op jit(solution)/shard_map/ppermute | solution.py:27
  422.8 6.3 %collective-permute-start.17 = (f32[5,1,8,128]{3,2,1,0:T(8,128)S(1)}, f32[5,1,8,128]{3,2,1,0:T(8,128)S(1)}, u32[]{:S(2)}, u32[]{:S(2)}) collective-permute-start(f32[5,1,8,128]{3,2,1,0:T(8,128)S(1)} %get-tuple-element.56), channel_id=1, source_target_pairs={{0,128},{128,256},{256,384},{384,0},{1,129},{129,257},{257,385},{3... | collective-permute-start | bytes 61448 | tf_op jit(solution)/shard_map/ppermute | solution.py:24
  429.1 15.3 %collective-permute-start.18 = (f32[5,6,1,128]{3,2,1,0:T(1,128)S(1)}, f32[5,6,1,128]{3,2,1,0:T(1,128)S(1)}, u32[]{:S(2)}, u32[]{:S(2)}) collective-permute-start(f32[5,6,1,128]{3,2,1,0:T(1,128)S(1)} %get-tuple-element.40), channel_id=1, source_target_pairs={{32,0},{64,32},{96,64},{0,96},{33,1},{65,33},{97,65},{1,97},{34,2}... | collective-permute-start | bytes 46088 | tf_op jit(solution)/shard_map/ppermute | solution.py:27
  437.7 6.8 %collective-permute-start.19 = (f32[5,6,1,128]{3,2,1,0:T(1,128)S(1)}, f32[5,6,1,128]{3,2,1,0:T(1,128)S(1)}, u32[]{:S(2)}, u32[]{:S(2)}) collective-permute-start(f32[5,6,1,128]{3,2,1,0:T(1,128)S(1)} %get-tuple-element.41), channel_id=1, source_target_pairs={{0,32},{32,64},{64,96},{96,0},{1,33},{33,65},{65,97},{97,1},{2,34}... | collective-permute-start | bytes 46088 | tf_op jit(solution)/shard_map/ppermute | solution.py:24
  446.8 5.4 %collective-permute-start.20 = (f32[5,1,4,64]{3,2,1,0:T(4,128)S(1)}, f32[5,1,4,64]{3,2,1,0:T(4,128)S(1)}, u32[]{:S(2)}, u32[]{:S(2)}) collective-permute-start(f32[5,1,4,64]{3,2,1,0:T(4,128)S(1)} %get-tuple-element.79), channel_id=1, source_target_pairs={{128,0},{256,128},{384,256},{0,384},{129,1},{257,129},{385,257},{1... | collective-permute-start | bytes 15368 | tf_op jit(solution)/shard_map/ppermute | solution.py:27
  448.7 6.2 %collective-permute-start.21 = (f32[5,1,4,64]{3,2,1,0:T(4,128)S(1)}, f32[5,1,4,64]{3,2,1,0:T(4,128)S(1)}, u32[]{:S(2)}, u32[]{:S(2)}) collective-permute-start(f32[5,1,4,64]{3,2,1,0:T(4,128)S(1)} %get-tuple-element.78), channel_id=1, source_target_pairs={{0,128},{128,256},{256,384},{384,0},{1,129},{129,257},{257,385},{3... | collective-permute-start | bytes 15368 | tf_op jit(solution)/shard_map/ppermute | solution.py:24
  454.9 10.3 %collective-permute-start.22 = (f32[5,4,1,64]{3,2,1,0:T(1,128)S(1)}, f32[5,4,1,64]{3,2,1,0:T(1,128)S(1)}, u32[]{:S(2)}, u32[]{:S(2)}) collective-permute-start(f32[5,4,1,64]{3,2,1,0:T(1,128)S(1)} %get-tuple-element.70), channel_id=1, source_target_pairs={{32,0},{64,32},{96,64},{0,96},{33,1},{65,33},{97,65},{1,97},{34,2}... | collective-permute-start | bytes 15368 | tf_op jit(solution)/shard_map/ppermute | solution.py:27
  460.2 5.7 %collective-permute-start.23 = (f32[5,4,1,64]{3,2,1,0:T(1,128)S(1)}, f32[5,4,1,64]{3,2,1,0:T(1,128)S(1)}, u32[]{:S(2)}, u32[]{:S(2)}) collective-permute-start(f32[5,4,1,64]{3,2,1,0:T(1,128)S(1)} %get-tuple-element.71), channel_id=1, source_target_pairs={{0,32},{32,64},{64,96},{96,0},{1,33},{33,65},{65,97},{97,1},{2,34}... | collective-permute-start | bytes 15368 | tf_op jit(solution)/shard_map/ppermute | solution.py:24
  467.9 26.1 %copy-start.17 = (f32[3,4096]{1,0:T(4,128)S(1)}, f32[3,4096]{1,0:T(4,128)}, u32[]{:S(2)}) copy-start(f32[3,4096]{1,0:T(4,128)} %slice.603) | copy-start | bytes 147460
  468.0 5.5 %collective-permute-start.24 = (f32[5,1,8,128]{3,2,1,0:T(8,128)S(1)}, f32[5,1,8,128]{3,2,1,0:T(8,128)S(1)}, u32[]{:S(2)}, u32[]{:S(2)}) collective-permute-start(f32[5,1,8,128]{3,2,1,0:T(8,128)S(1)} %get-tuple-element.51), channel_id=1, source_target_pairs={{128,0},{256,128},{384,256},{0,384},{129,1},{257,129},{385,257},{1... | collective-permute-start | bytes 61448 | tf_op jit(solution)/shard_map/ppermute | solution.py:27
  470.0 6.4 %collective-permute-start.25 = (f32[5,1,8,128]{3,2,1,0:T(8,128)S(1)}, f32[5,1,8,128]{3,2,1,0:T(8,128)S(1)}, u32[]{:S(2)}, u32[]{:S(2)}) collective-permute-start(f32[5,1,8,128]{3,2,1,0:T(8,128)S(1)} %get-tuple-element.50), channel_id=1, source_target_pairs={{0,128},{128,256},{256,384},{384,0},{1,129},{129,257},{257,385},{3... | collective-permute-start | bytes 61448 | tf_op jit(solution)/shard_map/ppermute | solution.py:24
  476.5 17.3 %collective-permute-start.26 = (f32[5,6,1,128]{3,2,1,0:T(1,128)S(1)}, f32[5,6,1,128]{3,2,1,0:T(1,128)S(1)}, u32[]{:S(2)}, u32[]{:S(2)}) collective-permute-start(f32[5,6,1,128]{3,2,1,0:T(1,128)S(1)} %get-tuple-element.38), channel_id=1, source_target_pairs={{32,0},{64,32},{96,64},{0,96},{33,1},{65,33},{97,65},{1,97},{34,2}... | collective-permute-start | bytes 46088 | tf_op jit(solution)/shard_map/ppermute | solution.py:27
  482.6 11.2 %collective-permute-start.27 = (f32[5,6,1,128]{3,2,1,0:T(1,128)S(1)}, f32[5,6,1,128]{3,2,1,0:T(1,128)S(1)}, u32[]{:S(2)}, u32[]{:S(2)}) collective-permute-start(f32[5,6,1,128]{3,2,1,0:T(1,128)S(1)} %get-tuple-element.39), channel_id=1, source_target_pairs={{0,32},{32,64},{64,96},{96,0},{1,33},{33,65},{65,97},{97,1},{2,34}... | collective-permute-start | bytes 46088 | tf_op jit(solution)/shard_map/ppermute | solution.py:24
  489.0 8.0 %collective-permute-start.30 = (f32[32,8,2,128]{3,1,2,0:T(8,128)S(1)}, f32[32,8,2,128]{3,1,2,0:T(8,128)S(1)}, u32[]{:S(2)}, u32[]{:S(2)}) collective-permute-start(f32[32,8,2,128]{3,1,2,0:T(8,128)S(1)} %copy.573), channel_id=1, source_target_pairs={{0,32},{32,64},{64,96},{96,0},{1,33},{33,65},{65,97},{97,1},{2,34}... | collective-permute-start | bytes 786440 | tf_op jit(solution)/shard_map/ppermute | solution.py:24
  491.4 12.2 %copy-start.10 = (f32[32,4,8,126]{3,2,1,0:T(8,128)S(1)}, f32[32,4,8,126]{3,2,1,0:T(8,128)}, u32[]{:S(2)}) copy-start(f32[32,4,8,126]{3,2,1,0:T(8,128)} %get-tuple-element.12) | copy-start | bytes 1548292
  491.4 12.2 %copy-start.11 = (f32[32,4,8,2]{3,2,1,0:T(8,128)S(1)}, f32[32,4,8,2]{3,2,1,0:T(8,128)}, u32[]{:S(2)}) copy-start(f32[32,4,8,2]{3,2,1,0:T(8,128)} %get-tuple-element.13) | copy-start | bytes 24580
  491.4 12.2 %copy-start.12 = (f32[32,4,8,2]{3,2,1,0:T(8,128)S(1)}, f32[32,4,8,2]{3,2,1,0:T(8,128)}, u32[]{:S(2)}) copy-start(f32[32,4,8,2]{3,2,1,0:T(8,128)} %get-tuple-element.14) | copy-start | bytes 24580
  491.4 12.2 %copy-start.13 = (f32[32,4,8,127]{3,2,1,0:T(8,128)S(1)}, f32[32,4,8,127]{3,2,1,0:T(8,128)}, u32[]{:S(2)}) copy-start(f32[32,4,8,127]{3,2,1,0:T(8,128)} %get-tuple-element.15) | copy-start | bytes 1560580
  491.4 12.2 %copy-start.14 = (f32[32,4,8,127]{3,2,1,0:T(8,128)S(1)}, f32[32,4,8,127]{3,2,1,0:T(8,128)}, u32[]{:S(2)}) copy-start(f32[32,4,8,127]{3,2,1,0:T(8,128)} %get-tuple-element.16) | copy-start | bytes 1560580
  491.5 12.2 %copy-start.15 = (f32[32,4,8,1]{3,2,1,0:T(8,128)S(1)}, f32[32,4,8,1]{3,2,1,0:T(8,128)}, u32[]{:S(2)}) copy-start(f32[32,4,8,1]{3,2,1,0:T(8,128)} %get-tuple-element.17) | copy-start | bytes 12292
  491.5 12.2 %copy-start.16 = (f32[32,4,8,1]{3,2,1,0:T(8,128)S(1)}, f32[32,4,8,1]{3,2,1,0:T(8,128)}, u32[]{:S(2)}) copy-start(f32[32,4,8,1]{3,2,1,0:T(8,128)} %get-tuple-element.18) | copy-start | bytes 12292
  491.5 12.2 %copy-start.20 = (f32[32]{0:T(128)S(1)}, f32[32]{0:T(128)}, u32[]{:S(2)}) copy-start(f32[32]{0:T(128)} %copy-done.19) | copy-start | bytes 388
  491.5 12.2 %copy-start.22 = (f32[32]{0:T(128)S(1)}, f32[32]{0:T(128)}, u32[]{:S(2)}) copy-start(f32[32]{0:T(128)} %copy-done.21) | copy-start | bytes 388
  491.5 12.2 %copy-start.24 = (f32[32]{0:T(128)S(1)}, f32[32]{0:T(128)}, u32[]{:S(2)}) copy-start(f32[32]{0:T(128)} %get-tuple-element.106) | copy-start | bytes 388
  491.5 12.2 %copy-start.26 = (f32[32]{0:T(128)S(1)}, f32[32]{0:T(128)}, u32[]{:S(2)}) copy-start(f32[32]{0:T(128)} %get-tuple-element.107) | copy-start | bytes 388
  491.5 12.2 %copy-start.28 = (f32[32]{0:T(128)S(1)}, f32[32]{0:T(128)}, u32[]{:S(2)}) copy-start(f32[32]{0:T(128)} %get-tuple-element.108) | copy-start | bytes 388
  491.5 12.2 %copy-start.30 = (f32[32]{0:T(128)S(1)}, f32[32]{0:T(128)}, u32[]{:S(2)}) copy-start(f32[32]{0:T(128)} %get-tuple-element.92) | copy-start | bytes 388
  491.5 12.2 %copy-start.32 = (f32[32]{0:T(128)S(1)}, f32[32]{0:T(128)}, u32[]{:S(2)}) copy-start(f32[32]{0:T(128)} %get-tuple-element.93) | copy-start | bytes 388
  491.6 12.2 %copy-start.34 = (f32[32]{0:T(128)S(1)}, f32[32]{0:T(128)}, u32[]{:S(2)}) copy-start(f32[32]{0:T(128)} %get-tuple-element.102) | copy-start | bytes 388
  491.6 11.9 %collective-permute-start.31 = (f32[32,8,2,128]{3,1,2,0:T(8,128)S(1)}, f32[32,8,2,128]{3,1,2,0:T(8,128)S(1)}, u32[]{:S(2)}, u32[]{:S(2)}) collective-permute-start(f32[32,8,2,128]{3,1,2,0:T(8,128)S(1)} %copy.575), channel_id=1, source_target_pairs={{32,0},{64,32},{96,64},{0,96},{33,1},{65,33},{97,65},{1,97},{34,2}... | collective-permute-start | bytes 786440 | tf_op jit(solution)/shard_map/ppermute | solution.py:27
  (7 other events, 74.0 us)
Sparse Core Ops, SparseCore 0:
  10.8 157.6 all-reduce.2
  270.7 145.3 all-reduce.4
where the time goes:
time: 515 us; the launch traced here: 514 us
  waiting for transfers between devices  322 us (63%)
  starting transfers between devices  134 us (26%)
  local copies, waits for them, and re-layouts  22.6 us (4%)
  between operations  14.7 us (3%)
  other arithmetic  12.5 us (2%)
  matrix products  7.46 us (1%)
    psum x2, waiting for transfers between devices, local(): summed = lax.psum(local_moments, 'vert')  285 us
    ppermute x16, starting transfers between devices, padded_2(): lax.ppermute(lax.slice_in_dim(block, 0, width, axis=dim), axis, backward)  75.8 us
    ppermute x16, starting transfers between devices, padded_2(): lax.ppermute(lax.slice_in_dim(block, block.shape[dim] - width, None, axis...  58.6 us
    ppermute x16, waiting for transfers between devices, padded_2(): lax.ppermute(lax.slice_in_dim(block, block.shape[dim] - width, None, axis...  24.8 us
    ppermute x16, waiting for transfers between devices, padded_2(): lax.ppermute(lax.slice_in_dim(block, 0, width, axis=dim), axis, backward)  12.7 us
  transfers between devices with their start and end apart: 34, of which 14 were waited for; matrix products, arithmetic and copies ran while one was open for 6% of the time, Pallas kernels for 0%

commit v1 on v0

v1 whole, which is shorter than its diff:
```python
import jax
import jax.numpy as jnp
import numpy as np
from jax import lax
from jax.experimental import pallas as pl
from jax.experimental.pallas import tpu as pltpu
from jax.sharding import PartitionSpec as P

V = 1024
INTERPRET = False

absorb = 0.5
damping = 0.8
fine_diag = 6.5
prandtl = 2.0 / 3.0

SX, SY, NZ = 4, 8, 128
COLS = SX * SY
ROWS = 8
LANES = ROWS * COLS
BLOCKS = 16
WIN = 24
WIN2 = 16
F32 = jnp.float32


def roll(x, shift, axis):
    return pltpu.roll(x, shift % x.shape[axis], axis)


def iota(shape, dim):
    return lax.broadcasted_iota(jnp.int32, shape, dim)


def velocity_tables(vel_index, signs, coupling):
    speeds = (vel_index.astype(F32) + 0.5) * 0.25
    positive = signs.astype(F32)
    veloc = speeds * (positive * 2.0 - 1.0)
    square = jnp.sum(veloc * veloc, axis=0)
    weight = 64.0 * jnp.exp(-square) / V
    vel_x, vel_y, vel_z = (veloc[0], veloc[1], veloc[2])
    unit_row = jnp.ones_like(vel_x)
    heat_term = square - 2.5
    basis = (
        jnp.stack(
            [
                unit_row,
                vel_x,
                vel_y,
                vel_z,
                square - 1.5,
                vel_x * vel_y,
                vel_x * vel_z,
                vel_y * vel_z,
                vel_x * vel_x - vel_y * vel_y,
                vel_y * vel_y - vel_z * vel_z,
                heat_term * vel_x,
                heat_term * vel_y,
                heat_term * vel_z,
            ]
        )
        * weight[None]
    )
    shakhov = 0.8 * (1.0 - prandtl)
    equil = jnp.stack(
        [
            unit_row,
            2.0 * vel_x,
            2.0 * vel_y,
            2.0 * vel_z,
            2.0 / 3.0 * (square - 1.5),
            shakhov * heat_term * vel_x,
            shakhov * heat_term * vel_y,
            shakhov * heat_term * vel_z,
        ]
    )
    mixed = jnp.sum(coupling[:, :, None] * basis[None, 5:13], axis=1)
    source_basis = jnp.concatenate([absorb * basis[0:5] + mixed, basis[10:13]], axis=0)
    centre = 0.5 - 0.3 * jnp.sum(speeds, axis=0)
    table = jnp.concatenate(
        [
            source_basis,
            equil,
            centre[None],
            0.4 * speeds * positive,
            0.4 * speeds * (1.0 - positive),
            jnp.zeros_like(centre)[None],
        ],
        axis=0,
    ).T
    cross = jnp.sum(source_basis[:, None] * equil[None], axis=2)
    cross_row = jnp.pad(cross, ((0, 0), (0, COLS - ROWS))).reshape(1, LANES)
    return table, cross_row


def moments(src, table, m_scr, ext):
    zero = jnp.zeros((SY, NZ), F32)

    def step(v, accs):
        tiles = [src[v, x] for x in range(SX)]
        out = []
        for r in range(ROWS):
            w = table[v, r]
            out += [accs[r * SX + x] + w * tiles[x] for x in range(SX)]
        return tuple(out)

    accs = lax.fori_loop(0, src.shape[0], step, (zero,) * (ROWS * SX), unroll=2)
    for i, acc in enumerate(accs):
        m_scr[i * SY : (i + 1) * SY, :] = acc
    for h in range(2):
        turned = m_scr[h * 128 : (h + 1) * 128, :].T
        lanes = slice(h * 128, (h + 1) * 128)
        ext[16:144, lanes] = turned
        ext[0:16, lanes] = turned[112:128]
        ext[144:168, lanes] = turned[0:24]


def first_kernel(table, f, win, north, south, m_scr, ext):
    moments(f, table, m_scr, ext)
    for j in range(win.shape[0]):
        win[j] = ext[4 * j + 6 : 4 * j + 6 + WIN, :]
    pack_rows(f, north, south)


def pack_rows(src, north, south):
    pair = iota((SY, NZ), 0) // 2

    def step(v, carry):
        top = roll(src[v, 0], 0, 0)
        low = roll(src[v, 0], -6, 0)
        for x in range(1, SX):
            tile = src[v, x]
            top = jnp.where(pair == x, roll(tile, 2 * x, 0), top)
            low = jnp.where(pair == x, roll(tile, 2 * x - 6, 0), low)
        north[v] = top
        south[v] = low
        return carry

    lax.fori_loop(0, src.shape[0], step, 0, unroll=4)


def row_halo(north, south, x, sub):
    return jnp.where(sub < 4, roll(north, -2 * x, 0), roll(south, 6 - 2 * x, 0))


def transport(table, v, tiles, edges, sub):
    centre = table[v, 16]
    up = [table[v, 17 + d] for d in range(3)]
    down = [table[v, 20 + d] for d in range(3)]
    out = []
    for x in range(SX):
        f = tiles[x + 2]
        e = edges[x]
        acc = centre * f
        acc += up[0] * (tiles[x + 1] - 0.25 * tiles[x])
        acc += down[0] * (tiles[x + 3] - 0.25 * tiles[x + 4])
        back_one = roll(jnp.where(sub >= 7, e, f), 1, 0)
        back_two = roll(jnp.where(sub >= 6, e, f), 2, 0)
        front_one = roll(jnp.where(sub < 1, e, f), -1, 0)
        front_two = roll(jnp.where(sub < 2, e, f), -2, 0)
        acc += up[1] * (back_one - 0.25 * back_two)
        acc += down[1] * (front_one - 0.25 * front_two)
        acc += up[2] * (roll(f, 1, 1) - 0.25 * roll(f, 2, 1))
        acc += down[2] * (roll(f, -1, 1) - 0.25 * roll(f, -2, 1))
        out.append(acc)
    return out


def second_kernel(table, f, low, high, north, south, fluid, cross, g, win, g_north, g_south, m_scr, ext):
    sub = iota((SY, NZ), 0)

    def step(v, carry):
        tiles = [low[v, 0], low[v, 1]] + [f[v, x] for x in range(SX)] + [high[v, 0], high[v, 1]]
        above, below = north[v], south[v]
        edges = [row_halo(above, below, x, sub) for x in range(SX)]
        moved = transport(table, v, tiles, edges, sub)
        for x in range(SX):
            g[v, x] = fluid[x] * moved[x]
        return carry

    lax.fori_loop(0, f.shape[0], step, 0, unroll=2)
    moments(g, table, m_scr, ext)
    for j in range(win.shape[0]):
        win[j] = ext[4 * j + 10 : 4 * j + 10 + WIN2, :]
        win[j, 0:1, :] = cross[...]
    pack_rows(g, g_north, g_south)


def solve_kernel(place, recv, coef, out, src, coarse, fine, gain, extra, first, msg):
    shape = (2 * WIN, 128)
    lane = iota(shape, 1)
    x_at = (lane // SY) % SX
    y_at = lane % SY
    z_odd = iota(shape, 0) % 2
    is_field = (iota(shape, 0) // WIN) * 4 + lane // COLS < 5
    tile_sub = iota((8, 128), 0)
    tile_lane = iota((8, 128), 1)

    def unpack(i, carry):
        for h in range(2):
            lanes = slice(h * 128, (h + 1) * 128)
            src[i, h * WIN : (h + 1) * WIN, :] = recv[i, 0:WIN, lanes]
            extra[i, h * WIN : h * WIN + 4, :] = jnp.zeros((4, 128), F32)
            extra[i, h * WIN + 20 : (h + 1) * WIN, :] = jnp.zeros((4, 128), F32)
            extra[i, h * WIN + 4 : h * WIN + 20, :] = recv[i, WIN : WIN + WIN2, lanes]
        gain[i] = jnp.zeros(shape, F32)
        for half, at in enumerate((WIN, WIN + WIN2 - 1)):
            left = jnp.broadcast_to(recv[i, at : at + 1, 0:128], (8, 128))
            right = jnp.broadcast_to(recv[i, at : at + 1, 128:256], (8, 128))
            t = jnp.where(tile_sub < 4, left, right)
            t = jnp.where(tile_lane // COLS == tile_sub % 4, t, 0.0)
            t = t + roll(t, 32, 1)
            t = t + roll(t, 64, 1)
            for h in range(2):
                gain[i, h * WIN + 4 + 8 * half : h * WIN + 12 + 8 * half, :] = t
        return carry

    lax.fori_loop(0, BLOCKS, unpack, 0)

    def around(i):
        gx, gy = i // 4, i % 4
        return (
            ((gx + 1) % 4) * 4 + gy,
            ((gx + 3) % 4) * 4 + gy,
            gx * 4 + (gy + 1) % 4,
            gx * 4 + (gy + 3) % 4,
        )

    def neighbours(ref, i, step):
        next_x, last_x, next_y, last_y = around(i)
        c = ref[i]
        dx, dy = SY * step, step
        total = jnp.where(x_at < SX - step, roll(c, -dx, 1), roll(ref[next_x], COLS - dx, 1))
        total += jnp.where(x_at >= step, roll(c, dx, 1), roll(ref[last_x], dx - COLS, 1))
        total += jnp.where(y_at < SY - step, roll(c, -dy, 1), roll(ref[next_y], SY - dy, 1))
        total += jnp.where(y_at >= step, roll(c, dy, 1), roll(ref[last_y], dy - SY, 1))
        return total + roll(c, step, 0) + roll(c, -step, 0)

    def restrict(i, carry):
        r = (1.0 - damping) * src[i] + (damping / fine_diag) * neighbours(src, i, 1)
        r = r + jnp.where(x_at % 2 == 0, roll(r, -SY, 1), roll(r, SY, 1))
        r = r + jnp.where(y_at % 2 == 0, roll(r, -1, 1), roll(r, 1, 1))
        r = r + jnp.where(z_odd == 0, roll(r, -1, 0), roll(r, 1, 0))
        coarse[i] = 0.125 * r
        return carry

    def correct(i, carry):
        two = 0.48 * coarse[i] + 0.04 * neighbours(coarse, i, 2)
        fine[i] = (damping / fine_diag) * src[i] + two
        return carry

    def smooth(i):
        y = (1.0 - damping) * fine[i] + (damping / fine_diag) * (src[i] + neighbours(fine, i, 1))
        return jnp.where(is_field, y, src[i])

    def mix(i, carry):
        field = smooth(i)
        first[i] = gain[i] * field
        parts = (field[0:WIN], field[WIN : 2 * WIN])
        here = lane[0:WIN]
        sums = [0.0, 0.0]
        for b in range(4):
            turned = [roll(p, -COLS * b, 1) for p in parts]
            near = here < 128 - COLS * b
            same = [
                jnp.where(near, turned[0], turned[1]),
                jnp.where(near, turned[1], turned[0]),
            ]
            for h in range(2):
                lanes = slice(h * 128, (h + 1) * 128)
                sums[h] = (
                    sums[h]
                    + coef[b : b + 1, lanes] * same[h]
                    + coef[4 + b : 5 + b, lanes] * same[1 - h]
                )
        for h in range(2):
            rows = slice(h * WIN, (h + 1) * WIN)
            coarse[i, rows, :] = gain[i, rows, :] * sums[h] + extra[i, rows, :]
        return carry

    def swap(i, carry):
        src[i] = coarse[i]
        return carry

    lax.fori_loop(0, BLOCKS, restrict, 0)
    lax.fori_loop(0, BLOCKS, correct, 0)
    lax.fori_loop(0, BLOCKS, mix, 0)
    lax.fori_loop(0, BLOCKS, swap, 0)
    lax.fori_loop(0, BLOCKS, restrict, 0)
    own = place[0]
    next_x, last_x, next_y, last_y = around(own)
    for i in (own, next_x, last_x, next_y, last_y):
        correct(i, 0)
    second = gain[own] * smooth(own)
    side_x = jnp.where(x_at < 2, roll(first[last_x], -16, 1), roll(first[next_x], 16, 1))
    side_y = jnp.where(y_at < 4, first[next_y], first[last_y])
    pieces = ((first[own], side_x), (side_y, second))
    for k in range(2):
        for m in range(2):
            for h in range(2):
                at = (2 * m + h) * 128
                coarse[0] = pieces[k][m]
                msg[4 * k : 4 * k + 4, at : at + 128] = coarse[0, h * WIN + 10 : h * WIN + 14, :]
    for j in range(out.shape[0]):
        out[j] = msg[...]


def last_kernel(table, recv, g, low, high, north, south, fluid, out, turn, fields):
    for j in range(recv.shape[0]):
        turn[4 * j : 4 * j + 4, 0:512] = recv[j, 0:4, :]
        turn[4 * j : 4 * j + 4, 512:1024] = recv[j, 4:8, :]
    for k in range(8):
        block = turn[:, k * 128 : (k + 1) * 128].T
        for r in range(4):
            for x in range(SX):
                at = (r * SX + x) * SY
                fields[k // 2, (k % 2) * 4 + r, x] = block[at : at + SY]
    sub = iota((SY, NZ), 0)

    def step(v, carry):
        psi = [table[v, ROWS + r] for r in range(ROWS)]

        def lift(part, x):
            total = psi[0] * fields[part, 0, x]
            for r in range(1, ROWS):
                total += psi[r] * fields[part, r, x]
            return total

        above, below = north[v], south[v]
        tiles = [lift(1, x) + low[v, x] for x in range(2)]
        tiles += [lift(0, x) + g[v, x] for x in range(SX)]
        tiles += [lift(1, 2 + x) + high[v, x] for x in range(2)]
        edges = [lift(2, x) + row_halo(above, below, x, sub) for x in range(SX)]
        moved = transport(table, v, tiles, edges, sub)
        for x in range(SX):
            out[v, x] = fluid[x] * moved[x] + lift(3, x)
        return carry

    lax.fori_loop(0, out.shape[0], step, 0)


VMEM = pltpu.MemorySpace.VMEM
SMEM = pltpu.MemorySpace.SMEM


def call(kernel, spaces, outs, scratch):
    specs = [pl.BlockSpec(memory_space=s) for s in spaces]
    shapes = [jax.ShapeDtypeStruct(s, F32) for s in outs]
    return pl.pallas_call(
        kernel,
        in_specs=specs,
        out_specs=[pl.BlockSpec(memory_space=VMEM) for _ in outs],
        out_shape=shapes,
        scratch_shapes=[pltpu.VMEM(s, F32) for s in scratch],
        interpret=INTERPRET,
        name=kernel.__name__,
    )


def stage_first(f, table, members):
    vels = f.shape[0]
    return call(
        first_kernel,
        (SMEM, VMEM),
        ((members, WIN, LANES), (vels, SY, NZ), (vels, SY, NZ)),
        ((LANES, NZ), (168, LANES)),
    )(table, f)


def stage_second(f, table, low, high, north, south, fluid, cross, members):
    vels = f.shape[0]
    return call(
        second_kernel,
        (SMEM,) + (VMEM,) * 7,
        (f.shape, (members, WIN2, LANES), (vels, SY, NZ), (vels, SY, NZ)),
        ((LANES, NZ), (168, LANES)),
    )(table, f, low, high, north, south, fluid, cross)


def wall_rows(cell_type, member):
    gain = jnp.where(cell_type == 1, 1.0, 0.5).astype(F32).reshape(COLS, NZ).T
    wrapped = jnp.concatenate([gain[NZ - 8 :], gain, gain[:16]], axis=0)
    return lax.dynamic_slice_in_dim(wrapped, 4 * member + 2, WIN2, axis=0).reshape(2, LANES)


def stage_middle(got_one, got_two, walls):
    one = jnp.sum(got_one, axis=0)
    two = jnp.sum(got_two, axis=0)
    whole = jnp.concatenate([one, walls[0:1], two[1 : WIN2 - 1], walls[1:2]], axis=0)
    cross = two[0].reshape(ROWS, COLS)[:, :ROWS]
    pick = np.zeros((ROWS, ROWS, ROWS), np.float32)
    for k in range(ROWS):
        for r in range(ROWS):
            pick[k, r, (r + k) % ROWS] = 1.0
    coef = jnp.sum(jnp.asarray(pick) * cross[None], axis=2)
    coef = jnp.broadcast_to(coef[:, :, None], (ROWS, ROWS, COLS)).reshape(ROWS, LANES)
    return jnp.broadcast_to(whole[None], (BLOCKS,) + whole.shape), coef


def stage_solve(place, got, coef, members):
    big = (BLOCKS, 2 * WIN, 128)
    return call(
        solve_kernel,
        (SMEM, VMEM, VMEM),
        ((members, 8, 512),),
        (big,) * 6 + ((8, 512),),
    )(place, got, coef)[0]


def stage_last(table, got, g, low, high, north, south, fluid):
    return call(
        last_kernel,
        (SMEM,) + (VMEM,) * 7,
        (g.shape,),
        ((NZ, 1024), (4, ROWS, SX, SY, NZ)),
    )(table, got, g, low, high, north, south, fluid)[0]


def halos(f, north, south):
    def ring(axis, step):
        count = lax.axis_size(axis)
        return [(i, (i + step) % count) for i in range(count)]

    low = lax.ppermute(f[:, SX - 2 :], "gx", ring("gx", 1))
    high = lax.ppermute(f[:, :2], "gx", ring("gx", -1))
    above = lax.ppermute(north, "gy", ring("gy", -1))
    below = lax.ppermute(south, "gy", ring("gy", 1))
    return low, high, above, below


def swap_all(x, axis):
    return lax.all_to_all(x, axis, 0, 0, tiled=True)


def local(f, vel_index, signs, cell_type, coupling):
    members = lax.axis_size("vert")
    table, cross = velocity_tables(vel_index, signs, coupling)
    fluid = jnp.where(cell_type == 1, 0.0, 1.0).astype(F32)
    walls = wall_rows(cell_type, lax.axis_index("vert"))
    place = (lax.axis_index("gx") * 4 + lax.axis_index("gy")).astype(jnp.int32).reshape(1)
    win_one, north, south = stage_first(f, table, members)
    got_one = swap_all(win_one, "vert")
    near = halos(f, north, south)
    g, win_two, north, south = stage_second(f, table, *near, fluid, cross, members)
    got_two = swap_all(win_two, "vert")
    near = halos(g, north, south)
    whole, coef = stage_middle(got_one, got_two, walls)
    got = swap_all(whole, ("gx", "gy"))
    sent = stage_solve(place, got, coef, members)
    got = swap_all(sent, "vert")
    return stage_last(table, got, g, *near, fluid)


def solution(mesh):
    in_specs = (
        P("vert", "gx", "gy", None),
        P(None, "vert"),
        P(None, "vert"),
        P("gx", "gy", None),
        P(),
    )
    out_specs = P("vert", "gx", "gy", None)
    return jax.shard_map(local, mesh=mesh, in_specs=in_specs, out_specs=out_specs, check_vma=False)
```

time: 515 us -> 173 us (0.34)
  waiting for transfers between devices: 322 us -> 39 us
  starting transfers between devices: 134 us -> 65 us
  Pallas kernels: 0 us -> 32.3 us
  blocking collectives: 0 us -> 22.5 us
  between operations: 14.7 us -> 0.34 us
  local copies, waits for them, and re-layouts: 22.6 us -> 10.8 us
  other arithmetic: 12.5 us -> 1.49 us
  matrix products: 7.46 us -> 0 us
    psum x2 -> x0, waiting for transfers between devices: 285 us -> none  [local(): summed = lax.psum(local_moments, 'vert')]
    ppermute x32 -> x8, starting transfers between devices: 134 us -> 35.9 us  [the longest x2 13.3 us: halos(): below = lax.ppermute(south, 'gy', ring('gy', 1))]
    all_to_all x0 -> x3, waiting for transfers between devices: none -> 33.1 us  [swap_all(): return lax.all_to_all(x, axis, 0, 0, tiled=True)]
    pallas_call x0 -> x4, Pallas kernels: none -> 32.3 us  [the longest x1 19.1 us: stage_solve(): call(solve_kernel, (SMEM, VMEM, VMEM), ((members, 8, 512),), (big,) * 6 +...]
    ppermute x32 -> x8, waiting for transfers between devices: 37.5 us -> 5.96 us  [the longest x2 4.95 us: halos(): above = lax.ppermute(north, 'gy', ring('gy', -1))]
    all_to_all x0 -> x3, starting transfers between devices: none -> 29.1 us  [swap_all(): return lax.all_to_all(x, axis, 0, 0, tiled=True)]
    all_to_all x0 -> x1, blocking collectives: none -> 22.5 us  [swap_all(): return lax.all_to_all(x, axis, 0, 0, tiled=True)]
    slice x35 -> x14, local copies, waits for them, and re-layouts: 15.3 us -> 1.86 us  [the longest x2 1.11 us: halos(): high = lax.ppermute(f[:, :2], 'gx', ring('gx', -1))]
  transfers between devices with their start and end apart: 34 -> 11, of which waited for: 14 -> 4; matrix products, arithmetic and copies ran while one was open for 6% -> 3% of each run, Pallas kernels for 0% -> 2%
where the time goes in v1:
time: 173 us; the launch traced here: 172 us
  starting transfers between devices  65 us (38%)
  waiting for transfers between devices  39 us (23%)
  Pallas kernels  32.3 us (19%)
  blocking collectives  22.5 us (13%)
  local copies, waits for them, and re-layouts  10.8 us (6%)
    all_to_all x3, waiting for transfers between devices, swap_all(): return lax.all_to_all(x, axis, 0, 0, tiled=True)  33.1 us
    all_to_all x3, starting transfers between devices, swap_all(): return lax.all_to_all(x, axis, 0, 0, tiled=True)  29.1 us
    all_to_all x1, blocking collectives, swap_all(): return lax.all_to_all(x, axis, 0, 0, tiled=True)  22.5 us
    pallas_call x1, Pallas kernels, stage_solve(): call(solve_kernel, (SMEM, VMEM, VMEM), ((members, 8, 512),), (big,) * 6 +...  19.1 us
    ppermute x2, starting transfers between devices, halos(): below = lax.ppermute(south, 'gy', ring('gy', 1))  13.3 us
    ppermute x2, starting transfers between devices, halos(): high = lax.ppermute(f[:, :2], 'gx', ring('gx', -1))  10.9 us
    ppermute x2, starting transfers between devices, halos(): above = lax.ppermute(north, 'gy', ring('gy', -1))  6.89 us
    pallas_call x1, Pallas kernels, stage_last(): call(last_kernel, (SMEM,) + (VMEM,) * 7, (g.shape,), ((NZ, 1024), (4, ROW...  5.83 us
  transfers between devices with their start and end apart: 11, of which 4 were waited for; matrix products, arithmetic and copies ran while one was open for 3% of the time, Pallas kernels for 2%

profile of v1, /device:TPU:1, one launch (start us, length us, event | category | flops | bytes accessed | tf_op | source)
XLA Modules:
  0.0 171.5 jit_solution(6478178770493803003)
XLA Ops:
  0.0 1.1 fusion.4
  1.1 8.4 %collective-permute-start.1 = (f32[32,2,8,128]{3,2,1,0:T(8,128)S(1)}, f32[32,2,8,128]{3,2,1,0:T(8,128)S(1)}, u32[]{:S(2)}, u32[]{:S(2)}) collective-permute-start(f32[32,2,8,128]{3,2,1,0:T(8,128)S(1)} %get-tuple-element.25), channel_id=1, source_target_pairs={{0,384},{128,0},{256,128},{384,256},{1,385},{129,1},{257,129},{385... | collective-permute-start | bytes 786440 | tf_op jit(solution)/shard_map/ppermute | solution.py:425
  9.5 1.9 %collective-permute-start = (f32[32,2,8,128]{3,2,1,0:T(8,128)S(1)}, f32[32,2,8,128]{3,2,1,0:T(8,128)S(1)}, u32[]{:S(2)}, u32[]{:S(2)}) collective-permute-start(f32[32,2,8,128]{3,2,1,0:T(8,128)S(1)} %get-tuple-element.26), channel_id=1, source_target_pairs={{0,128},{128,256},{256,384},{384,0},{1,129},{129,257},{257,385},{3... | collective-permute-start | bytes 786440 | tf_op jit(solution)/shard_map/ppermute | solution.py:424
  11.5 0.1 copy.77
  11.6 0.6 copy-done.14
  12.2 0.1 copy.79
  12.3 0.1 subtract_multiply_fusion
  12.4 0.1 copy.83
  12.5 0.1 copy.80
  12.6 0.1 multiply_multiply_fusion
  12.7 0.1 stack.5
  12.9 0.1 slice.82
  13.1 0.1 copy.94
  13.2 0.6 copy-done.13
  13.9 0.1 multiply_reduce_fusion.2
  14.0 0.1 copy.86
  14.1 0.7 concatenate.13
  14.8 2.7 %first_kernel.1 = (f32[32,24,256]{2,1,0:T(8,128)}, f32[32,8,128]{2,1,0:T(8,128)}, f32[32,8,128]{2,1,0:T(8,128)}) custom-call(f32[32,24]{1,0:T(8,128)} %bitcast.14, f32[32,4,8,128]{3,2,1,0:T(8,128)} %f.3), custom_call_target="tpu_custom_call" | custom-call | tf_op jit(solution)/shard_map/first_kernel/pallas_call | solution.py:362
  17.5 4.2 %collective-permute-start.2 = (f32[32,8,128]{2,1,0:T(8,128)}, f32[32,8,128]{2,1,0:T(8,128)S(1)}, u32[]{:S(2)}, u32[]{:S(2)}) collective-permute-start(f32[32,8,128]{2,1,0:T(8,128)} %get-tuple-element.13), channel_id=1, source_target_pairs={{0,96},{32,0},{64,32},{96,64},{1,97},{33,1},{65,33},{97,65},{2,98}... | collective-permute-start | bytes 393224 | tf_op jit(solution)/shard_map/ppermute | solution.py:426
  21.7 6.5 %collective-permute-start.3 = (f32[32,8,128]{2,1,0:T(8,128)}, f32[32,8,128]{2,1,0:T(8,128)S(1)}, u32[]{:S(2)}, u32[]{:S(2)}) collective-permute-start(f32[32,8,128]{2,1,0:T(8,128)} %get-tuple-element.14), channel_id=1, source_target_pairs={{0,32},{32,64},{64,96},{96,0},{1,33},{33,65},{65,97},{97,1},{2,34}... | collective-permute-start | bytes 393224 | tf_op jit(solution)/shard_map/ppermute | solution.py:427
  28.2 0.1 copy.100
  28.2 0.1 copy.102
  28.3 0.1 copy.105
  28.4 0.1 copy.104
  28.5 0.1 copy.103
  28.5 0.1 copy.99
  28.6 0.1 copy.101
  28.7 0.1 copy.97
  28.8 0.1 copy.96
  28.9 0.1 multiply_reduce_fusion.1
  29.0 0.7 reshape.79.cross
  29.7 0.6 broadcast_select_fusion
  30.3 1.0 collective-permute-done.3.south
  31.3 0.6 copy-done.8
  32.0 0.1 copy-done.5
  32.1 0.1 copy-done.6
  32.2 4.7 %second_kernel.1 = (f32[32,4,8,128]{3,2,1,0:T(8,128)}, f32[32,16,256]{2,1,0:T(8,128)}, f32[32,8,128]{2,1,0:T(8,128)}, f32[32,8,128]{2,1,0:T(8,128)}) custom-call(f32[32,24]{1,0:T(8,128)} %bitcast.15, f32[32,4,8,128]{3,2,1,0:T(8,128)} %f.3, f32[32,2,8,128]{3,2,1,0:T(8,128)} %copy-done.6, f32[32,2,8,128]{3,2,1,0:T(8,128)} %copy-done.5, ...), custom_call_target="tpu_custom_call" | custom-call | tf_op jit(solution)/shard_map/second_kernel/pallas_call | solution.py:372
  36.9 22.5 %all_to_all.20 = f32[32,16,256]{2,1,0:T(8,128)S(1)} all-to-all(f32[32,16,256]{2,1,0:T(8,128)} %get-tuple-element.15), channel_id=1, replica_groups=mesh['gx'=4,'gy'=4,'vert'=32] {'vert'}, dimensions={0} | all-to-all | bytes 1048576 | tf_op jit(solution)/shard_map/all_to_all | solution.py:432
  59.3 4.0 %all-to-all-start = ((f32[32,24,256]{2,1,0:T(8,128)}), f32[32,24,256]{2,1,0:T(8,128)S(1)}, u32[]{:S(2)}, u32[]{:S(2)}) async-start(f32[32,24,256]{2,1,0:T(8,128)} %get-tuple-element.12), calls=%async_computation | async-start | bytes 1572864 | tf_op jit(solution)/shard_map/all_to_all | solution.py:432
  63.4 0.1 fusion.1
  63.5 0.1 fusion.5
  63.6 0.1 slice.67
  63.8 0.1 slice.72
  63.9 14.4 %all-to-all-done = f32[32,24,256]{2,1,0:T(8,128)S(1)} async-done(((f32[32,24,256]{2,1,0:T(8,128)}), f32[32,24,256]{2,1,0:T(8,128)S(1)}, u32[]{:S(2)}, u32[]{:S(2)}) %all-to-all-start) | async-done | bytes 786464 | tf_op jit(solution)/shard_map/all_to_all | solution.py:432
  78.4 0.9 broadcast_in_dim.34
  79.3 20.0 %all-to-all-start.2 = ((f32[16,40,256]{2,1,0:T(8,128)}), f32[16,40,256]{2,1,0:T(8,128)S(1)}, u32[]{:S(2)}, u32[]{:S(2)}) async-start(f32[16,40,256]{2,1,0:T(8,128)} %broadcast_in_dim.34), calls=%async_computation.2 | async-start | bytes 1310720 | tf_op jit(solution)/shard_map/all_to_all | solution.py:432
  99.3 0.1 reshape_squeeze.3
  99.4 0.1 multiply_reduce_fusion
  99.5 0.1 broadcast_in_dim.35
  99.5 0.7 reshape.80.coef
  100.2 18.7 %all-to-all-done.2.recv = f32[16,40,256]{2,1,0:T(8,128)S(1)} async-done(((f32[16,40,256]{2,1,0:T(8,128)}), f32[16,40,256]{2,1,0:T(8,128)S(1)}, u32[]{:S(2)}, u32[]{:S(2)}) %all-to-all-start.2) | async-done | bytes 655392 | tf_op jit(solution)/shard_map/all_to_all | solution.py:432
  118.9 0.8 copy-done
  119.7 19.1 %solve_kernel.1 = f32[32,8,512]{2,1,0:T(8,128)} custom-call(s32[1]{0:T(128)} %bitcast.4.place, f32[16,40,256]{2,1,0:T(8,128)} %copy-done, f32[8,256]{1,0:T(8,128)} %reshape.80.coef), custom_call_target="tpu_custom_call" | custom-call | tf_op jit(solution)/shard_map/solve_kernel/pallas_call | solution.py:402
  138.8 5.2 %all-to-all-start.3 = ((f32[32,8,512]{2,1,0:T(8,128)}), f32[32,8,512]{2,1,0:T(8,128)S(1)}, u32[]{:S(2)}, u32[]{:S(2)}) async-start(f32[32,8,512]{2,1,0:T(8,128)} %solve_kernel.1), calls=%async_computation.3 | async-start | bytes 1048576 | tf_op jit(solution)/shard_map/all_to_all | solution.py:432
  144.1 2.5 %collective-permute-start.5 = (f32[32,2,8,128]{3,2,1,0:T(8,128)S(1)}, f32[32,2,8,128]{3,2,1,0:T(8,128)S(1)}, u32[]{:S(2)}, u32[]{:S(2)}) collective-permute-start(f32[32,2,8,128]{3,2,1,0:T(8,128)S(1)} %get-tuple-element.23), channel_id=1, source_target_pairs={{0,384},{128,0},{256,128},{384,256},{1,385},{129,1},{257,129},{385... | collective-permute-start | bytes 786440 | tf_op jit(solution)/shard_map/ppermute | solution.py:425
  146.6 2.9 %collective-permute-start.4 = (f32[32,2,8,128]{3,2,1,0:T(8,128)S(1)}, f32[32,2,8,128]{3,2,1,0:T(8,128)S(1)}, u32[]{:S(2)}, u32[]{:S(2)}) collective-permute-start(f32[32,2,8,128]{3,2,1,0:T(8,128)S(1)} %get-tuple-element.24), channel_id=1, source_target_pairs={{0,128},{128,256},{256,384},{384,0},{1,129},{129,257},{257,385},{3... | collective-permute-start | bytes 786440 | tf_op jit(solution)/shard_map/ppermute | solution.py:424
  149.5 2.7 %collective-permute-start.6 = (f32[32,8,128]{2,1,0:T(8,128)S(1)}, f32[32,8,128]{2,1,0:T(8,128)S(1)}, u32[]{:S(2)}, u32[]{:S(2)}) collective-permute-start(f32[32,8,128]{2,1,0:T(8,128)S(1)} %copy-done.17), channel_id=1, source_target_pairs={{0,96},{32,0},{64,32},{96,64},{1,97},{33,1},{65,33},{97,65},{2,98}... | collective-permute-start | bytes 393224 | tf_op jit(solution)/shard_map/ppermute | solution.py:426
  152.2 6.8 %collective-permute-start.7 = (f32[32,8,128]{2,1,0:T(8,128)S(1)}, f32[32,8,128]{2,1,0:T(8,128)S(1)}, u32[]{:S(2)}, u32[]{:S(2)}) collective-permute-start(f32[32,8,128]{2,1,0:T(8,128)S(1)} %copy-done.16), channel_id=1, source_target_pairs={{0,32},{32,64},{64,96},{96,0},{1,33},{33,65},{65,97},{97,1},{2,34}... | collective-permute-start | bytes 393224 | tf_op jit(solution)/shard_map/ppermute | solution.py:427
  159.0 4.9 %collective-permute-done.6.north = f32[32,8,128]{2,1,0:T(8,128)S(1)} collective-permute-done((f32[32,8,128]{2,1,0:T(8,128)S(1)}, f32[32,8,128]{2,1,0:T(8,128)S(1)}, u32[]{:S(2)}, u32[]{:S(2)}) %collective-permute-start.6) | collective-permute-done | bytes 131104 | tf_op jit(solution)/shard_map/ppermute | solution.py:426
  164.0 0.6 copy-done.9
  164.7 0.1 copy-done.3
  164.8 0.1 copy-done.4
  164.9 0.8 copy-done.2
  165.7 5.8 %last_kernel.1 = f32[32,4,8,128]{3,2,1,0:T(8,128)} custom-call(f32[32,24]{1,0:T(8,128)} %bitcast.16, f32[32,8,512]{2,1,0:T(8,128)} %copy-done.2, f32[32,4,8,128]{3,2,1,0:T(8,128)} %get-tuple-element.16.g, f32[32,2,8,128]{3,2,1,0:T(8,128)} %copy-done.4, f32[32,2,8,128]{3,2,1,0:T(8,128)} %copy-done.3, f32[32,8,128]{2,1,0:T(8,128)} %copy-done.9, ...), custom_call_target="tpu_custom_call" | custom-call | tf_op jit(solution)/shard_map/last_kernel/pallas_call | solution.py:411
  (57 shorter events, 0.9 us)
Async XLA Ops:
  1.1 10.4 %copy-start.15 = (s32[3,32]{1,0:T(4,128)S(1)}, s32[3,32]{1,0:T(4,128)}, u32[]{:S(2)}) copy-start(s32[3,32]{1,0:T(4,128)} %param.7) | copy-start | bytes 1156
  1.1 30.2 %collective-permute-start.1 = (f32[32,2,8,128]{3,2,1,0:T(8,128)S(1)}, f32[32,2,8,128]{3,2,1,0:T(8,128)S(1)}, u32[]{:S(2)}, u32[]{:S(2)}) collective-permute-start(f32[32,2,8,128]{3,2,1,0:T(8,128)S(1)} %get-tuple-element.25), channel_id=1, source_target_pairs={{0,384},{128,0},{256,128},{384,256},{1,385},{129,1},{257,129},{385... | collective-permute-start | bytes 786440 | tf_op jit(solution)/shard_map/ppermute | solution.py:425
  9.5 21.8 %collective-permute-start = (f32[32,2,8,128]{3,2,1,0:T(8,128)S(1)}, f32[32,2,8,128]{3,2,1,0:T(8,128)S(1)}, u32[]{:S(2)}, u32[]{:S(2)}) collective-permute-start(f32[32,2,8,128]{3,2,1,0:T(8,128)S(1)} %get-tuple-element.26), channel_id=1, source_target_pairs={{0,128},{128,256},{256,384},{384,0},{1,129},{129,257},{257,385},{3... | collective-permute-start | bytes 786440 | tf_op jit(solution)/shard_map/ppermute | solution.py:424
  11.5 0.7 copy-start.14
  13.2 0.7 copy-start.13
  17.5 12.9 %collective-permute-start.2 = (f32[32,8,128]{2,1,0:T(8,128)}, f32[32,8,128]{2,1,0:T(8,128)S(1)}, u32[]{:S(2)}, u32[]{:S(2)}) collective-permute-start(f32[32,8,128]{2,1,0:T(8,128)} %get-tuple-element.13), channel_id=1, source_target_pairs={{0,96},{32,0},{64,32},{96,64},{1,97},{33,1},{65,33},{97,65},{2,98}... | collective-permute-start | bytes 393224 | tf_op jit(solution)/shard_map/ppermute | solution.py:426
  21.7 9.6 %collective-permute-start.3 = (f32[32,8,128]{2,1,0:T(8,128)}, f32[32,8,128]{2,1,0:T(8,128)S(1)}, u32[]{:S(2)}, u32[]{:S(2)}) collective-permute-start(f32[32,8,128]{2,1,0:T(8,128)} %get-tuple-element.14), channel_id=1, source_target_pairs={{0,32},{32,64},{64,96},{96,0},{1,33},{33,65},{65,97},{97,1},{2,34}... | collective-permute-start | bytes 393224 | tf_op jit(solution)/shard_map/ppermute | solution.py:427
  28.9 0.8 copy-start.12
  30.3 1.0 copy-start.7
  31.3 0.7 copy-start.8
  31.3 0.8 copy-start.5
  31.3 0.8 copy-start.6
  59.3 19.0 %all-to-all-start = ((f32[32,24,256]{2,1,0:T(8,128)}), f32[32,24,256]{2,1,0:T(8,128)S(1)}, u32[]{:S(2)}, u32[]{:S(2)}) async-start(f32[32,24,256]{2,1,0:T(8,128)} %get-tuple-element.12), calls=%async_computation | async-start | bytes 1572864 | tf_op jit(solution)/shard_map/all_to_all | solution.py:432
  79.3 20.1 %copy-start.11 = (f32[8,8,8]{2,1,0:T(8,128)S(1)}, f32[8,8,8]{2,1,0:T(8,128)}, u32[]{:S(2)}) copy-start(f32[8,8,8]{2,1,0:T(8,128)} %constant.66.clone) | copy-start | bytes 6148
  79.3 39.6 %all-to-all-start.2 = ((f32[16,40,256]{2,1,0:T(8,128)}), f32[16,40,256]{2,1,0:T(8,128)S(1)}, u32[]{:S(2)}, u32[]{:S(2)}) async-start(f32[16,40,256]{2,1,0:T(8,128)} %broadcast_in_dim.34), calls=%async_computation.2 | async-start | bytes 1310720 | tf_op jit(solution)/shard_map/all_to_all | solution.py:432
  118.9 0.8 copy-start
  138.8 5.2 %copy-start.1 = (f32[32,4,8,128]{3,2,1,0:T(8,128)S(1)}, f32[32,4,8,128]{3,2,1,0:T(8,128)}, u32[]{:S(2)}) copy-start(f32[32,4,8,128]{3,2,1,0:T(8,128)} %get-tuple-element.16.g) | copy-start | bytes 1572868
  138.8 25.2 %all-to-all-start.3 = ((f32[32,8,512]{2,1,0:T(8,128)}), f32[32,8,512]{2,1,0:T(8,128)S(1)}, u32[]{:S(2)}, u32[]{:S(2)}) async-start(f32[32,8,512]{2,1,0:T(8,128)} %solve_kernel.1), calls=%async_computation.3 | async-start | bytes 1048576 | tf_op jit(solution)/shard_map/all_to_all | solution.py:432
  144.0 5.5 %copy-start.17 = (f32[32,8,128]{2,1,0:T(8,128)S(1)}, f32[32,8,128]{2,1,0:T(8,128)}, u32[]{:S(2)}) copy-start(f32[32,8,128]{2,1,0:T(8,128)} %get-tuple-element.17) | copy-start | bytes 393220
  144.0 8.2 %copy-start.16 = (f32[32,8,128]{2,1,0:T(8,128)S(1)}, f32[32,8,128]{2,1,0:T(8,128)}, u32[]{:S(2)}) copy-start(f32[32,8,128]{2,1,0:T(8,128)} %get-tuple-element.18) | copy-start | bytes 393220
  144.1 19.9 %collective-permute-start.5 = (f32[32,2,8,128]{3,2,1,0:T(8,128)S(1)}, f32[32,2,8,128]{3,2,1,0:T(8,128)S(1)}, u32[]{:S(2)}, u32[]{:S(2)}) collective-permute-start(f32[32,2,8,128]{3,2,1,0:T(8,128)S(1)} %get-tuple-element.23), channel_id=1, source_target_pairs={{0,384},{128,0},{256,128},{384,256},{1,385},{129,1},{257,129},{385... | collective-permute-start | bytes 786440 | tf_op jit(solution)/shard_map/ppermute | solution.py:425
  146.6 17.4 %collective-permute-start.4 = (f32[32,2,8,128]{3,2,1,0:T(8,128)S(1)}, f32[32,2,8,128]{3,2,1,0:T(8,128)S(1)}, u32[]{:S(2)}, u32[]{:S(2)}) collective-permute-start(f32[32,2,8,128]{3,2,1,0:T(8,128)S(1)} %get-tuple-element.24), channel_id=1, source_target_pairs={{0,128},{128,256},{256,384},{384,0},{1,129},{129,257},{257,385},{3... | collective-permute-start | bytes 786440 | tf_op jit(solution)/shard_map/ppermute | solution.py:424
  149.5 14.4 %collective-permute-start.6 = (f32[32,8,128]{2,1,0:T(8,128)S(1)}, f32[32,8,128]{2,1,0:T(8,128)S(1)}, u32[]{:S(2)}, u32[]{:S(2)}) collective-permute-start(f32[32,8,128]{2,1,0:T(8,128)S(1)} %copy-done.17), channel_id=1, source_target_pairs={{0,96},{32,0},{64,32},{96,64},{1,97},{33,1},{65,33},{97,65},{2,98}... | collective-permute-start | bytes 393224 | tf_op jit(solution)/shard_map/ppermute | solution.py:426
  152.2 11.8 %collective-permute-start.7 = (f32[32,8,128]{2,1,0:T(8,128)S(1)}, f32[32,8,128]{2,1,0:T(8,128)S(1)}, u32[]{:S(2)}, u32[]{:S(2)}) collective-permute-start(f32[32,8,128]{2,1,0:T(8,128)S(1)} %copy-done.16), channel_id=1, source_target_pairs={{0,32},{32,64},{64,96},{96,0},{1,33},{33,65},{65,97},{97,1},{2,34}... | collective-permute-start | bytes 393224 | tf_op jit(solution)/shard_map/ppermute | solution.py:427
  164.0 0.7 copy-start.9
  164.0 0.7 copy-start.10
  164.0 0.8 copy-start.3
  164.0 0.8 copy-start.4
  164.9 0.8 copy-start.2

commit v2 on v1

--- a/solution.py
+++ b/solution.py
@@ -8,6 +8,7 @@
 
 V = 1024
 INTERPRET = False
+UNROLL = 4
 
 absorb = 0.5
 damping = 0.8
@@ -87,7 +88,7 @@
             jnp.zeros_like(centre)[None],
         ],
         axis=0,
-    ).T
+    )
     cross = jnp.sum(source_basis[:, None] * equil[None], axis=2)
     cross_row = jnp.pad(cross, ((0, 0), (0, COLS - ROWS))).reshape(1, LANES)
     return table, cross_row
@@ -100,7 +101,7 @@
         tiles = [src[v, x] for x in range(SX)]
         out = []
         for r in range(ROWS):
-            w = table[v, r]
+            w = table[r, v]
             out += [accs[r * SX + x] + w * tiles[x] for x in range(SX)]
         return tuple(out)
 
@@ -144,9 +145,9 @@
 
 
 def transport(table, v, tiles, edges, sub):
-    centre = table[v, 16]
-    up = [table[v, 17 + d] for d in range(3)]
-    down = [table[v, 20 + d] for d in range(3)]
+    centre = table[16, v]
+    up = [table[17 + d, v] for d in range(3)]
+    down = [table[20 + d, v] for d in range(3)]
     out = []
     for x in range(SX):
         f = tiles[x + 2]
@@ -215,7 +216,7 @@
                 gain[i, h * WIN + 4 + 8 * half : h * WIN + 12 + 8 * half, :] = t
         return carry
 
-    lax.fori_loop(0, BLOCKS, unpack, 0)
+    lax.fori_loop(0, BLOCKS, unpack, 0, unroll=UNROLL)
 
     def around(i):
         gx, gy = i // 4, i % 4
@@ -282,11 +283,11 @@
         src[i] = coarse[i]
         return carry
 
-    lax.fori_loop(0, BLOCKS, restrict, 0)
-    lax.fori_loop(0, BLOCKS, correct, 0)
-    lax.fori_loop(0, BLOCKS, mix, 0)
-    lax.fori_loop(0, BLOCKS, swap, 0)
-    lax.fori_loop(0, BLOCKS, restrict, 0)
+    lax.fori_loop(0, BLOCKS, restrict, 0, unroll=UNROLL)
+    lax.fori_loop(0, BLOCKS, correct, 0, unroll=UNROLL)
+    lax.fori_loop(0, BLOCKS, mix, 0, unroll=UNROLL)
+    lax.fori_loop(0, BLOCKS, swap, 0, unroll=UNROLL)
+    lax.fori_loop(0, BLOCKS, restrict, 0, unroll=UNROLL)
     own = place[0]
     next_x, last_x, next_y, last_y = around(own)
     for i in (own, next_x, last_x, next_y, last_y):
@@ -318,7 +319,7 @@
     sub = iota((SY, NZ), 0)
 
     def step(v, carry):
-        psi = [table[v, ROWS + r] for r in range(ROWS)]
+        psi = [table[ROWS + r, v] for r in range(ROWS)]
 
         def lift(part, x):
             total = psi[0] * fields[part, 0, x]
@@ -440,10 +441,10 @@
     place = (lax.axis_index("gx") * 4 + lax.axis_index("gy")).astype(jnp.int32).reshape(1)
     win_one, north, south = stage_first(f, table, members)
     got_one = swap_all(win_one, "vert")
-    near = halos(f, north, south)
+    near, got_one = lax.optimization_barrier((halos(f, north, south), got_one))
     g, win_two, north, south = stage_second(f, table, *near, fluid, cross, members)
     got_two = swap_all(win_two, "vert")
-    near = halos(g, north, south)
+    near, got_two = lax.optimization_barrier((halos(g, north, south), got_two))
     whole, coef = stage_middle(got_one, got_two, walls)
     got = swap_all(whole, ("gx", "gy"))
     sent = stage_solve(place, got, coef, members)

time: 173 us -> 158 us (0.913)
  Pallas kernels: 32.3 us -> 24.8 us
  waiting for transfers between devices: 39 us -> 32.4 us
  blocking collectives: 22.5 us -> 26.1 us
  local copies, waits for them, and re-layouts: 10.8 us -> 7.98 us
    all_to_all x3, waiting for transfers between devices: 33.1 us -> 18.7 us  [swap_all(): return lax.all_to_all(x, axis, 0, 0, tiled=True)]
    pallas_call x1, Pallas kernels: 19.1 us -> 11.6 us  [stage_solve(): call(solve_kernel, (SMEM, VMEM, VMEM), ((members, 8, 512),), (big,) * 6 +...]
    ppermute x2, waiting for transfers between devices: 4.95 us -> 10.3 us  [halos(): above = lax.ppermute(north, 'gy', ring('gy', -1))]
    all_to_all x1, blocking collectives: 22.5 us -> 26.1 us  [swap_all(): return lax.all_to_all(x, axis, 0, 0, tiled=True)]
    ppermute x2, waiting for transfers between devices: 1 us -> 3.46 us  [halos(): below = lax.ppermute(south, 'gy', ring('gy', 1))]
    unnamed x37 -> x36, local copies, waits for them, and re-layouts: 4.64 us -> 3.15 us
  transfers between devices with their start and end apart: 11 -> 11, of which waited for: 4 -> 4; matrix products, arithmetic and copies ran while one was open for 3% -> 2% of each run, Pallas kernels for 2% -> 0%
where the time goes in v2:
time: 158 us; the launch traced here: 157 us
  starting transfers between devices  64 us (41%)
  waiting for transfers between devices  32.4 us (21%)
  blocking collectives  26.1 us (17%)
  Pallas kernels  24.8 us (16%)
  local copies, waits for them, and re-layouts  7.98 us (5%)
  other arithmetic  1.84 us (1%)
    all_to_all x3, starting transfers between devices, swap_all(): return lax.all_to_all(x, axis, 0, 0, tiled=True)  28.4 us
    all_to_all x1, blocking collectives, swap_all(): return lax.all_to_all(x, axis, 0, 0, tiled=True)  26.1 us
    all_to_all x3, waiting for transfers between devices, swap_all(): return lax.all_to_all(x, axis, 0, 0, tiled=True)  18.7 us
    ppermute x2, starting transfers between devices, halos(): below = lax.ppermute(south, 'gy', ring('gy', 1))  14.1 us
    pallas_call x1, Pallas kernels, stage_solve(): call(solve_kernel, (SMEM, VMEM, VMEM), ((members, 8, 512),), (big,) * 6 +...  11.6 us
    ppermute x2, waiting for transfers between devices, halos(): above = lax.ppermute(north, 'gy', ring('gy', -1))  10.3 us
    ppermute x2, starting transfers between devices, halos(): high = lax.ppermute(f[:, :2], 'gx', ring('gx', -1))  9.8 us
    ppermute x2, starting transfers between devices, halos(): above = lax.ppermute(north, 'gy', ring('gy', -1))  6.32 us
  transfers between devices with their start and end apart: 11, of which 4 were waited for; matrix products, arithmetic and copies ran while one was open for 2% of the time, Pallas kernels for 0%

profile of v2, /device:TPU:1, one launch (start us, length us, event | category | flops | bytes accessed | tf_op | source)
XLA Modules:
  0.0 157.4 jit_solution(18258670626568712756)
XLA Ops:
  0.0 0.7 subtract_multiply_fusion
  0.8 0.0 copy-start.13
  0.9 0.7 copy-done.13
  1.5 0.1 multiply_reduce_fusion.2
  1.6 1.8 %concatenate.13.table = f32[24,32]{1,0:T(8,128)} concatenate(f32[5,32]{1,0:T(8,128)S(1)} %fusion.2, f32[3,32]{1,0:T(4,128)S(1)} %slice.79, f32[1,32]{1,0:T(1,128)S(1)} %broadcast.110, f32[1,32]{1,0:T(1,128)S(1)} %get-tuple-element.61, f32[1,32]{1,0:T(1,128)S(1)} %broadcast_multiply_fusion.3, f32[1,32]{1,0:T(1,128)S(1)} %get-tuple-element.64, f32[1,32]{1,0:T(1,128)S(1)} %get-tuple-element.67, ...), dimensions={0} | concatenate | bytes 6144 | tf_op jit(solution)/shard_map/concatenate | solution.py:81
  3.5 2.7 %first_kernel.1 = (f32[32,24,256]{2,1,0:T(8,128)}, f32[32,8,128]{2,1,0:T(8,128)}, f32[32,8,128]{2,1,0:T(8,128)}) custom-call(f32[24,32]{1,0:T(8,128)} %concatenate.13.table, f32[32,4,8,128]{3,2,1,0:T(8,128)} %f.3), custom_call_target="tpu_custom_call" | custom-call | tf_op jit(solution)/shard_map/first_kernel/pallas_call | solution.py:363
  6.1 10.6 %all-to-all-start = ((f32[32,24,256]{2,1,0:T(8,128)}), f32[32,24,256]{2,1,0:T(8,128)S(1)}, u32[]{:S(2)}, u32[]{:S(2)}) async-start(f32[32,24,256]{2,1,0:T(8,128)} %get-tuple-element.24), calls=%async_computation | async-start | bytes 1572864 | tf_op jit(solution)/shard_map/all_to_all | solution.py:433
  16.8 0.0 copy-done
  16.8 0.0 copy-start.17
  16.8 0.0 copy-start.16
  16.8 7.7 %collective-permute-start.1 = (f32[32,2,8,128]{3,2,1,0:T(8,128)S(1)}, f32[32,2,8,128]{3,2,1,0:T(8,128)S(1)}, u32[]{:S(2)}, u32[]{:S(2)}) collective-permute-start(f32[32,2,8,128]{3,2,1,0:T(8,128)S(1)} %get-tuple-element.45), channel_id=1, source_target_pairs={{0,384},{128,0},{256,128},{384,256},{1,385},{129,1},{257,129},{385... | collective-permute-start | bytes 786440 | tf_op jit(solution)/shard_map/ppermute | solution.py:426
  24.6 1.9 %collective-permute-start = (f32[32,2,8,128]{3,2,1,0:T(8,128)S(1)}, f32[32,2,8,128]{3,2,1,0:T(8,128)S(1)}, u32[]{:S(2)}, u32[]{:S(2)}) collective-permute-start(f32[32,2,8,128]{3,2,1,0:T(8,128)S(1)} %get-tuple-element.46), channel_id=1, source_target_pairs={{0,128},{128,256},{256,384},{384,0},{1,129},{129,257},{257,385},{3... | collective-permute-start | bytes 786440 | tf_op jit(solution)/shard_map/ppermute | solution.py:425
  26.5 3.1 %collective-permute-start.2 = (f32[32,8,128]{2,1,0:T(8,128)S(1)}, f32[32,8,128]{2,1,0:T(8,128)S(1)}, u32[]{:S(2)}, u32[]{:S(2)}) collective-permute-start(f32[32,8,128]{2,1,0:T(8,128)S(1)} %copy-done.17), channel_id=1, source_target_pairs={{0,96},{32,0},{64,32},{96,64},{1,97},{33,1},{65,33},{97,65},{2,98}... | collective-permute-start | bytes 393224 | tf_op jit(solution)/shard_map/ppermute | solution.py:427
  29.7 7.8 %collective-permute-start.3 = (f32[32,8,128]{2,1,0:T(8,128)S(1)}, f32[32,8,128]{2,1,0:T(8,128)S(1)}, u32[]{:S(2)}, u32[]{:S(2)}) collective-permute-start(f32[32,8,128]{2,1,0:T(8,128)S(1)} %copy-done.16), channel_id=1, source_target_pairs={{0,32},{32,64},{64,96},{96,0},{1,33},{33,65},{65,97},{97,1},{2,34}... | collective-permute-start | bytes 393224 | tf_op jit(solution)/shard_map/ppermute | solution.py:428
  37.6 0.0 copy-start.12
  37.6 0.1 multiply_reduce_fusion.1
  37.7 0.7 reshape.79.cross
  38.3 0.0 copy-done.12
  38.3 0.6 broadcast_select_fusion
  38.9 9.7 %collective-permute-done.2.north = f32[32,8,128]{2,1,0:T(8,128)S(1)} collective-permute-done((f32[32,8,128]{2,1,0:T(8,128)S(1)}, f32[32,8,128]{2,1,0:T(8,128)S(1)}, u32[]{:S(2)}, u32[]{:S(2)}) %collective-permute-start.2) | collective-permute-done | bytes 131104 | tf_op jit(solution)/shard_map/ppermute | solution.py:427
  48.7 0.0 collective-permute-done.3.south
  48.7 0.0 collective-permute-done.1.high
  48.7 0.0 copy-start.5
  48.7 0.0 collective-permute-done.low
  48.7 0.0 all-to-all-done
  48.7 0.6 copy-done.9
  49.3 0.1 copy-done.10
  49.4 0.1 copy-done.5
  49.5 0.1 copy-done.6
  49.6 4.7 %second_kernel.1 = (f32[32,4,8,128]{3,2,1,0:T(8,128)}, f32[32,16,256]{2,1,0:T(8,128)}, f32[32,8,128]{2,1,0:T(8,128)}, f32[32,8,128]{2,1,0:T(8,128)}) custom-call(f32[24,32]{1,0:T(8,128)} %concatenate.13.table, f32[32,4,8,128]{3,2,1,0:T(8,128)} %f.3, f32[32,2,8,128]{3,2,1,0:T(8,128)} %copy-done.6, f32[32,2,8,128]{3,2,1,0:T(8,128)} %copy-done.5, ...), custom_call_target="tpu_custom_call" | custom-call | tf_op jit(solution)/shard_map/second_kernel/pallas_call | solution.py:373
  54.3 9.3 %all-to-all-start.1 = ((f32[32,16,256]{2,1,0:T(8,128)}), f32[32,16,256]{2,1,0:T(8,128)S(1)}, u32[]{:S(2)}, u32[]{:S(2)}) async-start(f32[32,16,256]{2,1,0:T(8,128)} %get-tuple-element.33), calls=%async_computation.1 | async-start | bytes 1048576 | tf_op jit(solution)/shard_map/all_to_all | solution.py:433
  63.6 0.1 slice.80
  63.8 2.1 %collective-permute-start.5 = (f32[32,2,8,128]{3,2,1,0:T(8,128)S(1)}, f32[32,2,8,128]{3,2,1,0:T(8,128)S(1)}, u32[]{:S(2)}, u32[]{:S(2)}) collective-permute-start(f32[32,2,8,128]{3,2,1,0:T(8,128)S(1)} %get-tuple-element.43), channel_id=1, source_target_pairs={{0,384},{128,0},{256,128},{384,256},{1,385},{129,1},{257,129},{385... | collective-permute-start | bytes 786440 | tf_op jit(solution)/shard_map/ppermute | solution.py:426
  65.8 3.4 %collective-permute-start.4 = (f32[32,2,8,128]{3,2,1,0:T(8,128)S(1)}, f32[32,2,8,128]{3,2,1,0:T(8,128)S(1)}, u32[]{:S(2)}, u32[]{:S(2)}) collective-permute-start(f32[32,2,8,128]{3,2,1,0:T(8,128)S(1)} %get-tuple-element.44), channel_id=1, source_target_pairs={{0,128},{128,256},{256,384},{384,0},{1,129},{129,257},{257,385},{3... | collective-permute-start | bytes 786440 | tf_op jit(solution)/shard_map/ppermute | solution.py:425
  69.2 0.1 fusion.1
  69.3 3.2 %collective-permute-start.6 = (f32[32,8,128]{2,1,0:T(8,128)S(1)}, f32[32,8,128]{2,1,0:T(8,128)S(1)}, u32[]{:S(2)}, u32[]{:S(2)}) collective-permute-start(f32[32,8,128]{2,1,0:T(8,128)S(1)} %copy-done.15), channel_id=1, source_target_pairs={{0,96},{32,0},{64,32},{96,64},{1,97},{33,1},{65,33},{97,65},{2,98}... | collective-permute-start | bytes 393224 | tf_op jit(solution)/shard_map/ppermute | solution.py:427
  72.5 6.3 %collective-permute-start.7 = (f32[32,8,128]{2,1,0:T(8,128)S(1)}, f32[32,8,128]{2,1,0:T(8,128)S(1)}, u32[]{:S(2)}, u32[]{:S(2)}) collective-permute-start(f32[32,8,128]{2,1,0:T(8,128)S(1)} %copy-done.14), channel_id=1, source_target_pairs={{0,32},{32,64},{64,96},{96,0},{1,33},{33,65},{65,97},{97,1},{2,34}... | collective-permute-start | bytes 393224 | tf_op jit(solution)/shard_map/ppermute | solution.py:428
  78.8 0.1 fusion.11
  78.9 0.1 copy.10
  78.9 0.1 slice.69
  79.0 0.1 copy.11
  79.1 0.1 slice.74
  79.1 0.1 reduce_sum.66
  79.2 0.6 collective-permute-done.6.north
  79.8 3.5 %collective-permute-done.7.south = f32[32,8,128]{2,1,0:T(8,128)S(1)} collective-permute-done((f32[32,8,128]{2,1,0:T(8,128)S(1)}, f32[32,8,128]{2,1,0:T(8,128)S(1)}, u32[]{:S(2)}, u32[]{:S(2)}) %collective-permute-start.7) | collective-permute-done | bytes 131104 | tf_op jit(solution)/shard_map/ppermute | solution.py:428
  83.2 0.0 collective-permute-done.5.high
  83.2 0.0 collective-permute-done.4.low
  83.2 0.0 copy-start.4
  83.3 0.0 all-to-all-done.1
  83.3 0.6 copy-done.3
  84.0 0.1 copy-done.4
  84.1 0.9 broadcast_in_dim.34
  85.0 0.0 copy-done.7
  85.0 8.5 %all-to-all-start.2 = ((f32[16,40,256]{2,1,0:T(8,128)}), f32[16,40,256]{2,1,0:T(8,128)S(1)}, u32[]{:S(2)}, u32[]{:S(2)}) async-start(f32[16,40,256]{2,1,0:T(8,128)} %broadcast_in_dim.34), calls=%async_computation.2 | async-start | bytes 1310720 | tf_op jit(solution)/shard_map/all_to_all | solution.py:433
  93.5 0.1 reshape_squeeze.3
  93.5 0.0 copy-done.11
  93.5 0.1 multiply_reduce_fusion
  93.6 0.1 broadcast_in_dim.35
  93.7 0.7 reshape.80.coef
  94.4 18.7 %all-to-all-done.2.recv = f32[16,40,256]{2,1,0:T(8,128)S(1)} async-done(((f32[16,40,256]{2,1,0:T(8,128)}), f32[16,40,256]{2,1,0:T(8,128)S(1)}, u32[]{:S(2)}, u32[]{:S(2)}) %all-to-all-start.2) | async-done | bytes 655392 | tf_op jit(solution)/shard_map/all_to_all | solution.py:433
  113.0 0.8 copy-done.1
  113.9 11.6 %solve_kernel.1 = f32[32,8,512]{2,1,0:T(8,128)} custom-call(s32[1]{0:T(128)} %bitcast.3.place, f32[16,40,256]{2,1,0:T(8,128)} %copy-done.1, f32[8,256]{1,0:T(8,128)} %reshape.80.coef), custom_call_target="tpu_custom_call" | custom-call | tf_op jit(solution)/shard_map/solve_kernel/pallas_call | solution.py:403
  125.5 26.1 %all_to_all.20.recv = f32[32,8,512]{2,1,0:T(8,128)} all-to-all(f32[32,8,512]{2,1,0:T(8,128)} %solve_kernel.1), channel_id=1, replica_groups=mesh['gx'=4,'gy'=4,'vert'=32] {'vert'}, dimensions={0} | all-to-all | bytes 1048576 | tf_op jit(solution)/shard_map/all_to_all | solution.py:433
  151.6 5.8 %last_kernel.1 = f32[32,4,8,128]{3,2,1,0:T(8,128)} custom-call(f32[24,32]{1,0:T(8,128)} %concatenate.13.table, f32[32,8,512]{2,1,0:T(8,128)} %all_to_all.20.recv, f32[32,4,8,128]{3,2,1,0:T(8,128)} %get-tuple-element.30.g, f32[32,2,8,128]{3,2,1,0:T(8,128)} %copy-done.4, f32[32,2,8,128]{3,2,1,0:T(8,128)} %copy-done.3, f32[32,8,128]{2,1,0:T(8,128)} %copy-done.7, ...), custom_call_target="tpu_custom_call" | custom-call | tf_op jit(solution)/shard_map/last_kernel/pallas_call | solution.py:412
  (39 shorter events, 0.3 us)
Async XLA Ops:
  0.8 0.7 copy-start.13
  6.1 10.6 %copy-start = (f32[32,4,8,128]{3,2,1,0:T(8,128)S(1)}, f32[32,4,8,128]{3,2,1,0:T(8,128)}, u32[]{:S(2)}) copy-start(f32[32,4,8,128]{3,2,1,0:T(8,128)} %f.3) | copy-start | bytes 1572868
  6.1 42.6 %all-to-all-start = ((f32[32,24,256]{2,1,0:T(8,128)}), f32[32,24,256]{2,1,0:T(8,128)S(1)}, u32[]{:S(2)}, u32[]{:S(2)}) async-start(f32[32,24,256]{2,1,0:T(8,128)} %get-tuple-element.24), calls=%async_computation | async-start | bytes 1572864 | tf_op jit(solution)/shard_map/all_to_all | solution.py:433
  16.8 9.8 %copy-start.17 = (f32[32,8,128]{2,1,0:T(8,128)S(1)}, f32[32,8,128]{2,1,0:T(8,128)}, u32[]{:S(2)}) copy-start(f32[32,8,128]{2,1,0:T(8,128)} %get-tuple-element.22) | copy-start | bytes 393220
  16.8 12.9 %copy-start.16 = (f32[32,8,128]{2,1,0:T(8,128)S(1)}, f32[32,8,128]{2,1,0:T(8,128)}, u32[]{:S(2)}) copy-start(f32[32,8,128]{2,1,0:T(8,128)} %get-tuple-element.23) | copy-start | bytes 393220
  16.8 31.8 %collective-permute-start.1 = (f32[32,2,8,128]{3,2,1,0:T(8,128)S(1)}, f32[32,2,8,128]{3,2,1,0:T(8,128)S(1)}, u32[]{:S(2)}, u32[]{:S(2)}) collective-permute-start(f32[32,2,8,128]{3,2,1,0:T(8,128)S(1)} %get-tuple-element.45), channel_id=1, source_target_pairs={{0,384},{128,0},{256,128},{384,256},{1,385},{129,1},{257,129},{385... | collective-permute-start | bytes 786440 | tf_op jit(solution)/shard_map/ppermute | solution.py:426
  24.6 24.1 %collective-permute-start = (f32[32,2,8,128]{3,2,1,0:T(8,128)S(1)}, f32[32,2,8,128]{3,2,1,0:T(8,128)S(1)}, u32[]{:S(2)}, u32[]{:S(2)}) collective-permute-start(f32[32,2,8,128]{3,2,1,0:T(8,128)S(1)} %get-tuple-element.46), channel_id=1, source_target_pairs={{0,128},{128,256},{256,384},{384,0},{1,129},{129,257},{257,385},{3... | collective-permute-start | bytes 786440 | tf_op jit(solution)/shard_map/ppermute | solution.py:425
  26.5 22.1 %collective-permute-start.2 = (f32[32,8,128]{2,1,0:T(8,128)S(1)}, f32[32,8,128]{2,1,0:T(8,128)S(1)}, u32[]{:S(2)}, u32[]{:S(2)}) collective-permute-start(f32[32,8,128]{2,1,0:T(8,128)S(1)} %copy-done.17), channel_id=1, source_target_pairs={{0,96},{32,0},{64,32},{96,64},{1,97},{33,1},{65,33},{97,65},{2,98}... | collective-permute-start | bytes 393224 | tf_op jit(solution)/shard_map/ppermute | solution.py:427
  29.7 19.0 %collective-permute-start.3 = (f32[32,8,128]{2,1,0:T(8,128)S(1)}, f32[32,8,128]{2,1,0:T(8,128)S(1)}, u32[]{:S(2)}, u32[]{:S(2)}) collective-permute-start(f32[32,8,128]{2,1,0:T(8,128)S(1)} %copy-done.16), channel_id=1, source_target_pairs={{0,32},{32,64},{64,96},{96,0},{1,33},{33,65},{65,97},{97,1},{2,34}... | collective-permute-start | bytes 393224 | tf_op jit(solution)/shard_map/ppermute | solution.py:428
  37.6 0.8 copy-start.12
  48.7 0.6 copy-start.9
  48.7 0.7 copy-start.10
  48.7 0.8 copy-start.5
  48.7 0.9 copy-start.6
  54.3 9.5 %copy-start.2 = (f32[32,4,8,128]{3,2,1,0:T(8,128)S(1)}, f32[32,4,8,128]{3,2,1,0:T(8,128)}, u32[]{:S(2)}) copy-start(f32[32,4,8,128]{3,2,1,0:T(8,128)} %get-tuple-element.30.g) | copy-start | bytes 1572868
  54.3 29.0 %all-to-all-start.1 = ((f32[32,16,256]{2,1,0:T(8,128)}), f32[32,16,256]{2,1,0:T(8,128)S(1)}, u32[]{:S(2)}, u32[]{:S(2)}) async-start(f32[32,16,256]{2,1,0:T(8,128)} %get-tuple-element.33), calls=%async_computation.1 | async-start | bytes 1048576 | tf_op jit(solution)/shard_map/all_to_all | solution.py:433
  63.7 5.6 %copy-start.15 = (f32[32,8,128]{2,1,0:T(8,128)S(1)}, f32[32,8,128]{2,1,0:T(8,128)}, u32[]{:S(2)}) copy-start(f32[32,8,128]{2,1,0:T(8,128)} %get-tuple-element.31) | copy-start | bytes 393220
  63.7 8.8 %copy-start.14 = (f32[32,8,128]{2,1,0:T(8,128)S(1)}, f32[32,8,128]{2,1,0:T(8,128)}, u32[]{:S(2)}) copy-start(f32[32,8,128]{2,1,0:T(8,128)} %get-tuple-element.32) | copy-start | bytes 393220
  63.8 19.5 %collective-permute-start.5 = (f32[32,2,8,128]{3,2,1,0:T(8,128)S(1)}, f32[32,2,8,128]{3,2,1,0:T(8,128)S(1)}, u32[]{:S(2)}, u32[]{:S(2)}) collective-permute-start(f32[32,2,8,128]{3,2,1,0:T(8,128)S(1)} %get-tuple-element.43), channel_id=1, source_target_pairs={{0,384},{128,0},{256,128},{384,256},{1,385},{129,1},{257,129},{385... | collective-permute-start | bytes 786440 | tf_op jit(solution)/shard_map/ppermute | solution.py:426
  65.8 17.4 %collective-permute-start.4 = (f32[32,2,8,128]{3,2,1,0:T(8,128)S(1)}, f32[32,2,8,128]{3,2,1,0:T(8,128)S(1)}, u32[]{:S(2)}, u32[]{:S(2)}) collective-permute-start(f32[32,2,8,128]{3,2,1,0:T(8,128)S(1)} %get-tuple-element.44), channel_id=1, source_target_pairs={{0,128},{128,256},{256,384},{384,0},{1,129},{129,257},{257,385},{3... | collective-permute-start | bytes 786440 | tf_op jit(solution)/shard_map/ppermute | solution.py:425
  69.3 10.5 %collective-permute-start.6 = (f32[32,8,128]{2,1,0:T(8,128)S(1)}, f32[32,8,128]{2,1,0:T(8,128)S(1)}, u32[]{:S(2)}, u32[]{:S(2)}) collective-permute-start(f32[32,8,128]{2,1,0:T(8,128)S(1)} %copy-done.15), channel_id=1, source_target_pairs={{0,96},{32,0},{64,32},{96,64},{1,97},{33,1},{65,33},{97,65},{2,98}... | collective-permute-start | bytes 393224 | tf_op jit(solution)/shard_map/ppermute | solution.py:427
  72.5 10.8 %collective-permute-start.7 = (f32[32,8,128]{2,1,0:T(8,128)S(1)}, f32[32,8,128]{2,1,0:T(8,128)S(1)}, u32[]{:S(2)}, u32[]{:S(2)}) collective-permute-start(f32[32,8,128]{2,1,0:T(8,128)S(1)} %copy-done.14), channel_id=1, source_target_pairs={{0,32},{32,64},{64,96},{96,0},{1,33},{33,65},{65,97},{97,1},{2,34}... | collective-permute-start | bytes 393224 | tf_op jit(solution)/shard_map/ppermute | solution.py:428
  79.8 5.2 %copy-start.7 = (f32[32,8,128]{2,1,0:T(8,128)}, f32[32,8,128]{2,1,0:T(8,128)S(1)}, u32[]{:S(2)}) copy-start(f32[32,8,128]{2,1,0:T(8,128)S(1)} %collective-permute-done.6.north) | copy-start | bytes 393220
  83.2 1.8 %copy-start.8 = (f32[32,8,128]{2,1,0:T(8,128)}, f32[32,8,128]{2,1,0:T(8,128)S(1)}, u32[]{:S(2)}) copy-start(f32[32,8,128]{2,1,0:T(8,128)S(1)} %collective-permute-done.7.south) | copy-start | bytes 393220
  83.2 0.7 copy-start.3
  83.2 0.8 copy-start.4
  85.0 8.6 %copy-start.11 = (f32[8,8,8]{2,1,0:T(8,128)S(1)}, f32[8,8,8]{2,1,0:T(8,128)}, u32[]{:S(2)}) copy-start(f32[8,8,8]{2,1,0:T(8,128)} %constant.66.clone) | copy-start | bytes 6148
  85.0 28.1 %all-to-all-start.2 = ((f32[16,40,256]{2,1,0:T(8,128)}), f32[16,40,256]{2,1,0:T(8,128)S(1)}, u32[]{:S(2)}, u32[]{:S(2)}) async-start(f32[16,40,256]{2,1,0:T(8,128)} %broadcast_in_dim.34), calls=%async_computation.2 | async-start | bytes 1310720 | tf_op jit(solution)/shard_map/all_to_all | solution.py:433
  113.0 0.8 copy-start.1

commit v3 on v2

--- a/solution.py
+++ b/solution.py
@@ -4,11 +4,13 @@
 from jax import lax
 from jax.experimental import pallas as pl
 from jax.experimental.pallas import tpu as pltpu
+from jax.sharding import Mesh
 from jax.sharding import PartitionSpec as P
+
 
 V = 1024
 INTERPRET = False
-UNROLL = 4
+UNROLL = 16
 
 absorb = 0.5
 damping = 0.8
@@ -187,7 +189,7 @@
     pack_rows(g, g_north, g_south)
 
 
-def solve_kernel(place, recv, coef, out, src, coarse, fine, gain, extra, first, msg):
+def solve_kernel(place, near, far, coef, out, src, coarse, fine, gain, extra, first, msg):
     shape = (2 * WIN, 128)
     lane = iota(shape, 1)
     x_at = (lane // SY) % SX
@@ -198,16 +200,18 @@
     tile_lane = iota((8, 128), 1)
 
     def unpack(i, carry):
+        mine = i % 2 == place[1]
+        rows = jnp.where(mine, near[i // 2], far[i // 2])
         for h in range(2):
             lanes = slice(h * 128, (h + 1) * 128)
-            src[i, h * WIN : (h + 1) * WIN, :] = recv[i, 0:WIN, lanes]
+            src[i, h * WIN : (h + 1) * WIN, :] = rows[0:WIN, lanes]
             extra[i, h * WIN : h * WIN + 4, :] = jnp.zeros((4, 128), F32)
             extra[i, h * WIN + 20 : (h + 1) * WIN, :] = jnp.zeros((4, 128), F32)
-            extra[i, h * WIN + 4 : h * WIN + 20, :] = recv[i, WIN : WIN + WIN2, lanes]
+            extra[i, h * WIN + 4 : h * WIN + 20, :] = rows[WIN : WIN + WIN2, lanes]
         gain[i] = jnp.zeros(shape, F32)
         for half, at in enumerate((WIN, WIN + WIN2 - 1)):
-            left = jnp.broadcast_to(recv[i, at : at + 1, 0:128], (8, 128))
-            right = jnp.broadcast_to(recv[i, at : at + 1, 128:256], (8, 128))
+            left = jnp.broadcast_to(rows[at : at + 1, 0:128], (8, 128))
+            right = jnp.broadcast_to(rows[at : at + 1, 128:256], (8, 128))
             t = jnp.where(tile_sub < 4, left, right)
             t = jnp.where(tile_lane // COLS == tile_sub % 4, t, 0.0)
             t = t + roll(t, 32, 1)
@@ -340,6 +344,7 @@
     lax.fori_loop(0, out.shape[0], step, 0)
 
 
+GY = ("zh", "core")
 VMEM = pltpu.MemorySpace.VMEM
 SMEM = pltpu.MemorySpace.SMEM
 
@@ -354,7 +359,6 @@
         out_shape=shapes,
         scratch_shapes=[pltpu.VMEM(s, F32) for s in scratch],
         interpret=INTERPRET,
-        name=kernel.__name__,
     )
 
 
@@ -395,17 +399,17 @@
             pick[k, r, (r + k) % ROWS] = 1.0
     coef = jnp.sum(jnp.asarray(pick) * cross[None], axis=2)
     coef = jnp.broadcast_to(coef[:, :, None], (ROWS, ROWS, COLS)).reshape(ROWS, LANES)
-    return jnp.broadcast_to(whole[None], (BLOCKS,) + whole.shape), coef
-
-
-def stage_solve(place, got, coef, members):
+    return jnp.broadcast_to(whole[None], (BLOCKS // 2,) + whole.shape), coef
+
+
+def stage_solve(place, near, far, coef, members):
     big = (BLOCKS, 2 * WIN, 128)
     return call(
         solve_kernel,
-        (SMEM, VMEM, VMEM),
+        (SMEM, VMEM, VMEM, VMEM),
         ((members, 8, 512),),
         (big,) * 6 + ((8, 512),),
-    )(place, got, coef)[0]
+    )(place, near, far, coef)[0]
 
 
 def stage_last(table, got, g, low, high, north, south, fluid):
@@ -424,8 +428,8 @@
 
     low = lax.ppermute(f[:, SX - 2 :], "gx", ring("gx", 1))
     high = lax.ppermute(f[:, :2], "gx", ring("gx", -1))
-    above = lax.ppermute(north, "gy", ring("gy", -1))
-    below = lax.ppermute(south, "gy", ring("gy", 1))
+    above = lax.ppermute(north, GY, ring(GY, -1))
+    below = lax.ppermute(south, GY, ring(GY, 1))
     return low, high, above, below
 
 
@@ -438,27 +442,33 @@
     table, cross = velocity_tables(vel_index, signs, coupling)
     fluid = jnp.where(cell_type == 1, 0.0, 1.0).astype(F32)
     walls = wall_rows(cell_type, lax.axis_index("vert"))
-    place = (lax.axis_index("gx") * 4 + lax.axis_index("gy")).astype(jnp.int32).reshape(1)
+    own = lax.axis_index("gx") * 4 + lax.axis_index(GY)
+    place = jnp.stack([own, lax.axis_index("core")]).astype(jnp.int32)
     win_one, north, south = stage_first(f, table, members)
     got_one = swap_all(win_one, "vert")
-    near, got_one = lax.optimization_barrier((halos(f, north, south), got_one))
+    near = halos(f, north, south)
+    near, got_one = lax.optimization_barrier((near, got_one))
     g, win_two, north, south = stage_second(f, table, *near, fluid, cross, members)
     got_two = swap_all(win_two, "vert")
-    near, got_two = lax.optimization_barrier((halos(g, north, south), got_two))
+    near = halos(g, north, south)
     whole, coef = stage_middle(got_one, got_two, walls)
-    got = swap_all(whole, ("gx", "gy"))
-    sent = stage_solve(place, got, coef, members)
+    this_core = swap_all(whole, ("gx", "zh"))
+    that_core = lax.ppermute(this_core, "core", [(0, 1), (1, 0)])
+    sent = stage_solve(place, this_core, that_core, coef, members)
     got = swap_all(sent, "vert")
     return stage_last(table, got, g, *near, fluid)
 
 
 def solution(mesh):
     in_specs = (
-        P("vert", "gx", "gy", None),
+        P("vert", "gx", GY, None),
         P(None, "vert"),
         P(None, "vert"),
-        P("gx", "gy", None),
+        P("gx", GY, None),
         P(),
     )
-    out_specs = P("vert", "gx", "gy", None)
-    return jax.shard_map(local, mesh=mesh, in_specs=in_specs, out_specs=out_specs, check_vma=False)
+    out_specs = P("vert", "gx", GY, None)
+    fine_mesh = Mesh(mesh.devices.reshape(4, 2, 2, -1), ("gx",) + GY + ("vert",))
+    return jax.shard_map(
+        local, mesh=fine_mesh, in_specs=in_specs, out_specs=out_specs, check_vma=False
+    )

time: 158 us -> 149 us (0.943)
  the two profiles are of different devices: /device:TPU:1 before, /device:TPU:66 now
where the time goes in v3:
time: 149 us; the launch traced here: 148 us
  starting transfers between devices  65.7 us (44%)
  waiting for transfers between devices  45.3 us (30%)
  Pallas kernels  25.6 us (17%)
  local copies, waits for them, and re-layouts  8.55 us (6%)
  other arithmetic  2.46 us (2%)
    all_to_all x4, starting transfers between devices, swap_all(): return lax.all_to_all(x, axis, 0, 0, tiled=True)  36.9 us
    all_to_all x4, waiting for transfers between devices, swap_all(): return lax.all_to_all(x, axis, 0, 0, tiled=True)  23.7 us
    ppermute x2, waiting for transfers between devices, halos(): below = lax.ppermute(south, GY, ring(GY, 1))  12.3 us
    pallas_call x1, Pallas kernels, stage_solve(): call(solve_kernel, (SMEM, VMEM, VMEM, VMEM), ((members, 8, 512),), (big,)...  12.3 us
    ppermute x2, starting transfers between devices, halos(): above = lax.ppermute(north, GY, ring(GY, -1))  10.8 us
    ppermute x2, waiting for transfers between devices, halos(): above = lax.ppermute(north, GY, ring(GY, -1))  9.26 us
    ppermute x2, starting transfers between devices, halos(): low = lax.ppermute(f[:, SX - 2:], 'gx', ring('gx', 1))  8.2 us
    pallas_call x1, Pallas kernels, stage_last(): call(last_kernel, (SMEM,) + (VMEM,) * 7, (g.shape,), ((NZ, 1024), (4, ROW...  5.83 us
  transfers between devices with their start and end apart: 13, of which 6 were waited for; matrix products, arithmetic and copies ran while one was open for 2% of the time, Pallas kernels for 0%

profile of v3, /device:TPU:66, one launch (start us, length us, event | category | flops | bytes accessed | tf_op | source)
XLA Modules:
  0.0 148.0 jit_solution(14269850902213107261)
XLA Ops:
  0.0 0.7 subtract_multiply_fusion
  0.8 0.0 copy-start.15
  0.9 0.7 copy-done.15
  1.5 0.1 multiply_reduce_fusion.2
  1.6 1.8 %concatenate.13.table = f32[24,32]{1,0:T(8,128)} concatenate(f32[5,32]{1,0:T(8,128)S(1)} %fusion.2, f32[3,32]{1,0:T(4,128)S(1)} %slice.79, f32[1,32]{1,0:T(1,128)S(1)} %broadcast.110, f32[1,32]{1,0:T(1,128)S(1)} %get-tuple-element.51, f32[1,32]{1,0:T(1,128)S(1)} %broadcast_multiply_fusion.3, f32[1,32]{1,0:T(1,128)S(1)} %get-tuple-element.54, f32[1,32]{1,0:T(1,128)S(1)} %get-tuple-element.57, ...), dimensions={0} | concatenate | bytes 6144 | tf_op jit(solution)/shard_map/concatenate | solution.py:83
  3.5 2.7 %shard_map.64 = (f32[32,24,256]{2,1,0:T(8,128)}, f32[32,8,128]{2,1,0:T(8,128)}, f32[32,8,128]{2,1,0:T(8,128)}) custom-call(f32[24,32]{1,0:T(8,128)} %concatenate.13.table, f32[32,4,8,128]{3,2,1,0:T(8,128)} %f.3), custom_call_target="tpu_custom_call" | custom-call | tf_op jit(solution)/shard_map/pallas_call | solution.py:367
  6.1 10.4 %all-to-all-start = ((f32[32,24,256]{2,1,0:T(8,128)}), f32[32,24,256]{2,1,0:T(8,128)S(1)}, u32[]{:S(2)}, u32[]{:S(2)}) async-start(f32[32,24,256]{2,1,0:T(8,128)} %get-tuple-element.19), calls=%async_computation | async-start | bytes 1572864 | tf_op jit(solution)/shard_map/all_to_all | solution.py:437
  16.5 0.0 copy-done
  16.5 0.0 copy-start.19
  16.6 2.1 %collective-permute-start.1 = (f32[32,2,8,128]{3,2,1,0:T(8,128)S(1)}, f32[32,2,8,128]{3,2,1,0:T(8,128)S(1)}, u32[]{:S(2)}, u32[]{:S(2)}) collective-permute-start(f32[32,2,8,128]{3,2,1,0:T(8,128)S(1)} %get-tuple-element.35), channel_id=1, source_target_pairs={{0,384},{128,0},{256,128},{384,256},{1,385},{129,1},{257,129},{385... | collective-permute-start | bytes 786440 | tf_op jit(solution)/shard_map/ppermute | solution.py:430
  18.7 4.3 %collective-permute-start = (f32[32,2,8,128]{3,2,1,0:T(8,128)S(1)}, f32[32,2,8,128]{3,2,1,0:T(8,128)S(1)}, u32[]{:S(2)}, u32[]{:S(2)}) collective-permute-start(f32[32,2,8,128]{3,2,1,0:T(8,128)S(1)} %get-tuple-element.36), channel_id=1, source_target_pairs={{0,128},{128,256},{256,384},{384,0},{1,129},{129,257},{257,385},{3... | collective-permute-start | bytes 786440 | tf_op jit(solution)/shard_map/ppermute | solution.py:429
  23.0 0.0 copy-done.19
  23.0 8.0 %collective-permute-start.2 = (f32[32,8,128]{2,1,0:T(8,128)S(1)}, f32[32,8,128]{2,1,0:T(8,128)S(1)}, u32[]{:S(2)}, u32[]{:S(2)}) collective-permute-start(f32[32,8,128]{2,1,0:T(8,128)S(1)} %copy-done.19), channel_id=1, source_target_pairs={{0,96},{32,0},{64,32},{96,64},{1,97},{33,1},{65,33},{97,65},{2,98}... | collective-permute-start | bytes 393224 | tf_op jit(solution)/shard_map/ppermute | solution.py:431
  31.0 1.9 %collective-permute-start.3 = (f32[32,8,128]{2,1,0:T(8,128)S(1)}, f32[32,8,128]{2,1,0:T(8,128)S(1)}, u32[]{:S(2)}, u32[]{:S(2)}) collective-permute-start(f32[32,8,128]{2,1,0:T(8,128)S(1)} %copy-done.18), channel_id=1, source_target_pairs={{0,32},{32,64},{64,96},{96,0},{1,33},{33,65},{65,97},{97,1},{2,34}... | collective-permute-start | bytes 393224 | tf_op jit(solution)/shard_map/ppermute | solution.py:432
  32.9 0.1 multiply_reduce_fusion.1
  33.0 0.6 reshape.75.cross
  33.7 0.6 broadcast_select_fusion
  34.3 0.3 collective-permute-done.2.north
  34.6 8.7 %collective-permute-done.3.south = f32[32,8,128]{2,1,0:T(8,128)S(1)} collective-permute-done((f32[32,8,128]{2,1,0:T(8,128)S(1)}, f32[32,8,128]{2,1,0:T(8,128)S(1)}, u32[]{:S(2)}, u32[]{:S(2)}) %collective-permute-start.3) | collective-permute-done | bytes 131104 | tf_op jit(solution)/shard_map/ppermute | solution.py:432
  43.2 0.0 collective-permute-done.1.high
  43.2 0.0 collective-permute-done.low
  43.2 0.0 all-to-all-done
  43.3 0.0 copy-done.9
  43.3 0.6 copy-done.10
  43.9 0.1 copy-done.7
  44.0 0.1 copy-done.8
  44.1 4.7 %shard_map.65 = (f32[32,4,8,128]{3,2,1,0:T(8,128)}, f32[32,16,256]{2,1,0:T(8,128)}, f32[32,8,128]{2,1,0:T(8,128)}, f32[32,8,128]{2,1,0:T(8,128)}) custom-call(f32[24,32]{1,0:T(8,128)} %concatenate.13.table, f32[32,4,8,128]{3,2,1,0:T(8,128)} %f.3, f32[32,2,8,128]{3,2,1,0:T(8,128)} %copy-done.8, f32[32,2,8,128]{3,2,1,0:T(8,128)} %copy-done.7, ...), custom_call_target="tpu_custom_call" | custom-call | tf_op jit(solution)/shard_map/pallas_call | solution.py:377
  48.8 9.8 %all-to-all-start.1 = ((f32[32,16,256]{2,1,0:T(8,128)}), f32[32,16,256]{2,1,0:T(8,128)S(1)}, u32[]{:S(2)}, u32[]{:S(2)}) async-start(f32[32,16,256]{2,1,0:T(8,128)} %get-tuple-element.25), calls=%async_computation.1 | async-start | bytes 1048576 | tf_op jit(solution)/shard_map/all_to_all | solution.py:437
  58.6 0.1 slice.80
  58.7 0.1 fusion.1
  58.8 0.1 fusion.11
  58.8 0.1 copy.10
  58.9 0.1 slice.69
  59.0 0.1 copy.11
  59.0 0.1 slice.72
  59.1 0.1 reduce_sum.66
  59.2 13.4 %all-to-all-done.1 = f32[32,16,256]{2,1,0:T(8,128)S(1)} async-done(((f32[32,16,256]{2,1,0:T(8,128)}), f32[32,16,256]{2,1,0:T(8,128)S(1)}, u32[]{:S(2)}, u32[]{:S(2)}) %all-to-all-start.1) | async-done | bytes 524320 | tf_op jit(solution)/shard_map/all_to_all | solution.py:437
  72.7 0.7 broadcast_in_dim.34
  73.5 10.5 %all-to-all-start.2 = ((f32[8,40,256]{2,1,0:T(8,128)}), f32[8,40,256]{2,1,0:T(8,128)S(1)}, u32[]{:S(2)}, u32[]{:S(2)}) async-start(f32[8,40,256]{2,1,0:T(8,128)} %broadcast_in_dim.34), calls=%async_computation.2 | async-start | bytes 655360 | tf_op jit(solution)/shard_map/all_to_all | solution.py:437
  83.9 10.2 %all-to-all-done.2.near = f32[8,40,256]{2,1,0:T(8,128)S(1)} async-done(((f32[8,40,256]{2,1,0:T(8,128)}), f32[8,40,256]{2,1,0:T(8,128)S(1)}, u32[]{:S(2)}, u32[]{:S(2)}) %all-to-all-start.2) | async-done | bytes 327712 | tf_op jit(solution)/shard_map/all_to_all | solution.py:437
  94.2 1.9 %collective-permute-start.4 = (f32[8,40,256]{2,1,0:T(8,128)S(1)}, f32[8,40,256]{2,1,0:T(8,128)S(1)}, u32[]{:S(2)}, u32[]{:S(2)}) collective-permute-start(f32[8,40,256]{2,1,0:T(8,128)S(1)} %all-to-all-done.2.near), channel_id=1, source_target_pairs={{0,32},{32,0},{1,33},{33,1},{2,34},{34,2},{3,35},{35,3},{4,36},{36... | collective-permute-start | bytes 983048 | tf_op jit(solution)/shard_map/ppermute | solution.py:456
  96.1 0.6 pad_add_fusion.place
  96.7 0.1 reshape_squeeze.3
  96.8 0.1 multiply_reduce_fusion
  96.9 0.1 broadcast_in_dim.35
  97.0 0.7 reshape.76.coef
  97.7 0.0 collective-permute-done.4.far
  97.7 0.7 copy-done.4
  98.4 12.3 %shard_map.66 = f32[32,8,512]{2,1,0:T(8,128)} custom-call(s32[2]{0:T(128)} %pad_add_fusion.place, f32[8,40,256]{2,1,0:T(8,128)} %copy-done.3, f32[8,40,256]{2,1,0:T(8,128)} %copy-done.4, f32[8,256]{1,0:T(8,128)} %reshape.76.coef), custom_call_target="tpu_custom_call" | custom-call | tf_op jit(solution)/shard_map/pallas_call | solution.py:407
  110.8 6.3 %all-to-all-start.3 = ((f32[32,8,512]{2,1,0:T(8,128)}), f32[32,8,512]{2,1,0:T(8,128)S(1)}, u32[]{:S(2)}, u32[]{:S(2)}) async-start(f32[32,8,512]{2,1,0:T(8,128)} %shard_map.66), calls=%async_computation.3 | async-start | bytes 1048576 | tf_op jit(solution)/shard_map/all_to_all | solution.py:437
  117.1 2.1 %collective-permute-start.6 = (f32[32,2,8,128]{3,2,1,0:T(8,128)S(1)}, f32[32,2,8,128]{3,2,1,0:T(8,128)S(1)}, u32[]{:S(2)}, u32[]{:S(2)}) collective-permute-start(f32[32,2,8,128]{3,2,1,0:T(8,128)S(1)} %get-tuple-element.33), channel_id=1, source_target_pairs={{0,384},{128,0},{256,128},{384,256},{1,385},{129,1},{257,129},{385... | collective-permute-start | bytes 786440 | tf_op jit(solution)/shard_map/ppermute | solution.py:430
  119.2 3.9 %collective-permute-start.5 = (f32[32,2,8,128]{3,2,1,0:T(8,128)S(1)}, f32[32,2,8,128]{3,2,1,0:T(8,128)S(1)}, u32[]{:S(2)}, u32[]{:S(2)}) collective-permute-start(f32[32,2,8,128]{3,2,1,0:T(8,128)S(1)} %get-tuple-element.34), channel_id=1, source_target_pairs={{0,128},{128,256},{256,384},{384,0},{1,129},{129,257},{257,385},{3... | collective-permute-start | bytes 786440 | tf_op jit(solution)/shard_map/ppermute | solution.py:429
  123.1 2.8 %collective-permute-start.7 = (f32[32,8,128]{2,1,0:T(8,128)S(1)}, f32[32,8,128]{2,1,0:T(8,128)S(1)}, u32[]{:S(2)}, u32[]{:S(2)}) collective-permute-start(f32[32,8,128]{2,1,0:T(8,128)S(1)} %copy-done.17), channel_id=1, source_target_pairs={{0,96},{32,0},{64,32},{96,64},{1,97},{33,1},{65,33},{97,65},{2,98}... | collective-permute-start | bytes 393224 | tf_op jit(solution)/shard_map/ppermute | solution.py:431
  125.9 1.9 %collective-permute-start.8 = (f32[32,8,128]{2,1,0:T(8,128)S(1)}, f32[32,8,128]{2,1,0:T(8,128)S(1)}, u32[]{:S(2)}, u32[]{:S(2)}) collective-permute-start(f32[32,8,128]{2,1,0:T(8,128)S(1)} %copy-done.16), channel_id=1, source_target_pairs={{0,32},{32,64},{64,96},{96,0},{1,33},{33,65},{65,97},{97,1},{2,34}... | collective-permute-start | bytes 393224 | tf_op jit(solution)/shard_map/ppermute | solution.py:432
  127.8 9.0 %collective-permute-done.7.north = f32[32,8,128]{2,1,0:T(8,128)S(1)} collective-permute-done((f32[32,8,128]{2,1,0:T(8,128)S(1)}, f32[32,8,128]{2,1,0:T(8,128)S(1)}, u32[]{:S(2)}, u32[]{:S(2)}) %collective-permute-start.7) | collective-permute-done | bytes 131104 | tf_op jit(solution)/shard_map/ppermute | solution.py:431
  136.8 3.7 %collective-permute-done.8.south = f32[32,8,128]{2,1,0:T(8,128)S(1)} collective-permute-done((f32[32,8,128]{2,1,0:T(8,128)S(1)}, f32[32,8,128]{2,1,0:T(8,128)S(1)}, u32[]{:S(2)}, u32[]{:S(2)}) %collective-permute-start.8) | collective-permute-done | bytes 131104 | tf_op jit(solution)/shard_map/ppermute | solution.py:432
  140.5 0.0 collective-permute-done.6.high
  140.5 0.0 collective-permute-done.5.low
  140.5 0.0 all-to-all-done.3.recv
  140.5 0.6 copy-done.12
  141.2 0.1 copy-done.5
  141.2 0.1 copy-done.6
  141.3 0.8 copy-done.2
  142.2 5.8 %shard_map.67 = f32[32,4,8,128]{3,2,1,0:T(8,128)} custom-call(f32[24,32]{1,0:T(8,128)} %concatenate.13.table, f32[32,8,512]{2,1,0:T(8,128)} %copy-done.2, f32[32,4,8,128]{3,2,1,0:T(8,128)} %get-tuple-element.26.g, f32[32,2,8,128]{3,2,1,0:T(8,128)} %copy-done.6, f32[32,2,8,128]{3,2,1,0:T(8,128)} %copy-done.5, f32[32,8,128]{2,1,0:T(8,128)} %copy-done.11, ...), custom_call_target="tpu_custom_call" | custom-call | tf_op jit(solution)/shard_map/pallas_call | solution.py:416
  (47 shorter events, 0.4 us)
Async XLA Ops:
  0.8 0.7 copy-start.15
  6.1 10.4 %copy-start = (f32[32,4,8,128]{3,2,1,0:T(8,128)S(1)}, f32[32,4,8,128]{3,2,1,0:T(8,128)}, u32[]{:S(2)}) copy-start(f32[32,4,8,128]{3,2,1,0:T(8,128)} %f.3) | copy-start | bytes 1572868
  6.1 37.1 %all-to-all-start = ((f32[32,24,256]{2,1,0:T(8,128)}), f32[32,24,256]{2,1,0:T(8,128)S(1)}, u32[]{:S(2)}, u32[]{:S(2)}) async-start(f32[32,24,256]{2,1,0:T(8,128)} %get-tuple-element.19), calls=%async_computation | async-start | bytes 1572864 | tf_op jit(solution)/shard_map/all_to_all | solution.py:437
  16.5 6.4 %copy-start.19 = (f32[32,8,128]{2,1,0:T(8,128)S(1)}, f32[32,8,128]{2,1,0:T(8,128)}, u32[]{:S(2)}) copy-start(f32[32,8,128]{2,1,0:T(8,128)} %get-tuple-element.17) | copy-start | bytes 393220
  16.5 14.4 %copy-start.18 = (f32[32,8,128]{2,1,0:T(8,128)S(1)}, f32[32,8,128]{2,1,0:T(8,128)}, u32[]{:S(2)}) copy-start(f32[32,8,128]{2,1,0:T(8,128)} %get-tuple-element.18) | copy-start | bytes 393220
  16.6 26.6 %collective-permute-start.1 = (f32[32,2,8,128]{3,2,1,0:T(8,128)S(1)}, f32[32,2,8,128]{3,2,1,0:T(8,128)S(1)}, u32[]{:S(2)}, u32[]{:S(2)}) collective-permute-start(f32[32,2,8,128]{3,2,1,0:T(8,128)S(1)} %get-tuple-element.35), channel_id=1, source_target_pairs={{0,384},{128,0},{256,128},{384,256},{1,385},{129,1},{257,129},{385... | collective-permute-start | bytes 786440 | tf_op jit(solution)/shard_map/ppermute | solution.py:430
  18.7 24.6 %collective-permute-start = (f32[32,2,8,128]{3,2,1,0:T(8,128)S(1)}, f32[32,2,8,128]{3,2,1,0:T(8,128)S(1)}, u32[]{:S(2)}, u32[]{:S(2)}) collective-permute-start(f32[32,2,8,128]{3,2,1,0:T(8,128)S(1)} %get-tuple-element.36), channel_id=1, source_target_pairs={{0,128},{128,256},{256,384},{384,0},{1,129},{129,257},{257,385},{3... | collective-permute-start | bytes 786440 | tf_op jit(solution)/shard_map/ppermute | solution.py:429
  23.0 11.6 %collective-permute-start.2 = (f32[32,8,128]{2,1,0:T(8,128)S(1)}, f32[32,8,128]{2,1,0:T(8,128)S(1)}, u32[]{:S(2)}, u32[]{:S(2)}) collective-permute-start(f32[32,8,128]{2,1,0:T(8,128)S(1)} %copy-done.19), channel_id=1, source_target_pairs={{0,96},{32,0},{64,32},{96,64},{1,97},{33,1},{65,33},{97,65},{2,98}... | collective-permute-start | bytes 393224 | tf_op jit(solution)/shard_map/ppermute | solution.py:431
  31.0 12.3 %collective-permute-start.3 = (f32[32,8,128]{2,1,0:T(8,128)S(1)}, f32[32,8,128]{2,1,0:T(8,128)S(1)}, u32[]{:S(2)}, u32[]{:S(2)}) collective-permute-start(f32[32,8,128]{2,1,0:T(8,128)S(1)} %copy-done.18), channel_id=1, source_target_pairs={{0,32},{32,64},{64,96},{96,0},{1,33},{33,65},{65,97},{97,1},{2,34}... | collective-permute-start | bytes 393224 | tf_op jit(solution)/shard_map/ppermute | solution.py:432
  32.9 0.8 copy-start.14
  34.6 8.7 %copy-start.9 = (f32[32,8,128]{2,1,0:T(8,128)}, f32[32,8,128]{2,1,0:T(8,128)S(1)}, u32[]{:S(2)}) copy-start(f32[32,8,128]{2,1,0:T(8,128)S(1)} %collective-permute-done.2.north) | copy-start | bytes 393220
  43.2 0.6 copy-start.10
  43.2 0.8 copy-start.7
  43.2 0.9 copy-start.8
  48.8 23.8 %all-to-all-start.1 = ((f32[32,16,256]{2,1,0:T(8,128)}), f32[32,16,256]{2,1,0:T(8,128)S(1)}, u32[]{:S(2)}, u32[]{:S(2)}) async-start(f32[32,16,256]{2,1,0:T(8,128)} %get-tuple-element.25), calls=%async_computation.1 | async-start | bytes 1048576 | tf_op jit(solution)/shard_map/all_to_all | solution.py:437
  73.5 20.7 %all-to-all-start.2 = ((f32[8,40,256]{2,1,0:T(8,128)}), f32[8,40,256]{2,1,0:T(8,128)S(1)}, u32[]{:S(2)}, u32[]{:S(2)}) async-start(f32[8,40,256]{2,1,0:T(8,128)} %broadcast_in_dim.34), calls=%async_computation.2 | async-start | bytes 655360 | tf_op jit(solution)/shard_map/all_to_all | solution.py:437
  83.9 12.9 %copy-start.13 = (f32[8,8,8]{2,1,0:T(8,128)S(1)}, f32[8,8,8]{2,1,0:T(8,128)}, u32[]{:S(2)}) copy-start(f32[8,8,8]{2,1,0:T(8,128)} %constant.72.clone) | copy-start | bytes 6148
  94.2 3.5 %copy-start.3 = (f32[8,40,256]{2,1,0:T(8,128)}, f32[8,40,256]{2,1,0:T(8,128)S(1)}, u32[]{:S(2)}) copy-start(f32[8,40,256]{2,1,0:T(8,128)S(1)} %all-to-all-done.2.near) | copy-start | bytes 983044
  94.2 3.5 %collective-permute-start.4 = (f32[8,40,256]{2,1,0:T(8,128)S(1)}, f32[8,40,256]{2,1,0:T(8,128)S(1)}, u32[]{:S(2)}, u32[]{:S(2)}) collective-permute-start(f32[8,40,256]{2,1,0:T(8,128)S(1)} %all-to-all-done.2.near), channel_id=1, source_target_pairs={{0,32},{32,0},{1,33},{33,1},{2,34},{34,2},{3,35},{35,3},{4,36},{36... | collective-permute-start | bytes 983048 | tf_op jit(solution)/shard_map/ppermute | solution.py:456
  97.7 0.7 copy-start.4
  110.8 6.3 %copy-start.1 = (f32[32,4,8,128]{3,2,1,0:T(8,128)S(1)}, f32[32,4,8,128]{3,2,1,0:T(8,128)}, u32[]{:S(2)}) copy-start(f32[32,4,8,128]{3,2,1,0:T(8,128)} %get-tuple-element.26.g) | copy-start | bytes 1572868
  110.8 29.8 %all-to-all-start.3 = ((f32[32,8,512]{2,1,0:T(8,128)}), f32[32,8,512]{2,1,0:T(8,128)S(1)}, u32[]{:S(2)}, u32[]{:S(2)}) async-start(f32[32,8,512]{2,1,0:T(8,128)} %shard_map.66), calls=%async_computation.3 | async-start | bytes 1048576 | tf_op jit(solution)/shard_map/all_to_all | solution.py:437
  117.0 6.1 %copy-start.17 = (f32[32,8,128]{2,1,0:T(8,128)S(1)}, f32[32,8,128]{2,1,0:T(8,128)}, u32[]{:S(2)}) copy-start(f32[32,8,128]{2,1,0:T(8,128)} %get-tuple-element.27) | copy-start | bytes 393220
  117.0 8.9 %copy-start.16 = (f32[32,8,128]{2,1,0:T(8,128)S(1)}, f32[32,8,128]{2,1,0:T(8,128)}, u32[]{:S(2)}) copy-start(f32[32,8,128]{2,1,0:T(8,128)} %get-tuple-element.28) | copy-start | bytes 393220
  117.1 23.4 %collective-permute-start.6 = (f32[32,2,8,128]{3,2,1,0:T(8,128)S(1)}, f32[32,2,8,128]{3,2,1,0:T(8,128)S(1)}, u32[]{:S(2)}, u32[]{:S(2)}) collective-permute-start(f32[32,2,8,128]{3,2,1,0:T(8,128)S(1)} %get-tuple-element.33), channel_id=1, source_target_pairs={{0,384},{128,0},{256,128},{384,256},{1,385},{129,1},{257,129},{385... | collective-permute-start | bytes 786440 | tf_op jit(solution)/shard_map/ppermute | solution.py:430
  119.2 21.3 %collective-permute-start.5 = (f32[32,2,8,128]{3,2,1,0:T(8,128)S(1)}, f32[32,2,8,128]{3,2,1,0:T(8,128)S(1)}, u32[]{:S(2)}, u32[]{:S(2)}) collective-permute-start(f32[32,2,8,128]{3,2,1,0:T(8,128)S(1)} %get-tuple-element.34), channel_id=1, source_target_pairs={{0,128},{128,256},{256,384},{384,0},{1,129},{129,257},{257,385},{3... | collective-permute-start | bytes 786440 | tf_op jit(solution)/shard_map/ppermute | solution.py:429
  123.1 13.7 %collective-permute-start.7 = (f32[32,8,128]{2,1,0:T(8,128)S(1)}, f32[32,8,128]{2,1,0:T(8,128)S(1)}, u32[]{:S(2)}, u32[]{:S(2)}) collective-permute-start(f32[32,8,128]{2,1,0:T(8,128)S(1)} %copy-done.17), channel_id=1, source_target_pairs={{0,96},{32,0},{64,32},{96,64},{1,97},{33,1},{65,33},{97,65},{2,98}... | collective-permute-start | bytes 393224 | tf_op jit(solution)/shard_map/ppermute | solution.py:431
  125.9 14.6 %collective-permute-start.8 = (f32[32,8,128]{2,1,0:T(8,128)S(1)}, f32[32,8,128]{2,1,0:T(8,128)S(1)}, u32[]{:S(2)}, u32[]{:S(2)}) collective-permute-start(f32[32,8,128]{2,1,0:T(8,128)S(1)} %copy-done.16), channel_id=1, source_target_pairs={{0,32},{32,64},{64,96},{96,0},{1,33},{33,65},{65,97},{97,1},{2,34}... | collective-permute-start | bytes 393224 | tf_op jit(solution)/shard_map/ppermute | solution.py:432
  136.8 3.7 %copy-start.11 = (f32[32,8,128]{2,1,0:T(8,128)}, f32[32,8,128]{2,1,0:T(8,128)S(1)}, u32[]{:S(2)}) copy-start(f32[32,8,128]{2,1,0:T(8,128)S(1)} %collective-permute-done.7.north) | copy-start | bytes 393220
  140.5 0.7 copy-start.12
  140.5 0.7 copy-start.5
  140.5 0.8 copy-start.6
  141.3 0.8 copy-start.2

commit v4 on v3

--- a/solution.py
+++ b/solution.py
@@ -11,6 +11,7 @@
 V = 1024
 INTERPRET = False
 UNROLL = 16
+LAST, SECOND, MOMENTS = 2, 8, 8
 
 absorb = 0.5
 damping = 0.8
@@ -107,7 +108,7 @@
             out += [accs[r * SX + x] + w * tiles[x] for x in range(SX)]
         return tuple(out)
 
-    accs = lax.fori_loop(0, src.shape[0], step, (zero,) * (ROWS * SX), unroll=2)
+    accs = lax.fori_loop(0, src.shape[0], step, (zero,) * (ROWS * SX), unroll=MOMENTS)
     for i, acc in enumerate(accs):
         m_scr[i * SY : (i + 1) * SY, :] = acc
     for h in range(2):
@@ -181,7 +182,7 @@
             g[v, x] = fluid[x] * moved[x]
         return carry
 
-    lax.fori_loop(0, f.shape[0], step, 0, unroll=2)
+    lax.fori_loop(0, f.shape[0], step, 0, unroll=SECOND)
     moments(g, table, m_scr, ext)
     for j in range(win.shape[0]):
         win[j] = ext[4 * j + 10 : 4 * j + 10 + WIN2, :]
@@ -341,7 +342,7 @@
             out[v, x] = fluid[x] * moved[x] + lift(3, x)
         return carry
 
-    lax.fori_loop(0, out.shape[0], step, 0)
+    lax.fori_loop(0, out.shape[0], step, 0, unroll=LAST)
 
 
 GY = ("zh", "core")

time: 149 us -> 146 us (0.980)
  Pallas kernels: 25.6 us -> 23.1 us
where the time goes in v4:
time: 146 us; the launch traced here: 145 us
  starting transfers between devices  65.7 us (45%)
  waiting for transfers between devices  45.3 us (31%)
  Pallas kernels  23.1 us (16%)
  local copies, waits for them, and re-layouts  8.55 us (6%)
  other arithmetic  2.46 us (2%)
    all_to_all x4, starting transfers between devices, swap_all(): return lax.all_to_all(x, axis, 0, 0, tiled=True)  36.9 us
    all_to_all x4, waiting for transfers between devices, swap_all(): return lax.all_to_all(x, axis, 0, 0, tiled=True)  23.7 us
    ppermute x2, waiting for transfers between devices, halos(): below = lax.ppermute(south, GY, ring(GY, 1))  12.3 us
    pallas_call x1, Pallas kernels, stage_solve(): call(solve_kernel, (SMEM, VMEM, VMEM, VMEM), ((members, 8, 512),), (big,)...  12.3 us
    ppermute x2, starting transfers between devices, halos(): above = lax.ppermute(north, GY, ring(GY, -1))  10.8 us
    ppermute x2, waiting for transfers between devices, halos(): above = lax.ppermute(north, GY, ring(GY, -1))  9.26 us
    ppermute x2, starting transfers between devices, halos(): low = lax.ppermute(f[:, SX - 2:], 'gx', ring('gx', 1))  8.2 us
    pallas_call x1, Pallas kernels, stage_last(): call(last_kernel, (SMEM,) + (VMEM,) * 7, (g.shape,), ((NZ, 1024), (4, ROW...  4.42 us
  transfers between devices with their start and end apart: 13, of which 6 were waited for; matrix products, arithmetic and copies ran while one was open for 2% of the time, Pallas kernels for 0%

profile of v4, /device:TPU:66, one launch (start us, length us, event | category | flops | bytes accessed | tf_op | source)
XLA Modules:
  0.0 145.5 jit_solution(8333777703458904117)
XLA Ops:
  0.0 0.7 subtract_multiply_fusion
  0.8 0.0 copy-start.15
  0.9 0.7 copy-done.15
  1.5 0.1 multiply_reduce_fusion.2
  1.6 1.8 %concatenate.13.table = f32[24,32]{1,0:T(8,128)} concatenate(f32[5,32]{1,0:T(8,128)S(1)} %fusion.2, f32[3,32]{1,0:T(4,128)S(1)} %slice.79, f32[1,32]{1,0:T(1,128)S(1)} %broadcast.110, f32[1,32]{1,0:T(1,128)S(1)} %get-tuple-element.51, f32[1,32]{1,0:T(1,128)S(1)} %broadcast_multiply_fusion.3, f32[1,32]{1,0:T(1,128)S(1)} %get-tuple-element.54, f32[1,32]{1,0:T(1,128)S(1)} %get-tuple-element.57, ...), dimensions={0} | concatenate | bytes 6144 | tf_op jit(solution)/shard_map/concatenate | solution.py:84
  3.5 2.6 %shard_map.64 = (f32[32,24,256]{2,1,0:T(8,128)}, f32[32,8,128]{2,1,0:T(8,128)}, f32[32,8,128]{2,1,0:T(8,128)}) custom-call(f32[24,32]{1,0:T(8,128)} %concatenate.13.table, f32[32,4,8,128]{3,2,1,0:T(8,128)} %f.3), custom_call_target="tpu_custom_call" | custom-call | tf_op jit(solution)/shard_map/pallas_call | solution.py:368
  6.0 10.4 %all-to-all-start = ((f32[32,24,256]{2,1,0:T(8,128)}), f32[32,24,256]{2,1,0:T(8,128)S(1)}, u32[]{:S(2)}, u32[]{:S(2)}) async-start(f32[32,24,256]{2,1,0:T(8,128)} %get-tuple-element.19), calls=%async_computation | async-start | bytes 1572864 | tf_op jit(solution)/shard_map/all_to_all | solution.py:438
  16.4 0.0 copy-start.19
  16.5 2.1 %collective-permute-start.1 = (f32[32,2,8,128]{3,2,1,0:T(8,128)S(1)}, f32[32,2,8,128]{3,2,1,0:T(8,128)S(1)}, u32[]{:S(2)}, u32[]{:S(2)}) collective-permute-start(f32[32,2,8,128]{3,2,1,0:T(8,128)S(1)} %get-tuple-element.35), channel_id=1, source_target_pairs={{0,384},{128,0},{256,128},{384,256},{1,385},{129,1},{257,129},{385... | collective-permute-start | bytes 786440 | tf_op jit(solution)/shard_map/ppermute | solution.py:431
  18.6 4.3 %collective-permute-start = (f32[32,2,8,128]{3,2,1,0:T(8,128)S(1)}, f32[32,2,8,128]{3,2,1,0:T(8,128)S(1)}, u32[]{:S(2)}, u32[]{:S(2)}) collective-permute-start(f32[32,2,8,128]{3,2,1,0:T(8,128)S(1)} %get-tuple-element.36), channel_id=1, source_target_pairs={{0,128},{128,256},{256,384},{384,0},{1,129},{129,257},{257,385},{3... | collective-permute-start | bytes 786440 | tf_op jit(solution)/shard_map/ppermute | solution.py:430
  22.8 0.0 copy-done.19
  22.8 8.0 %collective-permute-start.2 = (f32[32,8,128]{2,1,0:T(8,128)S(1)}, f32[32,8,128]{2,1,0:T(8,128)S(1)}, u32[]{:S(2)}, u32[]{:S(2)}) collective-permute-start(f32[32,8,128]{2,1,0:T(8,128)S(1)} %copy-done.19), channel_id=1, source_target_pairs={{0,96},{32,0},{64,32},{96,64},{1,97},{33,1},{65,33},{97,65},{2,98}... | collective-permute-start | bytes 393224 | tf_op jit(solution)/shard_map/ppermute | solution.py:432
  30.8 1.9 %collective-permute-start.3 = (f32[32,8,128]{2,1,0:T(8,128)S(1)}, f32[32,8,128]{2,1,0:T(8,128)S(1)}, u32[]{:S(2)}, u32[]{:S(2)}) collective-permute-start(f32[32,8,128]{2,1,0:T(8,128)S(1)} %copy-done.18), channel_id=1, source_target_pairs={{0,32},{32,64},{64,96},{96,0},{1,33},{33,65},{65,97},{97,1},{2,34}... | collective-permute-start | bytes 393224 | tf_op jit(solution)/shard_map/ppermute | solution.py:433
  32.8 0.1 multiply_reduce_fusion.1
  32.9 0.6 reshape.75.cross
  33.6 0.6 broadcast_select_fusion
  34.2 0.3 collective-permute-done.2.north
  34.5 8.7 %collective-permute-done.3.south = f32[32,8,128]{2,1,0:T(8,128)S(1)} collective-permute-done((f32[32,8,128]{2,1,0:T(8,128)S(1)}, f32[32,8,128]{2,1,0:T(8,128)S(1)}, u32[]{:S(2)}, u32[]{:S(2)}) %collective-permute-start.3) | collective-permute-done | bytes 131104 | tf_op jit(solution)/shard_map/ppermute | solution.py:433
  43.1 0.0 collective-permute-done.1.high
  43.1 0.0 collective-permute-done.low
  43.1 0.0 all-to-all-done
  43.2 0.6 copy-done.10
  43.8 0.1 copy-done.7
  43.9 0.1 copy-done.8
  44.0 3.7 %shard_map.65 = (f32[32,4,8,128]{3,2,1,0:T(8,128)}, f32[32,16,256]{2,1,0:T(8,128)}, f32[32,8,128]{2,1,0:T(8,128)}, f32[32,8,128]{2,1,0:T(8,128)}) custom-call(f32[24,32]{1,0:T(8,128)} %concatenate.13.table, f32[32,4,8,128]{3,2,1,0:T(8,128)} %f.3, f32[32,2,8,128]{3,2,1,0:T(8,128)} %copy-done.8, f32[32,2,8,128]{3,2,1,0:T(8,128)} %copy-done.7, ...), custom_call_target="tpu_custom_call" | custom-call | tf_op jit(solution)/shard_map/pallas_call | solution.py:378
  47.7 9.8 %all-to-all-start.1 = ((f32[32,16,256]{2,1,0:T(8,128)}), f32[32,16,256]{2,1,0:T(8,128)S(1)}, u32[]{:S(2)}, u32[]{:S(2)}) async-start(f32[32,16,256]{2,1,0:T(8,128)} %get-tuple-element.25), calls=%async_computation.1 | async-start | bytes 1048576 | tf_op jit(solution)/shard_map/all_to_all | solution.py:438
  57.5 0.1 slice.80
  57.6 0.1 fusion.1
  57.7 0.1 fusion.11
  57.7 0.1 copy.10
  57.8 0.1 slice.69
  57.9 0.1 copy.11
  58.0 0.1 slice.72
  58.0 0.1 reduce_sum.66
  58.1 13.4 %all-to-all-done.1 = f32[32,16,256]{2,1,0:T(8,128)S(1)} async-done(((f32[32,16,256]{2,1,0:T(8,128)}), f32[32,16,256]{2,1,0:T(8,128)S(1)}, u32[]{:S(2)}, u32[]{:S(2)}) %all-to-all-start.1) | async-done | bytes 524320 | tf_op jit(solution)/shard_map/all_to_all | solution.py:438
  71.6 0.7 broadcast_in_dim.34
  72.4 10.5 %all-to-all-start.2 = ((f32[8,40,256]{2,1,0:T(8,128)}), f32[8,40,256]{2,1,0:T(8,128)S(1)}, u32[]{:S(2)}, u32[]{:S(2)}) async-start(f32[8,40,256]{2,1,0:T(8,128)} %broadcast_in_dim.34), calls=%async_computation.2 | async-start | bytes 655360 | tf_op jit(solution)/shard_map/all_to_all | solution.py:438
  82.9 10.2 %all-to-all-done.2.near = f32[8,40,256]{2,1,0:T(8,128)S(1)} async-done(((f32[8,40,256]{2,1,0:T(8,128)}), f32[8,40,256]{2,1,0:T(8,128)S(1)}, u32[]{:S(2)}, u32[]{:S(2)}) %all-to-all-start.2) | async-done | bytes 327712 | tf_op jit(solution)/shard_map/all_to_all | solution.py:438
  93.1 1.9 %collective-permute-start.4 = (f32[8,40,256]{2,1,0:T(8,128)S(1)}, f32[8,40,256]{2,1,0:T(8,128)S(1)}, u32[]{:S(2)}, u32[]{:S(2)}) collective-permute-start(f32[8,40,256]{2,1,0:T(8,128)S(1)} %all-to-all-done.2.near), channel_id=1, source_target_pairs={{0,32},{32,0},{1,33},{33,1},{2,34},{34,2},{3,35},{35,3},{4,36},{36... | collective-permute-start | bytes 983048 | tf_op jit(solution)/shard_map/ppermute | solution.py:457
  95.0 0.6 pad_add_fusion.place
  95.7 0.1 reshape_squeeze.3
  95.7 0.1 multiply_reduce_fusion
  95.8 0.1 broadcast_in_dim.35
  95.9 0.7 reshape.76.coef
  96.6 0.0 collective-permute-done.4.far
  96.6 0.7 copy-done.4
  97.3 12.3 %shard_map.66 = f32[32,8,512]{2,1,0:T(8,128)} custom-call(s32[2]{0:T(128)} %pad_add_fusion.place, f32[8,40,256]{2,1,0:T(8,128)} %copy-done.3, f32[8,40,256]{2,1,0:T(8,128)} %copy-done.4, f32[8,256]{1,0:T(8,128)} %reshape.76.coef), custom_call_target="tpu_custom_call" | custom-call | tf_op jit(solution)/shard_map/pallas_call | solution.py:408
  109.7 6.3 %all-to-all-start.3 = ((f32[32,8,512]{2,1,0:T(8,128)}), f32[32,8,512]{2,1,0:T(8,128)S(1)}, u32[]{:S(2)}, u32[]{:S(2)}) async-start(f32[32,8,512]{2,1,0:T(8,128)} %shard_map.66), calls=%async_computation.3 | async-start | bytes 1048576 | tf_op jit(solution)/shard_map/all_to_all | solution.py:438
  116.0 2.1 %collective-permute-start.6 = (f32[32,2,8,128]{3,2,1,0:T(8,128)S(1)}, f32[32,2,8,128]{3,2,1,0:T(8,128)S(1)}, u32[]{:S(2)}, u32[]{:S(2)}) collective-permute-start(f32[32,2,8,128]{3,2,1,0:T(8,128)S(1)} %get-tuple-element.33), channel_id=1, source_target_pairs={{0,384},{128,0},{256,128},{384,256},{1,385},{129,1},{257,129},{385... | collective-permute-start | bytes 786440 | tf_op jit(solution)/shard_map/ppermute | solution.py:431
  118.1 3.9 %collective-permute-start.5 = (f32[32,2,8,128]{3,2,1,0:T(8,128)S(1)}, f32[32,2,8,128]{3,2,1,0:T(8,128)S(1)}, u32[]{:S(2)}, u32[]{:S(2)}) collective-permute-start(f32[32,2,8,128]{3,2,1,0:T(8,128)S(1)} %get-tuple-element.34), channel_id=1, source_target_pairs={{0,128},{128,256},{256,384},{384,0},{1,129},{129,257},{257,385},{3... | collective-permute-start | bytes 786440 | tf_op jit(solution)/shard_map/ppermute | solution.py:430
  122.0 0.0 copy-done.17
  122.0 2.8 %collective-permute-start.7 = (f32[32,8,128]{2,1,0:T(8,128)S(1)}, f32[32,8,128]{2,1,0:T(8,128)S(1)}, u32[]{:S(2)}, u32[]{:S(2)}) collective-permute-start(f32[32,8,128]{2,1,0:T(8,128)S(1)} %copy-done.17), channel_id=1, source_target_pairs={{0,96},{32,0},{64,32},{96,64},{1,97},{33,1},{65,33},{97,65},{2,98}... | collective-permute-start | bytes 393224 | tf_op jit(solution)/shard_map/ppermute | solution.py:432
  124.8 1.9 %collective-permute-start.8 = (f32[32,8,128]{2,1,0:T(8,128)S(1)}, f32[32,8,128]{2,1,0:T(8,128)S(1)}, u32[]{:S(2)}, u32[]{:S(2)}) collective-permute-start(f32[32,8,128]{2,1,0:T(8,128)S(1)} %copy-done.16), channel_id=1, source_target_pairs={{0,32},{32,64},{64,96},{96,0},{1,33},{33,65},{65,97},{97,1},{2,34}... | collective-permute-start | bytes 393224 | tf_op jit(solution)/shard_map/ppermute | solution.py:433
  126.7 9.0 %collective-permute-done.7.north = f32[32,8,128]{2,1,0:T(8,128)S(1)} collective-permute-done((f32[32,8,128]{2,1,0:T(8,128)S(1)}, f32[32,8,128]{2,1,0:T(8,128)S(1)}, u32[]{:S(2)}, u32[]{:S(2)}) %collective-permute-start.7) | collective-permute-done | bytes 131104 | tf_op jit(solution)/shard_map/ppermute | solution.py:432
  135.7 3.7 %collective-permute-done.8.south = f32[32,8,128]{2,1,0:T(8,128)S(1)} collective-permute-done((f32[32,8,128]{2,1,0:T(8,128)S(1)}, f32[32,8,128]{2,1,0:T(8,128)S(1)}, u32[]{:S(2)}, u32[]{:S(2)}) %collective-permute-start.8) | collective-permute-done | bytes 131104 | tf_op jit(solution)/shard_map/ppermute | solution.py:433
  139.4 0.0 collective-permute-done.6.high
  139.4 0.0 collective-permute-done.5.low
  139.4 0.0 all-to-all-done.3.recv
  139.4 0.0 copy-done.11
  139.4 0.6 copy-done.12
  140.1 0.1 copy-done.5
  140.1 0.1 copy-done.6
  140.3 0.8 copy-done.2
  141.1 4.4 %shard_map.67 = f32[32,4,8,128]{3,2,1,0:T(8,128)} custom-call(f32[24,32]{1,0:T(8,128)} %concatenate.13.table, f32[32,8,512]{2,1,0:T(8,128)} %copy-done.2, f32[32,4,8,128]{3,2,1,0:T(8,128)} %get-tuple-element.26.g, f32[32,2,8,128]{3,2,1,0:T(8,128)} %copy-done.6, f32[32,2,8,128]{3,2,1,0:T(8,128)} %copy-done.5, f32[32,8,128]{2,1,0:T(8,128)} %copy-done.11, ...), custom_call_target="tpu_custom_call" | custom-call | tf_op jit(solution)/shard_map/pallas_call | solution.py:417
  (47 shorter events, 0.4 us)
Async XLA Ops:
  0.8 0.7 copy-start.15
  6.0 10.4 %copy-start = (f32[32,4,8,128]{3,2,1,0:T(8,128)S(1)}, f32[32,4,8,128]{3,2,1,0:T(8,128)}, u32[]{:S(2)}) copy-start(f32[32,4,8,128]{3,2,1,0:T(8,128)} %f.3) | copy-start | bytes 1572868
  6.0 37.1 %all-to-all-start = ((f32[32,24,256]{2,1,0:T(8,128)}), f32[32,24,256]{2,1,0:T(8,128)S(1)}, u32[]{:S(2)}, u32[]{:S(2)}) async-start(f32[32,24,256]{2,1,0:T(8,128)} %get-tuple-element.19), calls=%async_computation | async-start | bytes 1572864 | tf_op jit(solution)/shard_map/all_to_all | solution.py:438
  16.4 6.4 %copy-start.19 = (f32[32,8,128]{2,1,0:T(8,128)S(1)}, f32[32,8,128]{2,1,0:T(8,128)}, u32[]{:S(2)}) copy-start(f32[32,8,128]{2,1,0:T(8,128)} %get-tuple-element.17) | copy-start | bytes 393220
  16.4 14.4 %copy-start.18 = (f32[32,8,128]{2,1,0:T(8,128)S(1)}, f32[32,8,128]{2,1,0:T(8,128)}, u32[]{:S(2)}) copy-start(f32[32,8,128]{2,1,0:T(8,128)} %get-tuple-element.18) | copy-start | bytes 393220
  16.5 26.6 %collective-permute-start.1 = (f32[32,2,8,128]{3,2,1,0:T(8,128)S(1)}, f32[32,2,8,128]{3,2,1,0:T(8,128)S(1)}, u32[]{:S(2)}, u32[]{:S(2)}) collective-permute-start(f32[32,2,8,128]{3,2,1,0:T(8,128)S(1)} %get-tuple-element.35), channel_id=1, source_target_pairs={{0,384},{128,0},{256,128},{384,256},{1,385},{129,1},{257,129},{385... | collective-permute-start | bytes 786440 | tf_op jit(solution)/shard_map/ppermute | solution.py:431
  18.6 24.6 %collective-permute-start = (f32[32,2,8,128]{3,2,1,0:T(8,128)S(1)}, f32[32,2,8,128]{3,2,1,0:T(8,128)S(1)}, u32[]{:S(2)}, u32[]{:S(2)}) collective-permute-start(f32[32,2,8,128]{3,2,1,0:T(8,128)S(1)} %get-tuple-element.36), channel_id=1, source_target_pairs={{0,128},{128,256},{256,384},{384,0},{1,129},{129,257},{257,385},{3... | collective-permute-start | bytes 786440 | tf_op jit(solution)/shard_map/ppermute | solution.py:430
  22.8 11.6 %collective-permute-start.2 = (f32[32,8,128]{2,1,0:T(8,128)S(1)}, f32[32,8,128]{2,1,0:T(8,128)S(1)}, u32[]{:S(2)}, u32[]{:S(2)}) collective-permute-start(f32[32,8,128]{2,1,0:T(8,128)S(1)} %copy-done.19), channel_id=1, source_target_pairs={{0,96},{32,0},{64,32},{96,64},{1,97},{33,1},{65,33},{97,65},{2,98}... | collective-permute-start | bytes 393224 | tf_op jit(solution)/shard_map/ppermute | solution.py:432
  30.8 12.3 %collective-permute-start.3 = (f32[32,8,128]{2,1,0:T(8,128)S(1)}, f32[32,8,128]{2,1,0:T(8,128)S(1)}, u32[]{:S(2)}, u32[]{:S(2)}) collective-permute-start(f32[32,8,128]{2,1,0:T(8,128)S(1)} %copy-done.18), channel_id=1, source_target_pairs={{0,32},{32,64},{64,96},{96,0},{1,33},{33,65},{65,97},{97,1},{2,34}... | collective-permute-start | bytes 393224 | tf_op jit(solution)/shard_map/ppermute | solution.py:433
  32.8 0.8 copy-start.14
  34.5 8.7 %copy-start.9 = (f32[32,8,128]{2,1,0:T(8,128)}, f32[32,8,128]{2,1,0:T(8,128)S(1)}, u32[]{:S(2)}) copy-start(f32[32,8,128]{2,1,0:T(8,128)S(1)} %collective-permute-done.2.north) | copy-start | bytes 393220
  43.1 0.6 copy-start.10
  43.1 0.8 copy-start.7
  43.1 0.9 copy-start.8
  47.7 23.8 %all-to-all-start.1 = ((f32[32,16,256]{2,1,0:T(8,128)}), f32[32,16,256]{2,1,0:T(8,128)S(1)}, u32[]{:S(2)}, u32[]{:S(2)}) async-start(f32[32,16,256]{2,1,0:T(8,128)} %get-tuple-element.25), calls=%async_computation.1 | async-start | bytes 1048576 | tf_op jit(solution)/shard_map/all_to_all | solution.py:438
  72.4 20.7 %all-to-all-start.2 = ((f32[8,40,256]{2,1,0:T(8,128)}), f32[8,40,256]{2,1,0:T(8,128)S(1)}, u32[]{:S(2)}, u32[]{:S(2)}) async-start(f32[8,40,256]{2,1,0:T(8,128)} %broadcast_in_dim.34), calls=%async_computation.2 | async-start | bytes 655360 | tf_op jit(solution)/shard_map/all_to_all | solution.py:438
  82.8 12.9 %copy-start.13 = (f32[8,8,8]{2,1,0:T(8,128)S(1)}, f32[8,8,8]{2,1,0:T(8,128)}, u32[]{:S(2)}) copy-start(f32[8,8,8]{2,1,0:T(8,128)} %constant.72.clone) | copy-start | bytes 6148
  93.1 3.5 %copy-start.3 = (f32[8,40,256]{2,1,0:T(8,128)}, f32[8,40,256]{2,1,0:T(8,128)S(1)}, u32[]{:S(2)}) copy-start(f32[8,40,256]{2,1,0:T(8,128)S(1)} %all-to-all-done.2.near) | copy-start | bytes 983044
  93.1 3.5 %collective-permute-start.4 = (f32[8,40,256]{2,1,0:T(8,128)S(1)}, f32[8,40,256]{2,1,0:T(8,128)S(1)}, u32[]{:S(2)}, u32[]{:S(2)}) collective-permute-start(f32[8,40,256]{2,1,0:T(8,128)S(1)} %all-to-all-done.2.near), channel_id=1, source_target_pairs={{0,32},{32,0},{1,33},{33,1},{2,34},{34,2},{3,35},{35,3},{4,36},{36... | collective-permute-start | bytes 983048 | tf_op jit(solution)/shard_map/ppermute | solution.py:457
  96.6 0.7 copy-start.4
  109.7 6.3 %copy-start.1 = (f32[32,4,8,128]{3,2,1,0:T(8,128)S(1)}, f32[32,4,8,128]{3,2,1,0:T(8,128)}, u32[]{:S(2)}) copy-start(f32[32,4,8,128]{3,2,1,0:T(8,128)} %get-tuple-element.26.g) | copy-start | bytes 1572868
  109.7 29.8 %all-to-all-start.3 = ((f32[32,8,512]{2,1,0:T(8,128)}), f32[32,8,512]{2,1,0:T(8,128)S(1)}, u32[]{:S(2)}, u32[]{:S(2)}) async-start(f32[32,8,512]{2,1,0:T(8,128)} %shard_map.66), calls=%async_computation.3 | async-start | bytes 1048576 | tf_op jit(solution)/shard_map/all_to_all | solution.py:438
  115.9 6.1 %copy-start.17 = (f32[32,8,128]{2,1,0:T(8,128)S(1)}, f32[32,8,128]{2,1,0:T(8,128)}, u32[]{:S(2)}) copy-start(f32[32,8,128]{2,1,0:T(8,128)} %get-tuple-element.27) | copy-start | bytes 393220
  115.9 8.9 %copy-start.16 = (f32[32,8,128]{2,1,0:T(8,128)S(1)}, f32[32,8,128]{2,1,0:T(8,128)}, u32[]{:S(2)}) copy-start(f32[32,8,128]{2,1,0:T(8,128)} %get-tuple-element.28) | copy-start | bytes 393220
  116.0 23.4 %collective-permute-start.6 = (f32[32,2,8,128]{3,2,1,0:T(8,128)S(1)}, f32[32,2,8,128]{3,2,1,0:T(8,128)S(1)}, u32[]{:S(2)}, u32[]{:S(2)}) collective-permute-start(f32[32,2,8,128]{3,2,1,0:T(8,128)S(1)} %get-tuple-element.33), channel_id=1, source_target_pairs={{0,384},{128,0},{256,128},{384,256},{1,385},{129,1},{257,129},{385... | collective-permute-start | bytes 786440 | tf_op jit(solution)/shard_map/ppermute | solution.py:431
  118.1 21.3 %collective-permute-start.5 = (f32[32,2,8,128]{3,2,1,0:T(8,128)S(1)}, f32[32,2,8,128]{3,2,1,0:T(8,128)S(1)}, u32[]{:S(2)}, u32[]{:S(2)}) collective-permute-start(f32[32,2,8,128]{3,2,1,0:T(8,128)S(1)} %get-tuple-element.34), channel_id=1, source_target_pairs={{0,128},{128,256},{256,384},{384,0},{1,129},{129,257},{257,385},{3... | collective-permute-start | bytes 786440 | tf_op jit(solution)/shard_map/ppermute | solution.py:430
  122.0 13.7 %collective-permute-start.7 = (f32[32,8,128]{2,1,0:T(8,128)S(1)}, f32[32,8,128]{2,1,0:T(8,128)S(1)}, u32[]{:S(2)}, u32[]{:S(2)}) collective-permute-start(f32[32,8,128]{2,1,0:T(8,128)S(1)} %copy-done.17), channel_id=1, source_target_pairs={{0,96},{32,0},{64,32},{96,64},{1,97},{33,1},{65,33},{97,65},{2,98}... | collective-permute-start | bytes 393224 | tf_op jit(solution)/shard_map/ppermute | solution.py:432
  124.8 14.6 %collective-permute-start.8 = (f32[32,8,128]{2,1,0:T(8,128)S(1)}, f32[32,8,128]{2,1,0:T(8,128)S(1)}, u32[]{:S(2)}, u32[]{:S(2)}) collective-permute-start(f32[32,8,128]{2,1,0:T(8,128)S(1)} %copy-done.16), channel_id=1, source_target_pairs={{0,32},{32,64},{64,96},{96,0},{1,33},{33,65},{65,97},{97,1},{2,34}... | collective-permute-start | bytes 393224 | tf_op jit(solution)/shard_map/ppermute | solution.py:433
  135.7 3.7 %copy-start.11 = (f32[32,8,128]{2,1,0:T(8,128)}, f32[32,8,128]{2,1,0:T(8,128)S(1)}, u32[]{:S(2)}) copy-start(f32[32,8,128]{2,1,0:T(8,128)S(1)} %collective-permute-done.7.north) | copy-start | bytes 393220
  139.4 0.7 copy-start.12
  139.4 0.7 copy-start.5
  139.4 0.8 copy-start.6
  140.2 0.8 copy-start.2

commit v5 on v4

--- a/solution.py
+++ b/solution.py
@@ -10,7 +10,6 @@
 
 V = 1024
 INTERPRET = False
-UNROLL = 16
 LAST, SECOND, MOMENTS = 2, 8, 8
 
 absorb = 0.5
@@ -190,88 +189,120 @@
     pack_rows(g, g_north, g_south)
 
 
-def solve_kernel(place, near, far, coef, out, src, coarse, fine, gain, extra, first, msg):
-    shape = (2 * WIN, 128)
-    lane = iota(shape, 1)
-    x_at = (lane // SY) % SX
-    y_at = lane % SY
-    z_odd = iota(shape, 0) % 2
-    is_field = (iota(shape, 0) // WIN) * 4 + lane // COLS < 5
+def neighbours(ref, k, around, step, low, rows):
+    lane = iota((rows, 128), 1)
+    x_at, y_at = (lane // SY) % SX, lane % SY
+
+    def load(q, shift=0):
+        return ref[q, 8 + low + shift : 8 + low + shift + rows, :]
+
+    c = load(k)
+    dx, dy = SY * step, step
+    if len(around) == 4:
+        up, down = roll(load(around[2]), SY - dy, 1), roll(load(around[3]), dy - SY, 1)
+    else:
+        up, down = roll(c, SY - COLS - dy, 1), roll(c, COLS - SY + dy, 1)
+    total = jnp.where(x_at < SX - step, roll(c, -dx, 1), roll(load(around[0]), COLS - dx, 1))
+    total += jnp.where(x_at >= step, roll(c, dx, 1), roll(load(around[1]), dx - COLS, 1))
+    total += jnp.where(y_at < SY - step, roll(c, -dy, 1), up)
+    total += jnp.where(y_at >= step, roll(c, dy, 1), down)
+    return total + load(k, step) + load(k, -step)
+
+
+def around_block(i):
+    gx, gy = i // 4, i % 4
+    return (
+        ((gx + 1) % 4) * 4 + gy,
+        ((gx + 3) % 4) * 4 + gy,
+        gx * 4 + (gy + 1) % 4,
+        gx * 4 + (gy + 3) % 4,
+    )
+
+
+def around_packed(gx):
+    return (BLOCKS + (gx + 1) % 4, BLOCKS + (gx + 3) % 4)
+
+
+EVERY = [(i, around_block(i)) for i in range(BLOCKS)]
+EVERY += [(BLOCKS + gx, around_packed(gx)) for gx in range(4)]
+
+
+def restrict(src, coarse, k, around, rows):
+    lane = iota((rows, 128), 1)
+    c = src[k, 8 : 8 + rows, :]
+    r = (1.0 - damping) * c + (damping / fine_diag) * neighbours(src, k, around, 1, 0, rows)
+    r = r + jnp.where((lane // SY) % 2 == 0, roll(r, -SY, 1), roll(r, SY, 1))
+    r = r + jnp.where(lane % 2 == 0, roll(r, -1, 1), roll(r, 1, 1))
+    r = r + jnp.where(iota((rows, 128), 0) % 2 == 0, roll(r, -1, 0), roll(r, 1, 0))
+    coarse[k, 8 : 8 + rows, :] = 0.125 * r
+
+
+def correct(src, coarse, fine, k, around, rows):
+    span = slice(8, 8 + rows)
+    two = 0.48 * coarse[k, span, :] + 0.04 * neighbours(coarse, k, around, 2, 0, rows)
+    fine[k, span, :] = (damping / fine_diag) * src[k, span, :] + two
+
+
+def smooth(src, fine, k, around, low, rows):
+    span = slice(8 + low, 8 + low + rows)
+    return (1.0 - damping) * fine[k, span, :] + (damping / fine_diag) * (
+        src[k, span, :] + neighbours(fine, k, around, 1, low, rows)
+    )
+
+
+def solve_kernel(place, near, far, coef, out, src, coarse, fine, tail, gain, extra, field, msg):
     tile_sub = iota((8, 128), 0)
     tile_lane = iota((8, 128), 1)
-
-    def unpack(i, carry):
-        mine = i % 2 == place[1]
-        rows = jnp.where(mine, near[i // 2], far[i // 2])
+    lane = iota((WIN2, 128), 1)
+    group = lane // COLS
+
+    def pack(ref, rows):
+        where = iota((rows, 128), 1) // COLS
+        for gx in range(4):
+            packed = ref[4 * gx, 0:rows, :]
+            for gy in range(1, 4):
+                moved = roll(ref[4 * gx + gy, 0:rows, :], COLS * gy, 1)
+                packed = jnp.where(where == gy, moved, packed)
+            src[BLOCKS + gx, 8 : 8 + rows, :] = packed
+
+    for i in range(BLOCKS):
+        rows = jnp.where(i % 2 == place[1], near[i // 2], far[i // 2])
+        src[i, 8 : 8 + WIN, :] = rows[0:WIN, 0:128]
+        tail[i] = rows[0:WIN, 128:256]
         for h in range(2):
-            lanes = slice(h * 128, (h + 1) * 128)
-            src[i, h * WIN : (h + 1) * WIN, :] = rows[0:WIN, lanes]
-            extra[i, h * WIN : h * WIN + 4, :] = jnp.zeros((4, 128), F32)
-            extra[i, h * WIN + 20 : (h + 1) * WIN, :] = jnp.zeros((4, 128), F32)
-            extra[i, h * WIN + 4 : h * WIN + 20, :] = rows[WIN : WIN + WIN2, lanes]
-        gain[i] = jnp.zeros(shape, F32)
+            extra[i, h] = rows[WIN : WIN + WIN2, h * 128 : (h + 1) * 128]
         for half, at in enumerate((WIN, WIN + WIN2 - 1)):
             left = jnp.broadcast_to(rows[at : at + 1, 0:128], (8, 128))
             right = jnp.broadcast_to(rows[at : at + 1, 128:256], (8, 128))
             t = jnp.where(tile_sub < 4, left, right)
             t = jnp.where(tile_lane // COLS == tile_sub % 4, t, 0.0)
             t = t + roll(t, 32, 1)
-            t = t + roll(t, 64, 1)
-            for h in range(2):
-                gain[i, h * WIN + 4 + 8 * half : h * WIN + 12 + 8 * half, :] = t
-        return carry
-
-    lax.fori_loop(0, BLOCKS, unpack, 0, unroll=UNROLL)
-
-    def around(i):
-        gx, gy = i // 4, i % 4
-        return (
-            ((gx + 1) % 4) * 4 + gy,
-            ((gx + 3) % 4) * 4 + gy,
-            gx * 4 + (gy + 1) % 4,
-            gx * 4 + (gy + 3) % 4,
-        )
-
-    def neighbours(ref, i, step):
-        next_x, last_x, next_y, last_y = around(i)
-        c = ref[i]
-        dx, dy = SY * step, step
-        total = jnp.where(x_at < SX - step, roll(c, -dx, 1), roll(ref[next_x], COLS - dx, 1))
-        total += jnp.where(x_at >= step, roll(c, dx, 1), roll(ref[last_x], dx - COLS, 1))
-        total += jnp.where(y_at < SY - step, roll(c, -dy, 1), roll(ref[next_y], SY - dy, 1))
-        total += jnp.where(y_at >= step, roll(c, dy, 1), roll(ref[last_y], dy - SY, 1))
-        return total + roll(c, step, 0) + roll(c, -step, 0)
-
-    def restrict(i, carry):
-        r = (1.0 - damping) * src[i] + (damping / fine_diag) * neighbours(src, i, 1)
-        r = r + jnp.where(x_at % 2 == 0, roll(r, -SY, 1), roll(r, SY, 1))
-        r = r + jnp.where(y_at % 2 == 0, roll(r, -1, 1), roll(r, 1, 1))
-        r = r + jnp.where(z_odd == 0, roll(r, -1, 0), roll(r, 1, 0))
-        coarse[i] = 0.125 * r
-        return carry
-
-    def correct(i, carry):
-        two = 0.48 * coarse[i] + 0.04 * neighbours(coarse, i, 2)
-        fine[i] = (damping / fine_diag) * src[i] + two
-        return carry
-
-    def smooth(i):
-        y = (1.0 - damping) * fine[i] + (damping / fine_diag) * (src[i] + neighbours(fine, i, 1))
-        return jnp.where(is_field, y, src[i])
-
-    def mix(i, carry):
-        field = smooth(i)
-        first[i] = gain[i] * field
-        parts = (field[0:WIN], field[WIN : 2 * WIN])
-        here = lane[0:WIN]
+            gain[i, 8 * half : 8 * half + 8, :] = t + roll(t, 64, 1)
+    pack(tail, WIN)
+    for k, around in EVERY:
+        restrict(src, coarse, k, around, WIN)
+    for k, around in EVERY:
+        correct(src, coarse, fine, k, around, WIN)
+    for k, around in EVERY[:BLOCKS]:
+        field[k, 0] = smooth(src, fine, k, around, 4, WIN2)
+    for gx in range(4):
+        packed = smooth(src, fine, BLOCKS + gx, around_packed(gx), 4, WIN2)
+        for gy in range(4):
+            moved = roll(packed, -COLS * gy, 1) if gy else packed
+            i = 4 * gx + gy
+            field[i, 1] = jnp.where(group == 0, moved, tail[i, 4 : 4 + WIN2, :])
+    for i in range(BLOCKS):
+        parts = (field[i, 0], field[i, 1])
         sums = [0.0, 0.0]
         for b in range(4):
-            turned = [roll(p, -COLS * b, 1) for p in parts]
-            near = here < 128 - COLS * b
-            same = [
-                jnp.where(near, turned[0], turned[1]),
-                jnp.where(near, turned[1], turned[0]),
-            ]
+            turned = [roll(p, -COLS * b, 1) if b else p for p in parts]
+            same = turned
+            if b:
+                inside = lane < 128 - COLS * b
+                same = [
+                    jnp.where(inside, turned[0], turned[1]),
+                    jnp.where(inside, turned[1], turned[0]),
+                ]
             for h in range(2):
                 lanes = slice(h * 128, (h + 1) * 128)
                 sums[h] = (
@@ -279,34 +310,43 @@
                     + coef[b : b + 1, lanes] * same[h]
                     + coef[4 + b : 5 + b, lanes] * same[1 - h]
                 )
-        for h in range(2):
-            rows = slice(h * WIN, (h + 1) * WIN)
-            coarse[i, rows, :] = gain[i, rows, :] * sums[h] + extra[i, rows, :]
-        return carry
-
-    def swap(i, carry):
-        src[i] = coarse[i]
-        return carry
-
-    lax.fori_loop(0, BLOCKS, restrict, 0, unroll=UNROLL)
-    lax.fori_loop(0, BLOCKS, correct, 0, unroll=UNROLL)
-    lax.fori_loop(0, BLOCKS, mix, 0, unroll=UNROLL)
-    lax.fori_loop(0, BLOCKS, swap, 0, unroll=UNROLL)
-    lax.fori_loop(0, BLOCKS, restrict, 0, unroll=UNROLL)
+        src[i, 8 : 8 + WIN2, :] = gain[i] * sums[0] + extra[i, 0]
+        tail[i, 0:WIN2, :] = gain[i] * sums[1] + extra[i, 1]
+    pack(tail, WIN2)
+    for k, around in EVERY:
+        restrict(src, coarse, k, around, WIN2)
     own = place[0]
-    next_x, last_x, next_y, last_y = around(own)
+    own_x = own // 4
+    next_x, last_x, next_y, last_y = around_block(own)
     for i in (own, next_x, last_x, next_y, last_y):
-        correct(i, 0)
-    second = gain[own] * smooth(own)
-    side_x = jnp.where(x_at < 2, roll(first[last_x], -16, 1), roll(first[next_x], 16, 1))
-    side_y = jnp.where(y_at < 4, first[next_y], first[last_y])
-    pieces = ((first[own], side_x), (side_y, second))
-    for k in range(2):
-        for m in range(2):
-            for h in range(2):
+        correct(src, coarse, fine, i, around_block(i), WIN2)
+    for gx in (own_x, (own_x + 1) % 4, (own_x + 3) % 4):
+        correct(src, coarse, fine, BLOCKS + gx, around_packed(gx), WIN2)
+    packed = smooth(src, fine, BLOCKS + own_x, around_packed(own_x), 0, WIN2)
+    moved = packed
+    for gy in range(1, 4):
+        moved = jnp.where(own % 4 == gy, roll(packed, -COLS * gy, 1), moved)
+    second = (
+        smooth(src, fine, own, around_block(own), 0, WIN2),
+        jnp.where(group == 0, moved, tail[own, 0:WIN2, :]),
+    )
+    x_at, y_at = (lane // SY) % SX, lane % SY
+
+    def first(i, h):
+        return gain[i] * field[i, h]
+
+    for h in range(2):
+        side_x = jnp.where(
+            x_at < 2, roll(first(last_x, h), -16, 1), roll(first(next_x, h), 16, 1)
+        )
+        side_y = jnp.where(y_at < 4, first(next_y, h), first(last_y, h))
+        pieces = ((first(own, h), side_x), (side_y, gain[own] * second[h]))
+        for k in range(2):
+            for m in range(2):
                 at = (2 * m + h) * 128
-                coarse[0] = pieces[k][m]
-                msg[4 * k : 4 * k + 4, at : at + 128] = coarse[0, h * WIN + 10 : h * WIN + 14, :]
+                spot = 4 * k + 2 * m + h
+                coarse[spot, 8 : 8 + WIN2, :] = pieces[k][m]
+                msg[4 * k : 4 * k + 4, at : at + 128] = coarse[spot, 14:18, :]
     for j in range(out.shape[0]):
         out[j] = msg[...]
 
@@ -404,12 +444,14 @@
 
 
 def stage_solve(place, near, far, coef, members):
-    big = (BLOCKS, 2 * WIN, 128)
+    padded = (BLOCKS + 4, WIN + 16, 128)
+    half = (BLOCKS, WIN2, 128)
+    pair = (BLOCKS, 2, WIN2, 128)
     return call(
         solve_kernel,
         (SMEM, VMEM, VMEM, VMEM),
         ((members, 8, 512),),
-        (big,) * 6 + ((8, 512),),
+        (padded,) * 3 + ((BLOCKS, WIN, 128), half, pair, pair, (8, 512)),
     )(place, near, far, coef)[0]
 
 

time: 146 us -> 144 us (0.986)
  Pallas kernels: 23.1 us -> 21.1 us
    pallas_call x1, Pallas kernels: 12.3 us -> 10.4 us  [stage_solve(): call(solve_kernel, (SMEM, VMEM, VMEM, VMEM), ((members, 8, 512),), (padde...]
  transfers between devices with their start and end apart: 13 -> 13, of which waited for: 6 -> 6; matrix products, arithmetic and copies ran while one was open for 2% -> 3% of each run, Pallas kernels for 0% -> 0%
where the time goes in v5:
time: 144 us
  starting transfers between devices  65.7 us (46%)
  waiting for transfers between devices  45.3 us (31%)
  Pallas kernels  21.1 us (15%)
  local copies, waits for them, and re-layouts  8.55 us (6%)
  other arithmetic  2.46 us (2%)
    all_to_all x4, starting transfers between devices, swap_all(): return lax.all_to_all(x, axis, 0, 0, tiled=True)  36.9 us
    all_to_all x4, waiting for transfers between devices, swap_all(): return lax.all_to_all(x, axis, 0, 0, tiled=True)  23.7 us
    ppermute x2, waiting for transfers between devices, halos(): below = lax.ppermute(south, GY, ring(GY, 1))  12.3 us
    ppermute x2, starting transfers between devices, halos(): above = lax.ppermute(north, GY, ring(GY, -1))  10.8 us
    pallas_call x1, Pallas kernels, stage_solve(): call(solve_kernel, (SMEM, VMEM, VMEM, VMEM), ((members, 8, 512),), (padde...  10.4 us
    ppermute x2, waiting for transfers between devices, halos(): above = lax.ppermute(north, GY, ring(GY, -1))  9.27 us
    ppermute x2, starting transfers between devices, halos(): low = lax.ppermute(f[:, SX - 2:], 'gx', ring('gx', 1))  8.2 us
    pallas_call x1, Pallas kernels, stage_last(): call(last_kernel, (SMEM,) + (VMEM,) * 7, (g.shape,), ((NZ, 1024), (4, ROW...  4.42 us
  transfers between devices with their start and end apart: 13, of which 6 were waited for; matrix products, arithmetic and copies ran while one was open for 3% of the time, Pallas kernels for 0%

profile of v5, /device:TPU:66, one launch (start us, length us, event | category | flops | bytes accessed | tf_op | source)
XLA Modules:
  0.0 143.5 jit_solution(6899580757997010464)
XLA Ops:
  0.0 0.7 subtract_multiply_fusion
  0.8 0.0 copy-start.15
  0.9 0.7 copy-done.15
  1.5 0.1 multiply_reduce_fusion.2
  1.6 1.8 %concatenate.13.table = f32[24,32]{1,0:T(8,128)} concatenate(f32[5,32]{1,0:T(8,128)S(1)} %fusion.2, f32[3,32]{1,0:T(4,128)S(1)} %slice.79, f32[1,32]{1,0:T(1,128)S(1)} %broadcast.110, f32[1,32]{1,0:T(1,128)S(1)} %get-tuple-element.51, f32[1,32]{1,0:T(1,128)S(1)} %broadcast_multiply_fusion.3, f32[1,32]{1,0:T(1,128)S(1)} %get-tuple-element.54, f32[1,32]{1,0:T(1,128)S(1)} %get-tuple-element.57, ...), dimensions={0} | concatenate | bytes 6144 | tf_op jit(solution)/shard_map/concatenate | solution.py:83
  3.5 2.6 %shard_map.64 = (f32[32,24,256]{2,1,0:T(8,128)}, f32[32,8,128]{2,1,0:T(8,128)}, f32[32,8,128]{2,1,0:T(8,128)}) custom-call(f32[24,32]{1,0:T(8,128)} %concatenate.13.table, f32[32,4,8,128]{3,2,1,0:T(8,128)} %f.3), custom_call_target="tpu_custom_call" | custom-call | tf_op jit(solution)/shard_map/pallas_call | solution.py:408
  6.0 10.4 %all-to-all-start = ((f32[32,24,256]{2,1,0:T(8,128)}), f32[32,24,256]{2,1,0:T(8,128)S(1)}, u32[]{:S(2)}, u32[]{:S(2)}) async-start(f32[32,24,256]{2,1,0:T(8,128)} %get-tuple-element.19), calls=%async_computation | async-start | bytes 1572864 | tf_op jit(solution)/shard_map/all_to_all | solution.py:480
  16.4 0.0 copy-start.19
  16.5 2.1 %collective-permute-start.1 = (f32[32,2,8,128]{3,2,1,0:T(8,128)S(1)}, f32[32,2,8,128]{3,2,1,0:T(8,128)S(1)}, u32[]{:S(2)}, u32[]{:S(2)}) collective-permute-start(f32[32,2,8,128]{3,2,1,0:T(8,128)S(1)} %get-tuple-element.35), channel_id=1, source_target_pairs={{0,384},{128,0},{256,128},{384,256},{1,385},{129,1},{257,129},{385... | collective-permute-start | bytes 786440 | tf_op jit(solution)/shard_map/ppermute | solution.py:473
  18.6 4.3 %collective-permute-start = (f32[32,2,8,128]{3,2,1,0:T(8,128)S(1)}, f32[32,2,8,128]{3,2,1,0:T(8,128)S(1)}, u32[]{:S(2)}, u32[]{:S(2)}) collective-permute-start(f32[32,2,8,128]{3,2,1,0:T(8,128)S(1)} %get-tuple-element.36), channel_id=1, source_target_pairs={{0,128},{128,256},{256,384},{384,0},{1,129},{129,257},{257,385},{3... | collective-permute-start | bytes 786440 | tf_op jit(solution)/shard_map/ppermute | solution.py:472
  22.8 0.0 copy-done.19
  22.8 8.0 %collective-permute-start.2 = (f32[32,8,128]{2,1,0:T(8,128)S(1)}, f32[32,8,128]{2,1,0:T(8,128)S(1)}, u32[]{:S(2)}, u32[]{:S(2)}) collective-permute-start(f32[32,8,128]{2,1,0:T(8,128)S(1)} %copy-done.19), channel_id=1, source_target_pairs={{0,96},{32,0},{64,32},{96,64},{1,97},{33,1},{65,33},{97,65},{2,98}... | collective-permute-start | bytes 393224 | tf_op jit(solution)/shard_map/ppermute | solution.py:474
  30.8 1.9 %collective-permute-start.3 = (f32[32,8,128]{2,1,0:T(8,128)S(1)}, f32[32,8,128]{2,1,0:T(8,128)S(1)}, u32[]{:S(2)}, u32[]{:S(2)}) collective-permute-start(f32[32,8,128]{2,1,0:T(8,128)S(1)} %copy-done.18), channel_id=1, source_target_pairs={{0,32},{32,64},{64,96},{96,0},{1,33},{33,65},{65,97},{97,1},{2,34}... | collective-permute-start | bytes 393224 | tf_op jit(solution)/shard_map/ppermute | solution.py:475
  32.8 0.1 multiply_reduce_fusion.1
  32.9 0.6 reshape.75.cross
  33.6 0.6 broadcast_select_fusion
  34.2 0.3 collective-permute-done.2.north
  34.5 8.7 %collective-permute-done.3.south = f32[32,8,128]{2,1,0:T(8,128)S(1)} collective-permute-done((f32[32,8,128]{2,1,0:T(8,128)S(1)}, f32[32,8,128]{2,1,0:T(8,128)S(1)}, u32[]{:S(2)}, u32[]{:S(2)}) %collective-permute-start.3) | collective-permute-done | bytes 131104 | tf_op jit(solution)/shard_map/ppermute | solution.py:475
  43.1 0.0 collective-permute-done.1.high
  43.1 0.0 collective-permute-done.low
  43.1 0.0 all-to-all-done
  43.2 0.6 copy-done.10
  43.8 0.1 copy-done.7
  43.9 0.1 copy-done.8
  44.0 3.7 %shard_map.65 = (f32[32,4,8,128]{3,2,1,0:T(8,128)}, f32[32,16,256]{2,1,0:T(8,128)}, f32[32,8,128]{2,1,0:T(8,128)}, f32[32,8,128]{2,1,0:T(8,128)}) custom-call(f32[24,32]{1,0:T(8,128)} %concatenate.13.table, f32[32,4,8,128]{3,2,1,0:T(8,128)} %f.3, f32[32,2,8,128]{3,2,1,0:T(8,128)} %copy-done.8, f32[32,2,8,128]{3,2,1,0:T(8,128)} %copy-done.7, ...), custom_call_target="tpu_custom_call" | custom-call | tf_op jit(solution)/shard_map/pallas_call | solution.py:418
  47.7 9.8 %all-to-all-start.1 = ((f32[32,16,256]{2,1,0:T(8,128)}), f32[32,16,256]{2,1,0:T(8,128)S(1)}, u32[]{:S(2)}, u32[]{:S(2)}) async-start(f32[32,16,256]{2,1,0:T(8,128)} %get-tuple-element.25), calls=%async_computation.1 | async-start | bytes 1048576 | tf_op jit(solution)/shard_map/all_to_all | solution.py:480
  57.5 0.1 slice.80
  57.6 0.1 fusion.1
  57.7 0.1 fusion.11
  57.7 0.1 copy.10
  57.8 0.1 slice.69
  57.9 0.1 copy.11
  58.0 0.1 slice.72
  58.0 0.1 reduce_sum.66
  58.1 13.4 %all-to-all-done.1 = f32[32,16,256]{2,1,0:T(8,128)S(1)} async-done(((f32[32,16,256]{2,1,0:T(8,128)}), f32[32,16,256]{2,1,0:T(8,128)S(1)}, u32[]{:S(2)}, u32[]{:S(2)}) %all-to-all-start.1) | async-done | bytes 524320 | tf_op jit(solution)/shard_map/all_to_all | solution.py:480
  71.6 0.7 broadcast_in_dim.34
  72.4 10.5 %all-to-all-start.2 = ((f32[8,40,256]{2,1,0:T(8,128)}), f32[8,40,256]{2,1,0:T(8,128)S(1)}, u32[]{:S(2)}, u32[]{:S(2)}) async-start(f32[8,40,256]{2,1,0:T(8,128)} %broadcast_in_dim.34), calls=%async_computation.2 | async-start | bytes 655360 | tf_op jit(solution)/shard_map/all_to_all | solution.py:480
  82.9 10.2 %all-to-all-done.2.near = f32[8,40,256]{2,1,0:T(8,128)S(1)} async-done(((f32[8,40,256]{2,1,0:T(8,128)}), f32[8,40,256]{2,1,0:T(8,128)S(1)}, u32[]{:S(2)}, u32[]{:S(2)}) %all-to-all-start.2) | async-done | bytes 327712 | tf_op jit(solution)/shard_map/all_to_all | solution.py:480
  93.1 1.9 %collective-permute-start.4 = (f32[8,40,256]{2,1,0:T(8,128)S(1)}, f32[8,40,256]{2,1,0:T(8,128)S(1)}, u32[]{:S(2)}, u32[]{:S(2)}) collective-permute-start(f32[8,40,256]{2,1,0:T(8,128)S(1)} %all-to-all-done.2.near), channel_id=1, source_target_pairs={{0,32},{32,0},{1,33},{33,1},{2,34},{34,2},{3,35},{35,3},{4,36},{36... | collective-permute-start | bytes 983048 | tf_op jit(solution)/shard_map/ppermute | solution.py:499
  95.0 0.6 pad_add_fusion.place
  95.7 0.1 reshape_squeeze.3
  95.7 0.1 multiply_reduce_fusion
  95.8 0.1 broadcast_in_dim.35
  95.9 0.7 reshape.76.coef
  96.6 0.0 collective-permute-done.4.far
  96.6 0.7 copy-done.4
  97.3 10.4 %shard_map.66 = f32[32,8,512]{2,1,0:T(8,128)} custom-call(s32[2]{0:T(128)} %pad_add_fusion.place, f32[8,40,256]{2,1,0:T(8,128)} %copy-done.3, f32[8,40,256]{2,1,0:T(8,128)} %copy-done.4, f32[8,256]{1,0:T(8,128)} %reshape.76.coef), custom_call_target="tpu_custom_call" | custom-call | tf_op jit(solution)/shard_map/pallas_call | solution.py:450
  107.7 6.3 %all-to-all-start.3 = ((f32[32,8,512]{2,1,0:T(8,128)}), f32[32,8,512]{2,1,0:T(8,128)S(1)}, u32[]{:S(2)}, u32[]{:S(2)}) async-start(f32[32,8,512]{2,1,0:T(8,128)} %shard_map.66), calls=%async_computation.3 | async-start | bytes 1048576 | tf_op jit(solution)/shard_map/all_to_all | solution.py:480
  114.0 2.1 %collective-permute-start.6 = (f32[32,2,8,128]{3,2,1,0:T(8,128)S(1)}, f32[32,2,8,128]{3,2,1,0:T(8,128)S(1)}, u32[]{:S(2)}, u32[]{:S(2)}) collective-permute-start(f32[32,2,8,128]{3,2,1,0:T(8,128)S(1)} %get-tuple-element.33), channel_id=1, source_target_pairs={{0,384},{128,0},{256,128},{384,256},{1,385},{129,1},{257,129},{385... | collective-permute-start | bytes 786440 | tf_op jit(solution)/shard_map/ppermute | solution.py:473
  116.1 3.9 %collective-permute-start.5 = (f32[32,2,8,128]{3,2,1,0:T(8,128)S(1)}, f32[32,2,8,128]{3,2,1,0:T(8,128)S(1)}, u32[]{:S(2)}, u32[]{:S(2)}) collective-permute-start(f32[32,2,8,128]{3,2,1,0:T(8,128)S(1)} %get-tuple-element.34), channel_id=1, source_target_pairs={{0,128},{128,256},{256,384},{384,0},{1,129},{129,257},{257,385},{3... | collective-permute-start | bytes 786440 | tf_op jit(solution)/shard_map/ppermute | solution.py:472
  120.0 0.0 copy-done.17
  120.0 2.8 %collective-permute-start.7 = (f32[32,8,128]{2,1,0:T(8,128)S(1)}, f32[32,8,128]{2,1,0:T(8,128)S(1)}, u32[]{:S(2)}, u32[]{:S(2)}) collective-permute-start(f32[32,8,128]{2,1,0:T(8,128)S(1)} %copy-done.17), channel_id=1, source_target_pairs={{0,96},{32,0},{64,32},{96,64},{1,97},{33,1},{65,33},{97,65},{2,98}... | collective-permute-start | bytes 393224 | tf_op jit(solution)/shard_map/ppermute | solution.py:474
  122.8 0.0 copy-done.16
  122.8 1.9 %collective-permute-start.8 = (f32[32,8,128]{2,1,0:T(8,128)S(1)}, f32[32,8,128]{2,1,0:T(8,128)S(1)}, u32[]{:S(2)}, u32[]{:S(2)}) collective-permute-start(f32[32,8,128]{2,1,0:T(8,128)S(1)} %copy-done.16), channel_id=1, source_target_pairs={{0,32},{32,64},{64,96},{96,0},{1,33},{33,65},{65,97},{97,1},{2,34}... | collective-permute-start | bytes 393224 | tf_op jit(solution)/shard_map/ppermute | solution.py:475
  124.8 9.0 %collective-permute-done.7.north = f32[32,8,128]{2,1,0:T(8,128)S(1)} collective-permute-done((f32[32,8,128]{2,1,0:T(8,128)S(1)}, f32[32,8,128]{2,1,0:T(8,128)S(1)}, u32[]{:S(2)}, u32[]{:S(2)}) %collective-permute-start.7) | collective-permute-done | bytes 131104 | tf_op jit(solution)/shard_map/ppermute | solution.py:474
  133.8 3.7 %collective-permute-done.8.south = f32[32,8,128]{2,1,0:T(8,128)S(1)} collective-permute-done((f32[32,8,128]{2,1,0:T(8,128)S(1)}, f32[32,8,128]{2,1,0:T(8,128)S(1)}, u32[]{:S(2)}, u32[]{:S(2)}) %collective-permute-start.8) | collective-permute-done | bytes 131104 | tf_op jit(solution)/shard_map/ppermute | solution.py:475
  137.4 0.0 collective-permute-done.6.high
  137.4 0.0 collective-permute-done.5.low
  137.4 0.0 all-to-all-done.3.recv
  137.5 0.6 copy-done.12
  138.1 0.1 copy-done.5
  138.2 0.1 copy-done.6
  138.3 0.8 copy-done.2
  139.1 4.4 %shard_map.67 = f32[32,4,8,128]{3,2,1,0:T(8,128)} custom-call(f32[24,32]{1,0:T(8,128)} %concatenate.13.table, f32[32,8,512]{2,1,0:T(8,128)} %copy-done.2, f32[32,4,8,128]{3,2,1,0:T(8,128)} %get-tuple-element.26.g, f32[32,2,8,128]{3,2,1,0:T(8,128)} %copy-done.6, f32[32,2,8,128]{3,2,1,0:T(8,128)} %copy-done.5, f32[32,8,128]{2,1,0:T(8,128)} %copy-done.11, ...), custom_call_target="tpu_custom_call" | custom-call | tf_op jit(solution)/shard_map/pallas_call | solution.py:459
  (47 shorter events, 0.4 us)
Async XLA Ops:
  0.8 0.7 copy-start.15
  6.0 10.4 %copy-start = (f32[32,4,8,128]{3,2,1,0:T(8,128)S(1)}, f32[32,4,8,128]{3,2,1,0:T(8,128)}, u32[]{:S(2)}) copy-start(f32[32,4,8,128]{3,2,1,0:T(8,128)} %f.3) | copy-start | bytes 1572868
  6.0 37.1 %all-to-all-start = ((f32[32,24,256]{2,1,0:T(8,128)}), f32[32,24,256]{2,1,0:T(8,128)S(1)}, u32[]{:S(2)}, u32[]{:S(2)}) async-start(f32[32,24,256]{2,1,0:T(8,128)} %get-tuple-element.19), calls=%async_computation | async-start | bytes 1572864 | tf_op jit(solution)/shard_map/all_to_all | solution.py:480
  16.4 6.4 %copy-start.19 = (f32[32,8,128]{2,1,0:T(8,128)S(1)}, f32[32,8,128]{2,1,0:T(8,128)}, u32[]{:S(2)}) copy-start(f32[32,8,128]{2,1,0:T(8,128)} %get-tuple-element.17) | copy-start | bytes 393220
  16.4 14.4 %copy-start.18 = (f32[32,8,128]{2,1,0:T(8,128)S(1)}, f32[32,8,128]{2,1,0:T(8,128)}, u32[]{:S(2)}) copy-start(f32[32,8,128]{2,1,0:T(8,128)} %get-tuple-element.18) | copy-start | bytes 393220
  16.5 26.6 %collective-permute-start.1 = (f32[32,2,8,128]{3,2,1,0:T(8,128)S(1)}, f32[32,2,8,128]{3,2,1,0:T(8,128)S(1)}, u32[]{:S(2)}, u32[]{:S(2)}) collective-permute-start(f32[32,2,8,128]{3,2,1,0:T(8,128)S(1)} %get-tuple-element.35), channel_id=1, source_target_pairs={{0,384},{128,0},{256,128},{384,256},{1,385},{129,1},{257,129},{385... | collective-permute-start | bytes 786440 | tf_op jit(solution)/shard_map/ppermute | solution.py:473
  18.6 24.6 %collective-permute-start = (f32[32,2,8,128]{3,2,1,0:T(8,128)S(1)}, f32[32,2,8,128]{3,2,1,0:T(8,128)S(1)}, u32[]{:S(2)}, u32[]{:S(2)}) collective-permute-start(f32[32,2,8,128]{3,2,1,0:T(8,128)S(1)} %get-tuple-element.36), channel_id=1, source_target_pairs={{0,128},{128,256},{256,384},{384,0},{1,129},{129,257},{257,385},{3... | collective-permute-start | bytes 786440 | tf_op jit(solution)/shard_map/ppermute | solution.py:472
  22.8 11.6 %collective-permute-start.2 = (f32[32,8,128]{2,1,0:T(8,128)S(1)}, f32[32,8,128]{2,1,0:T(8,128)S(1)}, u32[]{:S(2)}, u32[]{:S(2)}) collective-permute-start(f32[32,8,128]{2,1,0:T(8,128)S(1)} %copy-done.19), channel_id=1, source_target_pairs={{0,96},{32,0},{64,32},{96,64},{1,97},{33,1},{65,33},{97,65},{2,98}... | collective-permute-start | bytes 393224 | tf_op jit(solution)/shard_map/ppermute | solution.py:474
  30.8 12.3 %collective-permute-start.3 = (f32[32,8,128]{2,1,0:T(8,128)S(1)}, f32[32,8,128]{2,1,0:T(8,128)S(1)}, u32[]{:S(2)}, u32[]{:S(2)}) collective-permute-start(f32[32,8,128]{2,1,0:T(8,128)S(1)} %copy-done.18), channel_id=1, source_target_pairs={{0,32},{32,64},{64,96},{96,0},{1,33},{33,65},{65,97},{97,1},{2,34}... | collective-permute-start | bytes 393224 | tf_op jit(solution)/shard_map/ppermute | solution.py:475
  32.8 0.8 copy-start.14
  34.5 8.7 %copy-start.9 = (f32[32,8,128]{2,1,0:T(8,128)}, f32[32,8,128]{2,1,0:T(8,128)S(1)}, u32[]{:S(2)}) copy-start(f32[32,8,128]{2,1,0:T(8,128)S(1)} %collective-permute-done.2.north) | copy-start | bytes 393220
  43.1 0.6 copy-start.10
  43.1 0.8 copy-start.7
  43.1 0.9 copy-start.8
  47.7 23.8 %all-to-all-start.1 = ((f32[32,16,256]{2,1,0:T(8,128)}), f32[32,16,256]{2,1,0:T(8,128)S(1)}, u32[]{:S(2)}, u32[]{:S(2)}) async-start(f32[32,16,256]{2,1,0:T(8,128)} %get-tuple-element.25), calls=%async_computation.1 | async-start | bytes 1048576 | tf_op jit(solution)/shard_map/all_to_all | solution.py:480
  72.4 20.7 %all-to-all-start.2 = ((f32[8,40,256]{2,1,0:T(8,128)}), f32[8,40,256]{2,1,0:T(8,128)S(1)}, u32[]{:S(2)}, u32[]{:S(2)}) async-start(f32[8,40,256]{2,1,0:T(8,128)} %broadcast_in_dim.34), calls=%async_computation.2 | async-start | bytes 655360 | tf_op jit(solution)/shard_map/all_to_all | solution.py:480
  82.8 12.9 %copy-start.13 = (f32[8,8,8]{2,1,0:T(8,128)S(1)}, f32[8,8,8]{2,1,0:T(8,128)}, u32[]{:S(2)}) copy-start(f32[8,8,8]{2,1,0:T(8,128)} %constant.72.clone) | copy-start | bytes 6148
  93.1 3.5 %copy-start.3 = (f32[8,40,256]{2,1,0:T(8,128)}, f32[8,40,256]{2,1,0:T(8,128)S(1)}, u32[]{:S(2)}) copy-start(f32[8,40,256]{2,1,0:T(8,128)S(1)} %all-to-all-done.2.near) | copy-start | bytes 983044
  93.1 3.5 %collective-permute-start.4 = (f32[8,40,256]{2,1,0:T(8,128)S(1)}, f32[8,40,256]{2,1,0:T(8,128)S(1)}, u32[]{:S(2)}, u32[]{:S(2)}) collective-permute-start(f32[8,40,256]{2,1,0:T(8,128)S(1)} %all-to-all-done.2.near), channel_id=1, source_target_pairs={{0,32},{32,0},{1,33},{33,1},{2,34},{34,2},{3,35},{35,3},{4,36},{36... | collective-permute-start | bytes 983048 | tf_op jit(solution)/shard_map/ppermute | solution.py:499
  96.6 0.7 copy-start.4
  107.7 6.3 %copy-start.1 = (f32[32,4,8,128]{3,2,1,0:T(8,128)S(1)}, f32[32,4,8,128]{3,2,1,0:T(8,128)}, u32[]{:S(2)}) copy-start(f32[32,4,8,128]{3,2,1,0:T(8,128)} %get-tuple-element.26.g) | copy-start | bytes 1572868
  107.7 29.8 %all-to-all-start.3 = ((f32[32,8,512]{2,1,0:T(8,128)}), f32[32,8,512]{2,1,0:T(8,128)S(1)}, u32[]{:S(2)}, u32[]{:S(2)}) async-start(f32[32,8,512]{2,1,0:T(8,128)} %shard_map.66), calls=%async_computation.3 | async-start | bytes 1048576 | tf_op jit(solution)/shard_map/all_to_all | solution.py:480
  114.0 6.1 %copy-start.17 = (f32[32,8,128]{2,1,0:T(8,128)S(1)}, f32[32,8,128]{2,1,0:T(8,128)}, u32[]{:S(2)}) copy-start(f32[32,8,128]{2,1,0:T(8,128)} %get-tuple-element.27) | copy-start | bytes 393220
  114.0 8.9 %copy-start.16 = (f32[32,8,128]{2,1,0:T(8,128)S(1)}, f32[32,8,128]{2,1,0:T(8,128)}, u32[]{:S(2)}) copy-start(f32[32,8,128]{2,1,0:T(8,128)} %get-tuple-element.28) | copy-start | bytes 393220
  114.0 23.4 %collective-permute-start.6 = (f32[32,2,8,128]{3,2,1,0:T(8,128)S(1)}, f32[32,2,8,128]{3,2,1,0:T(8,128)S(1)}, u32[]{:S(2)}, u32[]{:S(2)}) collective-permute-start(f32[32,2,8,128]{3,2,1,0:T(8,128)S(1)} %get-tuple-element.33), channel_id=1, source_target_pairs={{0,384},{128,0},{256,128},{384,256},{1,385},{129,1},{257,129},{385... | collective-permute-start | bytes 786440 | tf_op jit(solution)/shard_map/ppermute | solution.py:473
  116.1 21.3 %collective-permute-start.5 = (f32[32,2,8,128]{3,2,1,0:T(8,128)S(1)}, f32[32,2,8,128]{3,2,1,0:T(8,128)S(1)}, u32[]{:S(2)}, u32[]{:S(2)}) collective-permute-start(f32[32,2,8,128]{3,2,1,0:T(8,128)S(1)} %get-tuple-element.34), channel_id=1, source_target_pairs={{0,128},{128,256},{256,384},{384,0},{1,129},{129,257},{257,385},{3... | collective-permute-start | bytes 786440 | tf_op jit(solution)/shard_map/ppermute | solution.py:472
  120.0 13.7 %collective-permute-start.7 = (f32[32,8,128]{2,1,0:T(8,128)S(1)}, f32[32,8,128]{2,1,0:T(8,128)S(1)}, u32[]{:S(2)}, u32[]{:S(2)}) collective-permute-start(f32[32,8,128]{2,1,0:T(8,128)S(1)} %copy-done.17), channel_id=1, source_target_pairs={{0,96},{32,0},{64,32},{96,64},{1,97},{33,1},{65,33},{97,65},{2,98}... | collective-permute-start | bytes 393224 | tf_op jit(solution)/shard_map/ppermute | solution.py:474
  122.8 14.6 %collective-permute-start.8 = (f32[32,8,128]{2,1,0:T(8,128)S(1)}, f32[32,8,128]{2,1,0:T(8,128)S(1)}, u32[]{:S(2)}, u32[]{:S(2)}) collective-permute-start(f32[32,8,128]{2,1,0:T(8,128)S(1)} %copy-done.16), channel_id=1, source_target_pairs={{0,32},{32,64},{64,96},{96,0},{1,33},{33,65},{65,97},{97,1},{2,34}... | collective-permute-start | bytes 393224 | tf_op jit(solution)/shard_map/ppermute | solution.py:475
  133.7 3.7 %copy-start.11 = (f32[32,8,128]{2,1,0:T(8,128)}, f32[32,8,128]{2,1,0:T(8,128)S(1)}, u32[]{:S(2)}) copy-start(f32[32,8,128]{2,1,0:T(8,128)S(1)} %collective-permute-done.7.north) | copy-start | bytes 393220
  137.4 0.7 copy-start.12
  137.4 0.7 copy-start.5
  137.4 0.8 copy-start.6
  138.3 0.8 copy-start.2
